TPU v7x, 32 devices: a whole 2x2x4 slice. The times are simulated.
32 devices in a mesh: fsdp: 8 (over z, x), tp: 4 (over y, core).
Axes of the slice: x: 2, y: 2, z: 4, core: 2. Of those that a mesh axis runs over, the one named last changes fastest.
Arguments:
- block_in: bfloat16 [3, 4096, 2048], P(None, ('fsdp', 'tp')), may hold values from -6 to 6
- span_start: int32 [3, 8], P(None, 'fsdp'), may hold values from 0 to 256
- w_query: bfloat16 [2048, 2048], P('fsdp', 'tp'), may hold values from -0.25 to 0.25
- w_key: bfloat16 [2048, 256], P('fsdp', 'tp'), may hold values from -0.125 to 0.125
- w_value: bfloat16 [2048, 256], P('fsdp', 'tp'), may hold values from -0.125 to 0.125
- w_out: bfloat16 [2048, 2048], P('tp', 'fsdp'), may hold values from -1.5 to 1.5
- w_gate: bfloat16 [2048, 5632], P('fsdp', 'tp'), may hold values from -0.125 to 0.125
- w_up: bfloat16 [2048, 5632], P('fsdp', 'tp'), may hold values from -0.125 to 0.125
- w_down: bfloat16 [5632, 2048], P('tp', 'fsdp'), may hold values from -0.078125 to 0.078125
- gain_attn: bfloat16 [2048], P('fsdp'), may hold values from 0.099609375 to 1.8984375
- gain_mlp: bfloat16 [2048], P('fsdp'), may hold values from 0.099609375 to 1.8984375
- cotangent: bfloat16 [3, 4096, 2048], P(None, ('fsdp', 'tp')), may hold values from -6 to 6
Outputs:
- block_out: float32 [3, 4096, 2048], P(None, ('fsdp', 'tp'))
- grad_in: float32 [3, 4096, 2048], P(None, ('fsdp', 'tp'))
- grad_query: float32 [2048, 2048], P('fsdp', 'tp')
- grad_key: float32 [2048, 256], P('fsdp', 'tp')
- grad_value: float32 [2048, 256], P('fsdp', 'tp')
- grad_out: float32 [2048, 2048], P('tp', 'fsdp')
- grad_gate: float32 [2048, 5632], P('fsdp', 'tp')
- grad_up: float32 [2048, 5632], P('fsdp', 'tp')
- grad_down: float32 [5632, 2048], P('tp', 'fsdp')
- grad_gain_attn: float32 [2048], P('fsdp')
- grad_gain_mlp: float32 [2048], P('fsdp')
Inputs may be any that keep to these rules, and one draw needn't show every extreme that they name: A sequence's image span covers positions span_start to span_start + 255.
All inputs are finite; a program needn't handle non-finite values.
Results may differ from a plain program's by a relative error of at most 0.018.
Values may be sent and summed in bfloat16 or wider, within the bound.
No kernel may reach another device: no remote copies, remote signals or barrier semaphores. Data moves between devices by JAX's collectives and lax.ppermute only.
A program may use at most 256 MiB of HBM per device.

v0:
```python
import math

import jax
import jax.numpy as jnp
from jax import lax
from jax.sharding import PartitionSpec as P

HD = 64
SPAN = 256


epsilon = 1e-05
masked_value = -1e30


def angle_tables(length, width):
    half_width = width // 2
    frequency = jnp.exp(
        jnp.arange(half_width, dtype=jnp.float32) * (-2.0 * math.log(10000.0) / width)
    )
    places = jnp.arange(length, dtype=jnp.float32)
    angles = places[:, None] * frequency[None, :]
    angles = jnp.concatenate([angles, angles], axis=1)
    return (jnp.cos(angles)[:, None, :], jnp.sin(angles)[:, None, :])


def rotate(values, cos_table, sine_table):
    half_width = values.shape[-1] // 2
    turned = jnp.concatenate([-values[..., half_width:], values[..., :half_width]], axis=-1)
    return values * cos_table + turned * sine_table


def rotate_back(values, cos_table, sine_table):
    half_width = values.shape[-1] // 2
    turned = jnp.concatenate([-values[..., half_width:], values[..., :half_width]], axis=-1)
    return values * cos_table - turned * sine_table


def visible_mask(length, span_first):
    places = jnp.arange(length, dtype=jnp.int32)
    inside = (places >= span_first) & (places < span_first + SPAN)
    return (places[:, None] >= places[None, :]) | inside[:, None] & inside[None, :]


def dot_plain(left_side, right_side):
    return jnp.dot(left_side, right_side, preferred_element_type=jnp.float32)


def dot_left_t(left_side, right_side):
    return lax.dot_general(
        left_side, right_side, (((0,), (0,)), ((), ())), preferred_element_type=jnp.float32
    )


def dot_right_t(left_side, right_side):
    return lax.dot_general(
        left_side, right_side, (((1,), (1,)), ((), ())), preferred_element_type=jnp.float32
    )


def norm_rows(tokens, gain_full):
    inv_rms = lax.rsqrt(jnp.mean(tokens * tokens, axis=-1, keepdims=True) + epsilon)
    return (inv_rms, (tokens * inv_rms * gain_full).astype(jnp.bfloat16))


def norm_back(tokens, inv_rms, gain_full, upstream):
    weighted = upstream * gain_full
    inner_mean = jnp.mean(weighted * tokens, axis=-1, keepdims=True)
    grad_tokens = inv_rms * weighted - tokens * (inv_rms * inv_rms * inv_rms) * inner_mean
    return (grad_tokens, jnp.sum(upstream * tokens * inv_rms, axis=0))


def spread_rows(shard_rows):
    return lax.all_gather(shard_rows, "tp", axis=0, tiled=True)


def spread_grads(shard_rows):
    return lax.all_gather(shard_rows, "tp", axis=0, tiled=True)


def collect_out(inputs, weight, local_rows):

    def term_rows(offset, extent):
        return dot_plain(inputs, weight)

    return lax.psum_scatter(
        term_rows(jnp.int32(0), local_rows * lax.axis_size("tp")),
        "tp",
        scatter_dimension=0,
        tiled=True,
    )


def collect_grads(inputs, weights, local_rows):

    def term_rows(offset, extent):
        running = jnp.zeros((extent, weights[0].shape[0]), jnp.float32)
        for grad_part, weight in zip(inputs, weights):
            running = running + dot_right_t(grad_part, weight)
        return running

    return lax.psum_scatter(
        term_rows(jnp.int32(0), local_rows * lax.axis_size("tp")),
        "tp",
        scatter_dimension=0,
        tiled=True,
    )


def add_tuples(running, incoming):
    if running is None:
        return incoming
    return tuple((first_one + second_one for first_one, second_one in zip(running, incoming)))


def scores_of(query_rot, key_rot, span_first, heads_kv):
    length = query_rot.shape[0]
    group_size = query_rot.shape[1] // heads_kv
    query_grp = query_rot.reshape(length, heads_kv, group_size, query_rot.shape[2])
    factor = query_rot.shape[2] ** (-0.5)
    scores = factor * jnp.einsum(
        "qgrd,sgd->grqs", query_grp, key_rot, preferred_element_type=jnp.float32
    )
    return (query_grp, factor, jnp.where(visible_mask(length, span_first), scores, masked_value))


def attend(query_rot, key_rot, value_low, span_first, heads_kv):
    length = query_rot.shape[0]
    query_grp, factor, scores = scores_of(query_rot, key_rot, span_first, heads_kv)
    row_max = jnp.max(scores, axis=-1, keepdims=True)
    raised = jnp.exp(scores - row_max)
    row_total = jnp.sum(raised, axis=-1, keepdims=True)
    weights_p = (raised / row_total).astype(jnp.bfloat16)
    mixed_low = jnp.einsum(
        "grqs,sgd->qgrd", weights_p, value_low, preferred_element_type=jnp.float32
    )
    return (mixed_low.reshape(length, -1).astype(jnp.bfloat16), row_max + jnp.log(row_total))


def attend_back(query_rot, key_rot, value_low, span_first, log_total, grad_mixed, heads_kv):
    query_grp, factor, scores = scores_of(query_rot, key_rot, span_first, heads_kv)
    weights_p = jnp.exp(scores - log_total)
    grad_grp = grad_mixed.reshape(query_grp.shape)
    grad_weights = jnp.einsum(
        "qgrd,sgd->grqs", grad_grp, value_low, preferred_element_type=jnp.float32
    )
    grad_value = jnp.einsum(
        "grqs,qgrd->sgd",
        weights_p.astype(jnp.bfloat16),
        grad_grp,
        preferred_element_type=jnp.float32,
    )
    row_delta = jnp.sum(weights_p * grad_weights, axis=-1, keepdims=True)
    grad_scores = (factor * (weights_p * (grad_weights - row_delta))).astype(jnp.bfloat16)
    grad_query = jnp.einsum(
        "grqs,sgd->qgrd", grad_scores, key_rot, preferred_element_type=jnp.float32
    )
    grad_key = jnp.einsum(
        "grqs,qgrd->sgd", grad_scores, query_grp, preferred_element_type=jnp.float32
    )
    return (grad_query.reshape(query_rot.shape), grad_key, grad_value)


def per_device(
    block_in,
    span_start,
    w_query,
    w_key,
    w_value,
    w_out,
    w_gate,
    w_up,
    w_down,
    gain_attn,
    gain_mlp,
    cotangent,
):
    local_rows = block_in.shape[1]
    length = local_rows * lax.axis_size("tp")
    heads_kv = w_key.shape[1] // HD
    cos_table, sine_table = angle_tables(length, HD)
    outputs = []
    input_grads = []
    local_sums = None
    owner_sums = None
    for batch_index in range(block_in.shape[0]):
        gathered = (
            lax.all_gather(w_query, "fsdp", axis=0, tiled=True),
            lax.all_gather(w_key, "fsdp", axis=0, tiled=True),
            lax.all_gather(w_value, "fsdp", axis=0, tiled=True),
            lax.all_gather(w_out, "fsdp", axis=1, tiled=True),
            lax.all_gather(w_gate, "fsdp", axis=0, tiled=True),
            lax.all_gather(w_up, "fsdp", axis=0, tiled=True),
            lax.all_gather(w_down, "fsdp", axis=1, tiled=True),
            lax.all_gather(gain_attn, "fsdp", axis=0, tiled=True),
            lax.all_gather(gain_mlp, "fsdp", axis=0, tiled=True),
        )
        (
            full_query,
            full_key,
            full_value,
            full_out,
            full_gate,
            full_up,
            full_down,
            gain_full_one,
            gain_full_two,
        ) = gathered
        gain_one = gain_full_one.astype(jnp.float32)
        gain_two = gain_full_two.astype(jnp.float32)
        tokens = block_in[batch_index].astype(jnp.float32)
        span_first = span_start[batch_index, 0]
        scale_one, normed_one = norm_rows(tokens, gain_one)
        seq_one = spread_rows(normed_one)
        query_raw = dot_plain(seq_one, full_query).reshape(length, -1, HD)
        key_raw = dot_plain(seq_one, full_key).reshape(length, heads_kv, HD)
        value_low = (
            dot_plain(seq_one, full_value).astype(jnp.bfloat16).reshape(length, heads_kv, HD)
        )
        query_rot = rotate(query_raw, cos_table, sine_table).astype(jnp.bfloat16)
        key_rot = rotate(key_raw, cos_table, sine_table).astype(jnp.bfloat16)
        mixed_low, log_total = attend(query_rot, key_rot, value_low, span_first, heads_kv)
        hidden_res = tokens + collect_out(mixed_low, full_out, local_rows)
        scale_two, normed_two = norm_rows(hidden_res, gain_two)
        seq_two = spread_rows(normed_two)
        gate_pre = dot_plain(seq_two, full_gate)
        up_pre = dot_plain(seq_two, full_up)
        sigmoid_gate = jax.nn.sigmoid(gate_pre)
        activated = gate_pre * sigmoid_gate
        inner_low = (activated * up_pre).astype(jnp.bfloat16)
        outputs.append(hidden_res + collect_out(inner_low, full_down, local_rows))
        gathered = (
            lax.all_gather(w_query, "fsdp", axis=0, tiled=True),
            lax.all_gather(w_key, "fsdp", axis=0, tiled=True),
            lax.all_gather(w_value, "fsdp", axis=0, tiled=True),
            lax.all_gather(w_out, "fsdp", axis=1, tiled=True),
            lax.all_gather(w_gate, "fsdp", axis=0, tiled=True),
            lax.all_gather(w_up, "fsdp", axis=0, tiled=True),
            lax.all_gather(w_down, "fsdp", axis=1, tiled=True),
            lax.all_gather(gain_attn, "fsdp", axis=0, tiled=True),
            lax.all_gather(gain_mlp, "fsdp", axis=0, tiled=True),
        )
        (
            full_query,
            full_key,
            full_value,
            full_out,
            full_gate,
            full_up,
            full_down,
            gain_full_one,
            gain_full_two,
        ) = gathered
        gain_one = gain_full_one.astype(jnp.float32)
        gain_two = gain_full_two.astype(jnp.float32)
        upstream = cotangent[batch_index].astype(jnp.float32)
        grad_branch = spread_grads(upstream.astype(jnp.bfloat16))
        term_down = dot_left_t(inner_low, grad_branch)
        grad_inner = dot_right_t(grad_branch, full_down)
        grad_gate_low = (
            grad_inner * up_pre * sigmoid_gate * (1.0 + gate_pre * (1.0 - sigmoid_gate))
        ).astype(jnp.bfloat16)
        grad_up_low = (grad_inner * activated).astype(jnp.bfloat16)
        term_gate = dot_left_t(seq_two, grad_gate_low)
        term_up = dot_left_t(seq_two, grad_up_low)
        grad_normed_two = collect_grads(
            (grad_gate_low, grad_up_low), (full_gate, full_up), local_rows
        )
        grad_res, term_gain_two = norm_back(hidden_res, scale_two, gain_two, grad_normed_two)
        grad_res = upstream + grad_res
        grad_attn = spread_grads(grad_res.astype(jnp.bfloat16))
        term_out = dot_left_t(mixed_low, grad_attn)
        grad_mixed = dot_right_t(grad_attn, full_out).astype(jnp.bfloat16)
        grad_qrot, grad_krot, grad_vfull = attend_back(
            query_rot, key_rot, value_low, span_first, log_total, grad_mixed, heads_kv
        )
        grad_query_low = (
            rotate_back(grad_qrot, cos_table, sine_table).astype(jnp.bfloat16).reshape(length, -1)
        )
        grad_key_low = (
            rotate_back(grad_krot, cos_table, sine_table).astype(jnp.bfloat16).reshape(length, -1)
        )
        grad_value_low = grad_vfull.astype(jnp.bfloat16).reshape(length, -1)
        term_query = dot_left_t(seq_one, grad_query_low)
        term_key = dot_left_t(seq_one, grad_key_low)
        term_value = dot_left_t(seq_one, grad_value_low)
        grad_normed_one = collect_grads(
            (grad_query_low, grad_key_low, grad_value_low),
            (full_query, full_key, full_value),
            local_rows,
        )
        grad_tokens, term_gain_one = norm_back(tokens, scale_one, gain_one, grad_normed_one)
        input_grads.append(grad_res + grad_tokens)
        local_sums = add_tuples(
            local_sums,
            (
                term_query,
                term_key,
                term_value,
                term_out,
                term_gate,
                term_up,
                term_down,
                term_gain_one,
                term_gain_two,
            ),
        )
    owner_sums = (
        lax.psum_scatter(
            local_sums[0].astype(jnp.bfloat16), "fsdp", scatter_dimension=0, tiled=True
        ).astype(jnp.float32),
        lax.psum_scatter(
            local_sums[1].astype(jnp.bfloat16), "fsdp", scatter_dimension=0, tiled=True
        ).astype(jnp.float32),
        lax.psum_scatter(
            local_sums[2].astype(jnp.bfloat16), "fsdp", scatter_dimension=0, tiled=True
        ).astype(jnp.float32),
        lax.psum_scatter(
            local_sums[3].astype(jnp.bfloat16), "fsdp", scatter_dimension=1, tiled=True
        ).astype(jnp.float32),
        lax.psum_scatter(
            local_sums[4].astype(jnp.bfloat16), "fsdp", scatter_dimension=0, tiled=True
        ).astype(jnp.float32),
        lax.psum_scatter(
            local_sums[5].astype(jnp.bfloat16), "fsdp", scatter_dimension=0, tiled=True
        ).astype(jnp.float32),
        lax.psum_scatter(
            local_sums[6].astype(jnp.bfloat16), "fsdp", scatter_dimension=1, tiled=True
        ).astype(jnp.float32),
        lax.psum_scatter(
            local_sums[7].astype(jnp.bfloat16), "fsdp", scatter_dimension=0, tiled=True
        ).astype(jnp.float32),
        lax.psum_scatter(
            local_sums[8].astype(jnp.bfloat16), "fsdp", scatter_dimension=0, tiled=True
        ).astype(jnp.float32),
    )
    gain_pair = lax.psum((owner_sums[7], owner_sums[8]), "tp")
    return (
        jnp.stack(outputs),
        jnp.stack(input_grads),
        owner_sums[0],
        owner_sums[1],
        owner_sums[2],
        owner_sums[3],
        owner_sums[4],
        owner_sums[5],
        owner_sums[6],
        gain_pair[0],
        gain_pair[1],
    )


def solution(mesh):
    placed = (
        P(None, ("fsdp", "tp"), None),
        P(None, "fsdp"),
        P("fsdp", "tp"),
        P("fsdp", "tp"),
        P("fsdp", "tp"),
        P("tp", "fsdp"),
        P("fsdp", "tp"),
        P("fsdp", "tp"),
        P("tp", "fsdp"),
        P("fsdp"),
        P("fsdp"),
        P(None, ("fsdp", "tp"), None),
    )
    return jax.shard_map(
        per_device,
        mesh=mesh,
        in_specs=placed,
        out_specs=(
            P(None, ("fsdp", "tp"), None),
            P(None, ("fsdp", "tp"), None),
            P("fsdp", "tp"),
            P("fsdp", "tp"),
            P("fsdp", "tp"),
            P("tp", "fsdp"),
            P("fsdp", "tp"),
            P("fsdp", "tp"),
            P("tp", "fsdp"),
            P("fsdp"),
            P("fsdp"),
        ),
        check_vma=False,
    )
```

profile of v0, /device:TPU:0, one launch (start us, length us, event | category | flops | bytes accessed | tf_op | source)
XLA Modules:
  0.0 1961.7 jit_solution(13358147699436139958)
XLA Ops:
  38.6 30.7 %all_gather.45 = bf16[2048,64]{0,1:T(8,128)(2,1)S(1)} all-gather(bf16[256,64]{0,1:T(8,128)(2,1)S(1)} %copy-done.128), channel_id=1, replica_groups=mesh['fsdp'=8,'tp'=4] {'fsdp'}, dimensions={0}, use_global_device_ids=true | all-gather | bytes 294912 | tf_op jit(solution)/shard_map/all_gather | solution.py:189
  72.1 30.7 %all_gather.44 = bf16[2048,64]{0,1:T(8,128)(2,1)S(1)} all-gather(bf16[256,64]{0,1:T(8,128)(2,1)S(1)} %copy-done.129), channel_id=1, replica_groups=mesh['fsdp'=8,'tp'=4] {'fsdp'}, dimensions={0}, use_global_device_ids=true | all-gather | bytes 294912 | tf_op jit(solution)/shard_map/all_gather | solution.py:190
  114.8 41.9 %all-gather.25.cloned.1.call-done = bf16[2048,512]{1,0:T(8,128)(2,1)} async-done(((bf16[256,512]{1,0:T(8,128)(2,1)}), bf16[2048,512]{1,0:T(8,128)(2,1)}) %all-gather.25.cloned.1.call-update) | async-done | bytes 2097168 | tf_op jit(solution)/shard_map/all_gather | solution.py:188
  172.8 35.4 %all-gather.27.cloned.1.call-done = bf16[512,2048]{1,0:T(8,128)(2,1)} async-done(((bf16[512,256]{1,0:T(8,128)(2,1)}), bf16[512,2048]{1,0:T(8,128)(2,1)}) %all-gather.27.cloned.1.call-update) | async-done | bytes 2097168 | tf_op jit(solution)/shard_map/all_gather | solution.py:191
  259.8 43.4 %reduce-scatter.28.cloned.1.call-done = f32[128,2048]{1,0:T(8,128)} async-done(((f32[512,2048]{1,0:T(8,128)}), f32[128,2048]{1,0:T(8,128)}) %reduce-scatter.28.cloned.1.call-update) | async-done | bytes 1048592 | tf_op jit(solution)/shard_map/reduce_scatter | solution.py:86
  303.2 47.1 %reduce-scatter.20.cloned.1.call-done = f32[128,2048]{1,0:T(8,128)} async-done(((f32[512,2048]{1,0:T(8,128)}), f32[128,2048]{1,0:T(8,128)}) %reduce-scatter.20.cloned.1.call-update) | async-done | bytes 1048592 | tf_op jit(solution)/shard_map/reduce_scatter | solution.py:86
  357.8 87.5 %all-gather.31.cloned.1.call-done = bf16[2048,1408]{1,0:T(8,128)(2,1)} async-done(((bf16[256,1408]{1,0:T(8,128)(2,1)}), bf16[2048,1408]{1,0:T(8,128)(2,1)}) %all-gather.31.cloned.1.call-update) | async-done | bytes 5767184 | tf_op jit(solution)/shard_map/all_gather | solution.py:192
  445.3 22.9 %all-gather.29.cloned.1.call-done = bf16[512,2048]{1,0:T(8,128)(2,1)} async-done(((bf16[128,2048]{1,0:T(8,128)(2,1)}), bf16[512,2048]{1,0:T(8,128)(2,1)}) %all-gather.29.cloned.1.call-update) | async-done | bytes 2097168 | tf_op jit(solution)/shard_map/all_gather | solution.py:74
  476.5 86.8 %all-gather.33.cloned.1.call-done = bf16[2048,1408]{1,0:T(8,128)(2,1)} async-done(((bf16[256,1408]{1,0:T(8,128)(2,1)}), bf16[2048,1408]{1,0:T(8,128)(2,1)}) %all-gather.33.cloned.1.call-update) | async-done | bytes 5767184 | tf_op jit(solution)/shard_map/all_gather | solution.py:193
  586.2 95.9 %all-gather.35.cloned.1.call-done = bf16[1408,2048]{1,0:T(8,128)(2,1)} async-done(((bf16[1408,256]{1,0:T(8,128)(2,1)}), bf16[1408,2048]{1,0:T(8,128)(2,1)}) %all-gather.35.cloned.1.call-update) | async-done | bytes 5767184 | tf_op jit(solution)/shard_map/all_gather | solution.py:194
  711.3 35.1 %reduce-scatter.32.cloned.1.call-done = f32[128,2048]{1,0:T(8,128)} async-done(((f32[512,2048]{1,0:T(8,128)}), f32[128,2048]{1,0:T(8,128)}) %reduce-scatter.32.cloned.1.call-update) | async-done | bytes 1048592 | tf_op jit(solution)/shard_map/reduce_scatter | solution.py:102
  746.4 46.9 %reduce-scatter.22.cloned.1.call-done = f32[128,2048]{1,0:T(8,128)} async-done(((f32[512,2048]{1,0:T(8,128)}), f32[128,2048]{1,0:T(8,128)}) %reduce-scatter.22.cloned.1.call-update) | async-done | bytes 1048592 | tf_op jit(solution)/shard_map/reduce_scatter | solution.py:86
  940.9 47.1 %reduce-scatter.30.cloned.1.call-done = f32[128,2048]{1,0:T(8,128)} async-done(((f32[512,2048]{1,0:T(8,128)}), f32[128,2048]{1,0:T(8,128)}) %reduce-scatter.30.cloned.1.call-update) | async-done | bytes 1048592 | tf_op jit(solution)/shard_map/reduce_scatter | solution.py:86
  988.0 47.2 %reduce-scatter.36.cloned.1.call-done = f32[128,2048]{1,0:T(8,128)} async-done(((f32[512,2048]{1,0:T(8,128)}), f32[128,2048]{1,0:T(8,128)}) %reduce-scatter.36.cloned.1.call-update) | async-done | bytes 1048592 | tf_op jit(solution)/shard_map/reduce_scatter | solution.py:102
  1035.2 47.1 %reduce-scatter.26.cloned.1.call-done = f32[128,2048]{1,0:T(8,128)} async-done(((f32[512,2048]{1,0:T(8,128)}), f32[128,2048]{1,0:T(8,128)}) %reduce-scatter.26.cloned.1.call-update) | async-done | bytes 1048592 | tf_op jit(solution)/shard_map/reduce_scatter | solution.py:86
  1285.0 107.5 %reduce-scatter.56.cloned.1.call-done = bf16[1408,256]{1,0:T(8,128)(2,1)} async-done(((bf16[1408,2048]{1,0:T(8,128)(2,1)}), bf16[1408,256]{1,0:T(8,128)(2,1)}) %reduce-scatter.56.cloned.1.call-update) | async-done | bytes 720912 | tf_op jit(solution)/shard_map/reduce_scatter | solution.py:327
  1394.9 111.6 %reduce-scatter.52.cloned.1.call-done = bf16[256,1408]{1,0:T(8,128)(2,1)} async-done(((bf16[2048,1408]{1,0:T(8,128)(2,1)}), bf16[256,1408]{1,0:T(8,128)(2,1)}) %reduce-scatter.52.cloned.1.call-update) | async-done | bytes 720912 | tf_op jit(solution)/shard_map/reduce_scatter | solution.py:321
  1508.7 62.7 %reduce-scatter.48.cloned.1.call-done = bf16[256,64]{0,1:T(8,128)(2,1)} async-done(((bf16[2048,64]{0,1:T(8,128)(2,1)}), bf16[256,64]{0,1:T(8,128)(2,1)}) %reduce-scatter.48.cloned.1.call-update) | async-done | bytes 32784 | tf_op jit(solution)/shard_map/reduce_scatter | solution.py:315
  1572.8 63.1 %reduce-scatter.46.cloned.1.call-done = bf16[256,64]{0,1:T(8,128)(2,1)} async-done(((bf16[2048,64]{0,1:T(8,128)(2,1)}), bf16[256,64]{0,1:T(8,128)(2,1)}) %reduce-scatter.46.cloned.1.call-update) | async-done | bytes 32784 | tf_op jit(solution)/shard_map/reduce_scatter | solution.py:312
  1637.3 69.8 %reduce-scatter.50.cloned.1.call-done = bf16[512,256]{1,0:T(8,128)(2,1)} async-done(((bf16[512,2048]{1,0:T(8,128)(2,1)}), bf16[512,256]{1,0:T(8,128)(2,1)}) %reduce-scatter.50.cloned.1.call-update) | async-done | bytes 262160 | tf_op jit(solution)/shard_map/reduce_scatter | solution.py:318
  1708.9 69.2 %reduce-scatter.44.cloned.1.call-done = bf16[256,512]{1,0:T(8,128)(2,1)} async-done(((bf16[2048,512]{1,0:T(8,128)(2,1)}), bf16[256,512]{1,0:T(8,128)(2,1)}) %reduce-scatter.44.cloned.1.call-update) | async-done | bytes 262160 | tf_op jit(solution)/shard_map/reduce_scatter | solution.py:309
  1779.9 44.4 %reduce-scatter.38.cloned.1.call-done = f32[128,2048]{1,0:T(8,128)} async-done(((f32[512,2048]{1,0:T(8,128)}), f32[128,2048]{1,0:T(8,128)}) %reduce-scatter.38.cloned.1.call-update) | async-done | bytes 1048592 | tf_op jit(solution)/shard_map/reduce_scatter | solution.py:102
  1824.3 47.1 %reduce-scatter.42.cloned.1.call-done = f32[128,2048]{1,0:T(8,128)} async-done(((f32[512,2048]{1,0:T(8,128)}), f32[128,2048]{1,0:T(8,128)}) %reduce-scatter.42.cloned.1.call-update) | async-done | bytes 1048592 | tf_op jit(solution)/shard_map/reduce_scatter | solution.py:102
  1871.4 47.1 %reduce-scatter.34.cloned.1.call-done = f32[128,2048]{1,0:T(8,128)} async-done(((f32[512,2048]{1,0:T(8,128)}), f32[128,2048]{1,0:T(8,128)}) %reduce-scatter.34.cloned.1.call-update) | async-done | bytes 1048592 | tf_op jit(solution)/shard_map/reduce_scatter | solution.py:102
  (591 shorter events, 574.1 us)
Async XLA Ops:
  37.3 119.4 %all-gather.25.cloned.1.call-start = ((), (), s32[]{:S(2)}) async-start(), calls=%async_computation.20 | async-start | bytes 2359296 | tf_op jit(solution)/shard_map/all_gather | solution.py:188
  37.9 170.3 %all-gather.27.cloned.1.call-start = ((), (), s32[]{:S(2)}) async-start(), calls=%async_computation.21 | async-start | bytes 2359296 | tf_op jit(solution)/shard_map/all_gather | solution.py:191
  38.5 221.3 %reduce-scatter.24.cloned.1.call-start = ((), (), s32[]{:S(2)}) async-start(), calls=%async_computation.29 | async-start | bytes 5242880 | tf_op jit(solution)/shard_map/reduce_scatter | solution.py:86
  228.2 122.0 %reduce-scatter.20.cloned.1.call-start = ((), (), s32[]{:S(2)}) async-start(), calls=%async_computation.22 | async-start | bytes 5242880 | tf_op jit(solution)/shard_map/reduce_scatter | solution.py:86
  241.1 204.3 %all-gather.31.cloned.1.call-start = ((), (), s32[]{:S(2)}) async-start(), calls=%async_computation.24 | async-start | bytes 6488064 | tf_op jit(solution)/shard_map/all_gather | solution.py:192
  241.8 226.4 %all-gather.29.cloned.1.call-start = ((), (), s32[]{:S(2)}) async-start(), calls=%async_computation.23 | async-start | bytes 2621440 | tf_op jit(solution)/shard_map/all_gather | solution.py:74
  354.9 208.4 %all-gather.33.cloned.1.call-start = ((), (), s32[]{:S(2)}) async-start(), calls=%async_computation.25 | async-start | bytes 6488064 | tf_op jit(solution)/shard_map/all_gather | solution.py:193
  355.6 230.6 %all-gather.51.cloned.1.call-start = ((), (), s32[]{:S(2)}) async-start(), calls=%async_computation.52 | async-start | bytes 2621440 | tf_op jit(solution)/shard_map/all_gather | solution.py:78
  356.9 325.2 %all-gather.35.cloned.1.call-start = ((), (), s32[]{:S(2)}) async-start(), calls=%async_computation.26 | async-start | bytes 6488064 | tf_op jit(solution)/shard_map/all_gather | solution.py:194
  357.6 388.8 %reduce-scatter.32.cloned.1.call-start = ((), (), s32[]{:S(2)}) async-start(), calls=%async_computation.36 | async-start | bytes 5242880 | tf_op jit(solution)/shard_map/reduce_scatter | solution.py:102
  799.4 141.6 %reduce-scatter.40.cloned.1.call-start = ((), (), s32[]{:S(2)}) async-start(), calls=%async_computation.42 | async-start | bytes 5242880 | tf_op jit(solution)/shard_map/reduce_scatter | solution.py:102
  878.6 156.6 %reduce-scatter.36.cloned.1.call-start = ((), (), s32[]{:S(2)}) async-start(), calls=%async_computation.39 | async-start | bytes 5242880 | tf_op jit(solution)/shard_map/reduce_scatter | solution.py:102
  919.8 162.5 %reduce-scatter.26.cloned.1.call-start = ((), (), s32[]{:S(2)}) async-start(), calls=%async_computation.31 | async-start | bytes 5242880 | tf_op jit(solution)/shard_map/reduce_scatter | solution.py:86
  928.6 250.2 %all-gather.49.cloned.1.call-start = ((), (), s32[]{:S(2)}) async-start(), calls=%async_computation.43 | async-start | bytes 2621440 | tf_op jit(solution)/shard_map/all_gather | solution.py:78
  1093.4 189.3 %reduce-scatter.54.cloned.1.call-start = ((), (), s32[]{:S(2)}) async-start(), calls=%async_computation.50 | async-start | bytes 6488064 | tf_op jit(solution)/shard_map/reduce_scatter | solution.py:324
  1121.7 270.8 %reduce-scatter.56.cloned.1.call-start = ((), (), s32[]{:S(2)}) async-start(), calls=%async_computation.51 | async-start | bytes 6488064 | tf_op jit(solution)/shard_map/reduce_scatter | solution.py:327
  1150.5 355.9 %reduce-scatter.52.cloned.1.call-start = ((), (), s32[]{:S(2)}) async-start(), calls=%async_computation.49 | async-start | bytes 6488064 | tf_op jit(solution)/shard_map/reduce_scatter | solution.py:321
  1178.0 393.4 %reduce-scatter.48.cloned.1.call-start = ((), (), s32[]{:S(2)}) async-start(), calls=%async_computation.47 | async-start | bytes 294912 | tf_op jit(solution)/shard_map/reduce_scatter | solution.py:315
  1233.9 402.0 %reduce-scatter.46.cloned.1.call-start = ((), (), s32[]{:S(2)}) async-start(), calls=%async_computation.46 | async-start | bytes 294912 | tf_op jit(solution)/shard_map/reduce_scatter | solution.py:312
  1238.3 468.8 %reduce-scatter.50.cloned.1.call-start = ((), (), s32[]{:S(2)}) async-start(), calls=%async_computation.48 | async-start | bytes 2359296 | tf_op jit(solution)/shard_map/reduce_scatter | solution.py:318
  1245.7 532.4 %reduce-scatter.44.cloned.1.call-start = ((), (), s32[]{:S(2)}) async-start(), calls=%async_computation.45 | async-start | bytes 2359296 | tf_op jit(solution)/shard_map/reduce_scatter | solution.py:309
  1260.4 563.9 %reduce-scatter.38.cloned.1.call-start = ((), (), s32[]{:S(2)}) async-start(), calls=%async_computation.41 | async-start | bytes 5242880 | tf_op jit(solution)/shard_map/reduce_scatter | solution.py:102
  1267.2 604.2 %reduce-scatter.42.cloned.1.call-start = ((), (), s32[]{:S(2)}) async-start(), calls=%async_computation.44 | async-start | bytes 5242880 | tf_op jit(solution)/shard_map/reduce_scatter | solution.py:102
  1273.2 645.2 %reduce-scatter.34.cloned.1.call-start = ((), (), s32[]{:S(2)}) async-start(), calls=%async_computation.38 | async-start | bytes 5242880 | tf_op jit(solution)/shard_map/reduce_scatter | solution.py:102
  (182 other events, 7110.2 us)
Sparse Core Ops, SparseCore 0:
  107.4 49.2 all-gather.24
  158.6 49.5 all-gather.26
  213.2 42.7 reduce-scatter.23
  258.7 44.4 reduce-scatter.27
  305.7 44.5 reduce-scatter.19
  352.7 92.6 all-gather.30
  470.6 92.6 all-gather.32
  588.4 93.5 all-gather.34
  703.6 42.6 reduce-scatter.31
  748.8 44.4 reduce-scatter.21
  896.4 44.5 reduce-scatter.39
  943.5 44.4 reduce-scatter.29
  990.7 44.4 reduce-scatter.35
  1037.7 44.4 reduce-scatter.25
  1168.2 109.9 reduce-scatter.53
  1282.3 110.1 reduce-scatter.55
  1396.6 109.7 reduce-scatter.51
  1510.0 61.4 reduce-scatter.47
  1575.1 60.7 reduce-scatter.45
  1639.8 67.2 reduce-scatter.49
  1711.5 66.5 reduce-scatter.43
  1780.8 43.5 reduce-scatter.37
  1826.9 44.4 reduce-scatter.41
  1873.9 44.4 reduce-scatter.33
  (12 shorter events, 264.1 us)
where the time goes:
time: 1970 us; the launch traced here: 1960 us
  waiting for transfers between devices  1370 us (70%)
  matrix products  336 us (17%)
  blocking collectives  130 us (7%)
  other arithmetic  72.6 us (4%)
  local copies, waits for them, and re-layouts  30.3 us (2%)
    reduce_scatter x6, waiting for transfers between devices, collect_grads(): lax.psum_scatter(term_rows(jnp.int32(0), local_rows * lax.axis_size('tp')...  233 us
    reduce_scatter x6, waiting for transfers between devices, collect_out(): lax.psum_scatter(term_rows(jnp.int32(0), local_rows * lax.axis_size('tp')...  232 us
    reduce_scatter x1, waiting for transfers between devices, per_device(): lax.psum_scatter(local_sums[4].astype(jnp.bfloat16), 'fsdp', scatter_dime...  112 us
    reduce_scatter x1, waiting for transfers between devices, per_device(): lax.psum_scatter(local_sums[6].astype(jnp.bfloat16), 'fsdp', scatter_dime...  108 us
    dot_general x21, matrix products, dot_plain(): return jnp.dot(left_side, right_side, preferred_element_type=jnp.float32)  104 us
    dot_general x21, matrix products, dot_left_t(): lax.dot_general(left_side, right_side, (((0,), (0,)), ((), ())), preferre...  98.1 us
    all_gather x1, waiting for transfers between devices, per_device(): lax.all_gather(w_down, 'fsdp', axis=1, tiled=True)  95.9 us
    dot_general x21, matrix products, dot_right_t(): lax.dot_general(left_side, right_side, (((1,), (1,)), ((), ())), preferre...  95.1 us
  transfers between devices with their start and end apart: 36, of which 26 were waited for; matrix products, arithmetic and copies ran while one was open for 18% of the time, Pallas kernels for 0%

commit v1 on v0

v1 whole, which is shorter than its diff:
```python
import functools
import math

import jax
import jax.numpy as jnp
from jax import lax
from jax.experimental import pallas as pl
from jax.experimental.pallas import tpu as pltpu
from jax.sharding import Mesh, PartitionSpec as P

HD = 64
PAIR = 2 * HD
SPAN = 256
EPS = 1e-05
MASKED = -1e30
F32 = jnp.float32
BF16 = jnp.bfloat16
SWAP = [(0, 1), (1, 0)]
ROW_PAD = 16


def dot(a, b):
    return jnp.dot(a, b, preferred_element_type=F32)


def dot_lt(a, b):
    return lax.dot_general(a, b, (((0,), (0,)), ((), ())), preferred_element_type=F32)


def dot_rt(a, b):
    return lax.dot_general(a, b, (((1,), (1,)), ((), ())), preferred_element_type=F32)


def swap(value, axis):
    return lax.ppermute(value, axis, SWAP)


def after(value, *others):
    return lax.optimization_barrier((value, *others))[0]


def both_after(pair, *others):
    kept = lax.optimization_barrier((*pair, *others))
    return kept[0], kept[1]


def full_spec(shape):
    return pl.BlockSpec(shape, lambda i, *_: (0,) * len(shape))


def row_spec(rows, cols, offset=0):
    return pl.BlockSpec((rows, cols), lambda i, *_: (i + offset, 0))


def quad_spec(rows, cols):
    return pl.BlockSpec((4, 1, rows, cols), lambda i, *_: (0, i, 0, 0))


def call(kernel, scalars, grid, ins, outs, scratch=(), flops=0, exps=0):
    moved = sum(a.size * a.dtype.itemsize for a, _ in ins)
    moved += sum(math.prod(shape) * jnp.dtype(kind).itemsize for shape, kind, _ in outs)
    return pl.pallas_call(
        kernel,
        out_shape=[jax.ShapeDtypeStruct(shape, kind) for shape, kind, _ in outs],
        grid_spec=pltpu.PrefetchScalarGridSpec(
            num_scalar_prefetch=len(scalars),
            grid=(grid,),
            in_specs=[spec for _, spec in ins],
            out_specs=[spec for _, _, spec in outs],
            scratch_shapes=list(scratch),
        ),
        cost_estimate=pl.CostEstimate(flops=flops, bytes_accessed=moved, transcendentals=exps),
        compiler_params=pltpu.CompilerParams(vmem_limit_bytes=56 << 20),
    )(*scalars, *[a for a, _ in ins])


def halves_of(value, hi, x):
    width = value.shape[-1] // (2 * hi)
    parts = [value[:, k * width : (k + 1) * width] for k in range(2 * hi)]
    even, odd = parts[0::2], parts[1::2]
    own = [jnp.where(x == 0, a, b) for a, b in zip(even, odd)]
    oth = [jnp.where(x == 0, b, a) for a, b in zip(even, odd)]
    return own, oth


def put_cols(ref, index, parts):
    width = parts[0].shape[-1]
    for k, part in enumerate(parts):
        ref[(*index, slice(None), slice(k * width, (k + 1) * width))] = part.astype(ref.dtype)


def join_to(ref, own, oth, hi, x):
    width = own.shape[-1] // hi
    for k in range(hi):
        a, b = own[:, k * width : (k + 1) * width], oth[:, k * width : (k + 1) * width]
        ref[:, 2 * k * width : (2 * k + 1) * width] = jnp.where(x == 0, a, b)
        ref[:, (2 * k + 1) * width : (2 * k + 2) * width] = jnp.where(x == 0, b, a)


def norm_in_kernel(hi, at, p0, p1, p2, p3, gain_own, gain_oth, n_own, n_oth, x_own, x_oth):
    x = at[0]
    half = n_own.shape[-1]
    for k, piece in enumerate((p0, p1, p2, p3)):
        low = piece[...]
        value = low.astype(F32)
        scale = lax.rsqrt(jnp.mean(value * value, axis=-1, keepdims=True) + EPS)
        own, oth = halves_of(value, hi, x)
        width = half // hi
        for part, gain, ref in ((own, gain_own, n_own), (oth, gain_oth, n_oth)):
            put_cols(
                ref, (k, 0), [v * scale * gain[:, z * width : (z + 1) * width] for z, v in enumerate(part)]
            )
        if k == 0:
            put_cols(x_own, (), own)
            put_cols(x_oth, (), oth)


def spread_kernel(hi, at, p0, p1, p2, p3, o_own, o_oth):
    x = at[0]
    for k, piece in enumerate((p0, p1, p2, p3)):
        own, oth = halves_of(piece[...], hi, x)
        put_cols(o_own, (k, 0), own)
        put_cols(o_oth, (k, 0), oth)


def stack_kernel(p0, p1, p2, p3, o_own, o_oth):
    half = o_own.shape[-1]
    for k, piece in enumerate((p0, p1, p2, p3)):
        o_own[k, 0] = piece[:, :half]
        o_oth[k, 0] = piece[:, half:]


def rows_scale(own, oth):
    total = jnp.sum(own * own, axis=-1, keepdims=True) + jnp.sum(oth * oth, axis=-1, keepdims=True)
    return lax.rsqrt(total / (own.shape[-1] + oth.shape[-1]) + EPS)


def summed(refs):
    return refs[0][...].astype(F32) + refs[1][...].astype(F32) + refs[2][...].astype(F32)


def residual_kernel(x_own, x_oth, a0, a1, a2, b0, b1, b2, gain_own, gain_oth, h_own, h_oth, n_out):
    own = x_own[...].astype(F32) + summed((a0, a1, a2))
    oth = x_oth[...].astype(F32) + summed((b0, b1, b2))
    scale = rows_scale(own, oth)
    half = own.shape[-1]
    h_own[...] = own
    h_oth[...] = oth
    n_out[:, :half] = (own * scale * gain_own[...]).astype(BF16)
    n_out[:, half:] = (oth * scale * gain_oth[...]).astype(BF16)


def block_out_kernel(hi, at, h_own, h_oth, a0, a1, a2, b0, b1, b2, out):
    join_to(out, h_own[...] + summed((a0, a1, a2)), h_oth[...] + summed((b0, b1, b2)), hi, at[0])


def back_of(own, oth, scale, gain_own, gain_oth, up_own, up_oth):
    w_own, w_oth = up_own * gain_own, up_oth * gain_oth
    total = jnp.sum(w_own * own, axis=-1, keepdims=True) + jnp.sum(w_oth * oth, axis=-1, keepdims=True)
    cube = scale * scale * scale * (total / (own.shape[-1] + oth.shape[-1]))
    return scale * w_own - own * cube, scale * w_oth - oth * cube


def middle_kernel(
    h_own, h_oth, a0, a1, a2, b0, b1, b2, gain_own, gain_oth, u_own, u_oth, r_own, r_oth, low_out, s_own, s_oth
):
    own, oth = h_own[...], h_oth[...]
    up_own, up_oth = summed((a0, a1, a2)), summed((b0, b1, b2))
    scale = rows_scale(own, oth)
    back_own, back_oth = back_of(own, oth, scale, gain_own[...], gain_oth[...], up_own, up_oth)
    back_own = u_own[...].astype(F32) + back_own
    back_oth = u_oth[...].astype(F32) + back_oth
    half = own.shape[-1]
    r_own[...] = back_own
    r_oth[...] = back_oth
    low_out[:, :half] = back_own.astype(BF16)
    low_out[:, half:] = back_oth.astype(BF16)

    @pl.when(pl.program_id(0) == 0)
    def _():
        s_own[...] = jnp.zeros_like(s_own)
        s_oth[...] = jnp.zeros_like(s_oth)

    s_own[...] += jnp.sum(up_own * own * scale, axis=0, keepdims=True)
    s_oth[...] += jnp.sum(up_oth * oth * scale, axis=0, keepdims=True)


def grad_in_kernel(hi, at, x_own, x_oth, a0, a1, a2, b0, b1, b2, gain_own, gain_oth, r_own, r_oth, out):
    own, oth = x_own[...].astype(F32), x_oth[...].astype(F32)
    scale = rows_scale(own, oth)
    back_own, back_oth = back_of(
        own, oth, scale, gain_own[...], gain_oth[...], summed((a0, a1, a2)), summed((b0, b1, b2))
    )
    join_to(out, r_own[...] + back_own, r_oth[...] + back_oth, hi, at[0])


def partner(value):
    lane = lax.broadcasted_iota(jnp.int32, value.shape, 1)
    return jnp.where(lane % HD < HD // 2, pltpu.roll(value, PAIR - HD // 2, 1), pltpu.roll(value, HD // 2, 1))


def low_lanes(shape):
    return lax.broadcasted_iota(jnp.int32, shape, 1) < HD


def set_bias(bias, key_at, query_at, first):
    keys, queries = key_at[...], query_at[...]
    key_in = ((keys >= first) & (keys < first + SPAN)).astype(jnp.int32)
    query_in = ((queries >= first) & (queries < first + SPAN)).astype(jnp.int32)
    seen = (keys <= queries).astype(jnp.int32) + key_in * query_in
    bias[...] = jnp.where(seen > 0, 0.0, MASKED)


def attend_kernel(pairs, span, qkv, cos, sine, key_at, query_at, q_out, kv_out, o_out, lse_out, bias, key_s, val_s):
    length = cos.shape[0]
    set_bias(bias, key_at, query_at, span[pl.program_id(0)])
    kv = qkv[:, 0, :, pairs * PAIR :].reshape(length, PAIR)
    low = low_lanes(kv.shape)
    turned = kv * cos[...] + partner(kv) * sine[...]
    kv = jnp.where(low, turned, kv).astype(BF16)
    kv_out[:, 0] = kv.reshape(4, length // 4, PAIR)
    wide = kv.astype(F32)
    key_even = jnp.where(low, wide, 0.0)
    val_odd = jnp.where(low, 0.0, wide)
    key_s[0] = key_even.astype(BF16)
    key_s[1] = pltpu.roll(key_even, HD, 1).astype(BF16)
    val_s[0] = pltpu.roll(val_odd, HD, 1).T.astype(BF16)
    val_s[1] = val_odd.T.astype(BF16)

    def pair_step(j, _):
        cols = pl.ds(pl.multiple_of(j * PAIR, PAIR), PAIR)
        raw = qkv[:, 0, :, cols].reshape(length, PAIR)
        query = (raw * cos[...] + partner(raw) * sine[...]).astype(BF16)
        q_out[:, 0, :, cols] = query.reshape(4, length // 4, PAIR)
        query_t = (query.astype(F32) * HD**-0.5).T.astype(BF16)
        mixed = jnp.zeros((PAIR, length), F32)
        for k in range(2):
            scores = dot(key_s[k], query_t) + bias[...]
            top = jnp.max(scores, axis=0, keepdims=True)
            raised = jnp.exp(scores - top)
            total = jnp.sum(raised, axis=0, keepdims=True)
            lse_out[0, pl.ds(2 * j + k, 1), :] = top + jnp.log(total)
            mixed += dot(val_s[k], (raised * (1.0 / total)).astype(BF16))
        o_out[:, 0, :, cols] = mixed.T.astype(BF16).reshape(4, length // 4, PAIR)
        return 0

    lax.fori_loop(0, pairs, pair_step, 0)


def attend_back_kernel(
    pairs, span, query_in, kv_in, grad_in, lse, cos, sine, key_at, query_at, out, bias, key_s, key_t, val_s, key_g, val_g
):
    length = cos.shape[0]
    set_bias(bias, key_at, query_at, span[pl.program_id(0)])
    kv = kv_in[:, 0].reshape(length, PAIR).astype(F32)
    low = low_lanes(kv.shape)
    key_even = jnp.where(low, kv, 0.0)
    key_odd = pltpu.roll(key_even, HD, 1)
    val_odd = jnp.where(low, 0.0, kv)
    key_s[0] = key_even.astype(BF16)
    key_s[1] = key_odd.astype(BF16)
    key_t[0] = key_even.T.astype(BF16)
    key_t[1] = key_odd.T.astype(BF16)
    val_s[0] = pltpu.roll(val_odd, HD, 1).astype(BF16)
    val_s[1] = val_odd.astype(BF16)
    key_g[...] = jnp.zeros_like(key_g)
    val_g[...] = jnp.zeros_like(val_g)

    def pair_step(j, _):
        cols = pl.ds(pl.multiple_of(j * PAIR, PAIR), PAIR)
        query = query_in[:, 0, :, cols].reshape(length, PAIR)
        grad = grad_in[:, 0, :, cols].reshape(length, PAIR)
        query_t = (query.astype(F32) * HD**-0.5).T.astype(BF16)
        grad_t = grad.astype(F32).T.astype(BF16)
        query_g = jnp.zeros((PAIR, length), F32)
        for k in range(2):
            scores = dot(key_s[k], query_t) + bias[...]
            weight = jnp.exp(scores - lse[0, pl.ds(2 * j + k, 1), :])
            weight_g = dot(val_s[k], grad_t)
            val_g[k] += dot(weight.astype(BF16), grad)
            delta = jnp.sum(weight * weight_g, axis=0, keepdims=True)
            score_g = (HD**-0.5 * (weight * (weight_g - delta))).astype(BF16)
            key_g[k] += dot(score_g, query)
            query_g += dot(key_t[k], score_g)
        value = query_g.T
        value = value * cos[...] - partner(value) * sine[...]
        out[:, 0, :, cols] = value.astype(BF16).reshape(4, length // 4, PAIR)
        return 0

    lax.fori_loop(0, pairs, pair_step, 0)
    keys = key_g[0] + pltpu.roll(key_g[1], HD, 1)
    vals = val_g[1] + pltpu.roll(val_g[0], HD, 1)
    keys = keys * cos[...] - partner(keys) * sine[...]
    out[:, 0, :, pairs * PAIR :] = jnp.where(low, keys, vals).astype(BF16).reshape(4, length // 4, PAIR)


def per_device(
    block_in, span_start, w_query, w_key, w_value, w_out, w_gate, w_up, w_down, gain_attn, gain_mlp, cotangent
):
    x, y, c = lax.axis_index("fl"), lax.axis_index("th"), lax.axis_index("tl")
    hi = lax.axis_size("fh")
    batch, rows, width = block_in.shape
    own_rows, half = batch * rows, width // 2
    length = rows * 4
    depth = w_query.shape[0]
    q_cols, kv_cols = w_query.shape[1], w_key.shape[1]
    pairs = q_cols // PAIR
    at = jnp.stack([x]).astype(jnp.int32)

    shard = jnp.concatenate([w_query, w_key, w_value], axis=1)
    gains = jnp.concatenate([gain_attn, gain_mlp])[None]
    gains = jnp.pad(gains, ((0, ROW_PAD - 1), (0, shard.shape[1] - gains.shape[1])))
    shards = (jnp.concatenate([shard, gains], axis=0), w_out.T, w_gate, w_up, w_down.T)

    def gather_x(own):
        return own, swap(own, "fl")

    def flat(pair):
        return tuple(part.reshape(hi * depth, -1) for part in pair)

    own_parts = [lax.all_gather(part, "fh", axis=0, tiled=True) for part in shards]
    own_parts[0] = own_parts[0].reshape(hi, depth + ROW_PAD, -1)

    def gather_rows(piece):
        beside = swap(piece, "tl")
        across = swap(piece, "th")
        return piece, across, beside, swap(across, "tl")

    token_parts = gather_rows(block_in.reshape(own_rows, width))
    cot_parts = gather_rows(cotangent.reshape(own_rows, width))

    place = jnp.concatenate(
        [(((y + dy) % 2) * 2 + (c + dc) % 2) * rows + jnp.arange(rows, dtype=jnp.int32) for dc in (0, 1) for dy in (0, 1)]
    )
    frequency = jnp.exp(jnp.arange(HD // 2, dtype=F32) * (-2.0 * math.log(10000.0) / HD))
    angles = place.astype(F32)[:, None] * frequency[None, :]
    cos = jnp.tile(jnp.cos(angles), (1, 4))
    sine = jnp.sin(angles)
    sine = jnp.concatenate([-sine, sine, -sine, sine], axis=1)
    key_at, query_at = place[:, None], place[None, :]
    span = span_start[:, 0]
    tables = [(t, full_spec(t.shape)) for t in (cos, sine, key_at, query_at)]

    quad = (4, batch, rows)
    pieces = lambda parts: [(p, row_spec(rows, width)) for p in parts]
    spread_outs = [(quad + (half,), BF16, quad_spec(rows, half))] * 2

    def as_rows(value):
        return value.reshape(4 * own_rows, value.shape[-1])

    seq_cot = call(functools.partial(spread_kernel, hi), [at], batch, pieces(cot_parts), spread_outs)
    seq_cot = tuple(as_rows(v) for v in seq_cot)

    qkv_pair = gather_x(own_parts[0])
    out_pair = gather_x(own_parts[1])
    qkv_w = tuple(part[:, :depth].reshape(hi * depth, -1) for part in qkv_pair)
    gain_one = tuple(part[:, depth, :depth].reshape(1, half).astype(F32) for part in qkv_pair)
    gain_two = tuple(part[:, depth, depth : 2 * depth].reshape(1, half).astype(F32) for part in qkv_pair)
    gain_in = lambda gain: [(g, full_spec((1, half))) for g in gain]

    *seq_one, x_own, x_oth = call(
        functools.partial(norm_in_kernel, hi),
        [at],
        batch,
        pieces(token_parts) + gain_in(gain_one),
        spread_outs + [((own_rows, half), BF16, row_spec(rows, half))] * 2,
    )
    seq_one = tuple(as_rows(v) for v in seq_one)

    qkv = dot(seq_one[0], qkv_w[0]) + dot(seq_one[1], qkv_w[1])
    all_cols = qkv.shape[1]
    pair_spec, q_spec = quad_spec(rows, PAIR), quad_spec(rows, q_cols)
    lse_spec = pl.BlockSpec((1, 2 * pairs, length), lambda i, *_: (i, 0, 0))
    score_flops = 2 * batch * 2 * pairs * length * length * PAIR
    score_exps = batch * 2 * pairs * length * length
    query_rot, kv_rot, mixed, lse = call(
        functools.partial(attend_kernel, pairs),
        [span],
        batch,
        [(qkv.reshape(quad + (all_cols,)), quad_spec(rows, all_cols)), *tables],
        [
            (quad + (q_cols,), BF16, q_spec),
            (quad + (PAIR,), BF16, pair_spec),
            (quad + (q_cols,), BF16, q_spec),
            ((batch, 2 * pairs, length), F32, lse_spec),
        ],
        [
            pltpu.VMEM((length, length), F32),
            pltpu.VMEM((2, length, PAIR), BF16),
            pltpu.VMEM((2, PAIR, length), BF16),
        ],
        flops=2 * score_flops,
        exps=score_exps,
    )
    mixed = after(as_rows(mixed), own_parts[2])

    def scatter_rows(partial):
        came = swap(partial[2 * own_rows :], "tl")
        sent = (partial[own_rows : 2 * own_rows].astype(F32) + came[own_rows:].astype(F32)).astype(BF16)
        return partial, came, swap(sent, "th")

    def terms(pair):
        return [(t, row_spec(rows, half)) for part in pair for t in part]

    out_w = flat(out_pair)
    attn_terms = [scatter_rows(dot_rt(mixed, w).astype(BF16)) for w in out_w]
    half_ins = lambda *values: [(v, row_spec(rows, half)) for v in values]
    half_outs = [((own_rows, half), F32, row_spec(rows, half))] * 2
    low_out = [((own_rows, width), BF16, row_spec(rows, width))]
    h_own, h_oth, normed_two = call(
        residual_kernel,
        [],
        batch,
        half_ins(after(x_own, own_parts[3]), x_oth) + terms(attn_terms) + gain_in(gain_two),
        half_outs + low_out,
    )

    def stack_rows(low, *others):
        parts = gather_rows(low)
        parts = (after(parts[0], *others), *parts[1:]) if others else parts
        return tuple(as_rows(v) for v in call(stack_kernel, [], batch, pieces(parts), spread_outs))

    gate_w, up_w = flat(gather_x(own_parts[2])), flat(gather_x(own_parts[3]))
    normed_two = after(normed_two, gate_w[1])
    seq_two = stack_rows(normed_two, own_parts[4], up_w[1])

    gate_pre = dot(seq_two[0], gate_w[0]) + dot(seq_two[1], gate_w[1])
    up_pre = dot(seq_two[0], up_w[0]) + dot(seq_two[1], up_w[1])
    sigmoid = jax.nn.sigmoid(gate_pre)
    activated = gate_pre * sigmoid
    inner = (activated * up_pre).astype(BF16)
    down_w = flat(gather_x(own_parts[4]))

    def send_grad(oth, grad):
        return dot_lt(oth, grad).astype(BF16)

    def total_grad(own, grad, came):
        return (dot_lt(own, grad) + came.astype(F32)).astype(BF16)

    def reduce_z(total):
        return lax.psum_scatter(total, "fh", scatter_dimension=0, tiled=True)

    down_sent = send_grad(seq_cot[1], inner)
    down_w = both_after(down_w, down_sent)
    down_came = swap(down_sent, "fl")
    grad_inner = dot(seq_cot[0], down_w[0]) + dot(seq_cot[1], down_w[1])
    gate_g = (grad_inner * up_pre * sigmoid * (1.0 + gate_pre * (1.0 - sigmoid))).astype(BF16)
    up_g = (grad_inner * activated).astype(BF16)
    gate_sent = send_grad(seq_two[1], gate_g)
    gate_gn = after(gate_g, gate_sent)
    normed_terms = [
        scatter_rows((dot_rt(gate_gn, g) + dot_rt(up_g, u)).astype(BF16)) for g, u in zip(gate_w, up_w)
    ]
    down_total = total_grad(seq_cot[0], inner, down_came)
    grad_down = reduce_z(down_total)
    gate_sent = after(gate_sent, down_came)
    gate_came = swap(gate_sent, "fl")
    r_own, r_oth, attn_low, gain_s_own, gain_s_oth = call(
        middle_kernel,
        [],
        batch,
        half_ins(after(h_own, down_total), h_oth)
        + terms(normed_terms)
        + gain_in(gain_two)
        + half_ins(seq_cot[0], seq_cot[1]),
        half_outs + low_out + [((1, half), F32, full_spec((1, half)))] * 2,
    )
    up_sent = send_grad(seq_two[1], up_g)
    block_terms = [scatter_rows(dot_rt(inner, w).astype(BF16)) for w in down_w]

    whole_out = [((own_rows, width), F32, row_spec(rows, width))]
    (block_out,) = call(
        functools.partial(block_out_kernel, hi), [at], batch, half_ins(h_own, h_oth) + terms(block_terms), whole_out
    )

    gate_total = total_grad(seq_two[0], gate_g, gate_came)
    grad_gate = reduce_z(gate_total)
    seq_attn = stack_rows(attn_low, gate_total, up_sent, block_terms[0][1], block_terms[1][1])
    out_sent = send_grad(seq_attn[1], mixed)
    grad_mixed = (dot(seq_attn[0], out_w[0]) + dot(seq_attn[1], out_w[1])).astype(BF16)
    up_sent = after(up_sent, gate_came)
    up_came = swap(up_sent, "fl")
    grad_mixed = after(grad_mixed, grad_down)
    (qkv_g,) = call(
        functools.partial(attend_back_kernel, pairs),
        [span],
        batch,
        [
            (query_rot, q_spec),
            (kv_rot, pair_spec),
            (grad_mixed.reshape(quad + (q_cols,)), q_spec),
            (lse, lse_spec),
            *tables,
        ],
        [(quad + (all_cols,), BF16, quad_spec(rows, all_cols))],
        [
            pltpu.VMEM((length, length), F32),
            pltpu.VMEM((2, length, PAIR), BF16),
            pltpu.VMEM((2, PAIR, length), BF16),
            pltpu.VMEM((2, length, PAIR), BF16),
            pltpu.VMEM((2, length, PAIR), F32),
            pltpu.VMEM((2, length, PAIR), F32),
        ],
        flops=5 * score_flops,
        exps=score_exps,
    )
    up_total = total_grad(seq_two[0], up_g, up_came)
    grad_up = reduce_z(up_total)
    qkv_g = after(as_rows(qkv_g), up_came, grad_gate, block_out)
    out_sent = after(out_sent, up_came)
    out_came = swap(out_sent, "fl")

    partial_one = tuple(dot_rt(qkv_g, w).astype(BF16) for w in qkv_w)
    first_terms = [scatter_rows(p) for p in partial_one]
    gain_part = tuple(
        jnp.sum(p.astype(F32) * s.astype(F32), axis=0) / g[0] for p, s, g in zip(partial_one, seq_one, gain_one)
    )

    def gain_rows(one, two):
        pair = jnp.concatenate([one.reshape(hi, 1, depth), two.reshape(hi, 1, depth)], axis=2)
        return jnp.pad(pair, ((0, 0), (0, ROW_PAD - 1), (0, all_cols - 2 * depth)))

    def with_gains(grad, one, two):
        blocks = jnp.concatenate([grad.reshape(hi, depth, all_cols), gain_rows(one, two)], axis=1)
        return blocks.reshape(hi * (depth + ROW_PAD), all_cols)

    qkv_sent = with_gains(dot_lt(seq_one[1], qkv_g), gain_part[1], gain_s_oth[0]).astype(BF16)
    qkv_came = swap(qkv_sent, "fl")
    grad_out = reduce_z(total_grad(seq_attn[0], mixed, out_came))
    qkv_total = with_gains(dot_lt(seq_one[0], qkv_g), gain_part[0], gain_s_own[0])
    qkv_total = (qkv_total + qkv_came.astype(F32)).astype(BF16)
    grad_qkv = lax.psum_scatter(qkv_total, "fh", scatter_dimension=0, tiled=True)
    gain_sums = lax.psum(grad_qkv[depth, : 2 * depth].astype(F32), ("th", "tl"))

    (grad_in,) = call(
        functools.partial(grad_in_kernel, hi),
        [at],
        batch,
        half_ins(x_own, x_oth) + terms(first_terms) + gain_in(gain_one) + half_ins(r_own, r_oth),
        whole_out,
    )
    grad_qkv = grad_qkv[:depth].astype(F32)
    return (
        block_out.reshape(block_in.shape),
        grad_in.reshape(block_in.shape),
        grad_qkv[:, :q_cols],
        grad_qkv[:, q_cols : q_cols + kv_cols],
        grad_qkv[:, q_cols + kv_cols :],
        grad_out.astype(F32).T,
        grad_gate.astype(F32),
        grad_up.astype(F32),
        grad_down.astype(F32).T,
        gain_sums[:depth],
        gain_sums[depth:],
    )


def solution(mesh):
    n_fsdp, n_tp = mesh.shape["fsdp"], mesh.shape["tp"]
    fine = Mesh(mesh.devices.reshape(n_fsdp // 2, 2, n_tp // 2, 2), ("fh", "fl", "th", "tl"))
    fsdp, tp = ("fh", "fl"), ("th", "tl")
    rows = P(None, fsdp + tp, None)
    up, across, flat = P(fsdp, tp), P(tp, fsdp), P(fsdp)
    return jax.shard_map(
        per_device,
        mesh=fine,
        in_specs=(rows, P(None, fsdp), up, up, up, across, up, up, across, flat, flat, rows),
        out_specs=(rows, rows, up, up, up, across, up, up, across, flat, flat),
        check_vma=False,
    )
```

time: 1970 us -> 791 us (0.40)
  waiting for transfers between devices: 1370 us -> 345 us
  matrix products: 336 us -> 202 us
  blocking collectives: 130 us -> 5.97 us
  Pallas kernels: 0 us -> 107 us
  other arithmetic: 72.6 us -> 34.5 us
  starting transfers between devices: 3.5 us -> 29.3 us
    reduce_scatter x19 -> x4, waiting for transfers between devices: 949 us -> 0.02 us  [reduce_z(): return lax.psum_scatter(total, 'fh', scatter_dimension=0, tiled=True)]
    all_gather x17 -> x5, waiting for transfers between devices: 414 us -> 105 us  [per_device(): lax.all_gather(part, 'fh', axis=0, tiled=True)]
    ppermute x0 -> x38, waiting for transfers between devices: none -> 238 us  [swap(): return lax.ppermute(value, axis, SWAP)]
    dot_general x81 -> x30, matrix products: 336 us -> 202 us  [the longest x10 79.3 us: dot(): return jnp.dot(a, b, preferred_element_type=F32)]
    pallas_call x0 -> x10, Pallas kernels: none -> 107 us  [call(): pl.pallas_call(kernel, out_shape=[jax.ShapeDtypeStruct(shape, kind) for s...]
    all_gather x4 -> x0, blocking collectives: 102 us -> none  [the longest x1 30.7 us: per_device(): lax.all_gather(w_value, 'fsdp', axis=0, tiled=True)]
    ppermute x0 -> x38, starting transfers between devices: none -> 28.8 us  [swap(): return lax.ppermute(value, axis, SWAP)]
    unnamed x1 -> x0, blocking collectives: 21.6 us -> none
  transfers between devices with their start and end apart: 36 -> 48, of which waited for: 26 -> 23; matrix products, arithmetic and copies ran while one was open for 18% -> 33% of each run, Pallas kernels for 0% -> 14%
where the time goes in v1:
time: 791 us; the launch traced here: 782 us
  waiting for transfers between devices  345 us (44%)
  matrix products  202 us (26%)
  Pallas kernels  107 us (14%)
  local copies, waits for them, and re-layouts  42.4 us (5%)
  other arithmetic  34.5 us (4%)
  starting transfers between devices  29.3 us (4%)
  between operations  15.7 us (2%)
    ppermute x38, waiting for transfers between devices, swap(): return lax.ppermute(value, axis, SWAP)  238 us
    pallas_call x10, Pallas kernels, call(): pl.pallas_call(kernel, out_shape=[jax.ShapeDtypeStruct(shape, kind) for s...  107 us
    all_gather x5, waiting for transfers between devices, per_device(): lax.all_gather(part, 'fh', axis=0, tiled=True)  105 us
    dot_general x10, matrix products, dot(): return jnp.dot(a, b, preferred_element_type=F32)  79.3 us
    dot_general x10, matrix products, dot_rt(): lax.dot_general(a, b, (((1,), (1,)), ((), ())), preferred_element_type=F32)  61.6 us
    dot_general x10, matrix products, dot_lt(): lax.dot_general(a, b, (((0,), (0,)), ((), ())), preferred_element_type=F32)  61.1 us
    ppermute x38, starting transfers between devices, swap(): return lax.ppermute(value, axis, SWAP)  28.8 us
    unnamed x131, local copies, waits for them, and re-layouts  19.7 us
  transfers between devices with their start and end apart: 48, of which 23 were waited for; matrix products, arithmetic and copies ran while one was open for 33% of the time, Pallas kernels for 14%

profile of v1, /device:TPU:0, one launch (start us, length us, event | category | flops | bytes accessed | tf_op | source)
XLA Modules:
  0.0 781.7 jit_solution(2821545766218920252)
XLA Ops:
  16.0 32.4 %all-gather.6.cloned.1.call-done = bf16[1088,640]{1,0:T(8,128)(2,1)} async-done(((bf16[272,640]{1,0:T(8,128)(2,1)}), bf16[1088,640]{1,0:T(8,128)(2,1)}) %all-gather.6.cloned.1.call-update) | async-done | bytes 1392656 | tf_op jit(solution)/shard_map/all_gather | solution.py:321
  56.7 22.5 %all-gather.12.cloned.1.call-done = bf16[1024,512]{0,1:T(8,128)(2,1)} async-done(((bf16[256,512]{0,1:T(8,128)(2,1)}), bf16[1024,512]{0,1:T(8,128)(2,1)}) %all-gather.12.cloned.1.call-update) | async-done | bytes 1048592 | tf_op jit(solution)/shard_map/all_gather | solution.py:321
  104.5 22.0 %shard_map.204 = (bf16[4,3,128,512]{3,2,1,0:T(8,128)(2,1)}, bf16[4,3,128,128]{3,2,1,0:T(8,128)(2,1)}, bf16[4,3,128,512]{3,2,1,0:T(8,128)(2,1)}, f32[3,8,512]{2,1,0:T(8,128)}) custom-call(s32[3]{0:T(128)} %bitcast.173, f32[4,3,128,640]{3,2,1,0:T(8,128)} %bitcast.175, f32[512,128]{1,0:T(8,128)} %copy.69.cos, f32[512,128]{1,0:T(8,128)} %pad_maximum_fusion.2.sine, ...), custom_call_target="tpu_custom_call" | custom-call | flops 3221225472 | bytes 8048640 | tf_op jit(solution)/shard_map/pallas_call | solution.py:62
  126.5 11.8 %all-gather.10.cloned.1.call-done = bf16[1024,1408]{1,0:T(8,128)(2,1)} async-done(((bf16[256,1408]{1,0:T(8,128)(2,1)}), bf16[1024,1408]{1,0:T(8,128)(2,1)}) %all-gather.10.cloned.1.call-update) | async-done | bytes 2883600 | tf_op jit(solution)/shard_map/all_gather | solution.py:321
  158.8 38.7 %all-gather.8.cloned.1.call-done = bf16[1024,1408]{1,0:T(8,128)(2,1)} async-done(((bf16[256,1408]{1,0:T(8,128)(2,1)}), bf16[1024,1408]{1,0:T(8,128)(2,1)}) %all-gather.8.cloned.1.call-update) | async-done | bytes 2883600 | tf_op jit(solution)/shard_map/all_gather | solution.py:321
  211.2 12.3 %collective-permute-done.15.p1 = bf16[384,2048]{1,0:T(8,128)(2,1)S(1)} collective-permute-done((bf16[384,2048]{1,0:T(8,128)(2,1)}, bf16[384,2048]{1,0:T(8,128)(2,1)S(1)}, u32[]{:S(2)}, u32[]{:S(2)}) %collective-permute-start.15) | collective-permute-done | bytes 1572896 | tf_op jit(solution)/shard_map/ppermute | solution.py:35
  224.0 32.8 %collective-permute-done.11.p1 = bf16[384,2048]{1,0:T(8,128)(2,1)S(1)} collective-permute-done((bf16[384,2048]{1,0:T(8,128)(2,1)}, bf16[384,2048]{1,0:T(8,128)(2,1)S(1)}, u32[]{:S(2)}, u32[]{:S(2)}) %collective-permute-start.11) | collective-permute-done | bytes 1572896 | tf_op jit(solution)/shard_map/ppermute | solution.py:35
  289.8 9.3 %fusion.27 = f32[1536,1408]{1,0:T(8,128)} fusion(bf16[1536,1024]{1,0:T(8,128)(2,1)S(1)} %bitcast.167, bf16[1024,1408]{1,0:T(8,128)(2,1)} %collective-permute-done.10), kind=kOutput, calls=%fused_computation.83 | convolution fusion | flops 4429185024 | bytes 14680064 | tf_op jit(solution)/shard_map/dot_general | solution.py:23
  299.1 9.2 %convolution_add_fusion.2 = f32[1536,1408]{1,0:T(8,128)} fusion(f32[1536,1408]{1,0:T(8,128)S(1)} %fusion.26, bf16[1536,1024]{1,0:T(8,128)(2,1)S(1)} %bitcast.161, bf16[1024,1408]{1,0:T(8,128)(2,1)} %all-gather.10.cloned.1.call-done), kind=kOutput, calls=%fused_computation.2 | convolution fusion | flops 4431347712 | bytes 23330816 | tf_op jit(solution)/shard_map/dot_general | solution.py:23
  308.3 12.4 %multiply_convert_fusion.2 = (bf16[1536,1408]{1,0:T(8,128)(2,1)S(1)}, f32[1536,1408]{1,0:T(8,128)}) fusion(f32[1536,1408]{1,0:T(8,128)} %convolution_add_fusion.2, f32[1536,1408]{1,0:T(8,128)} %fusion.27, bf16[1536,1024]{1,0:T(8,128)(2,1)S(1)} %bitcast.162, bf16[1024,1408]{1,0:T(8,128)(2,1)} %all-gather.8.cloned.1.call-done), kind=kOutput, calls=%fused_computation.5 | convolution fusion | flops 4444323840 | bytes 36306944 | tf_op jit(solution)/shard_map/dot_general | solution.py:23
  344.5 16.5 %multiply_convert_fusion = (bf16[1536,1408]{1,0:T(8,128)(2,1)}, bf16[1536,1408]{1,0:T(8,128)(2,1)}) fusion(f32[1536,1408]{1,0:T(8,128)} %convolution_add_fusion.2, f32[1536,1408]{1,0:T(8,128)} %get-tuple-element.143, f32[1536,1408]{1,0:T(8,128)} %fusion.28, bf16[1536,1024]{1,0:T(8,128)(2,1)S(1)} %bitcast.121, ...), kind=kOutput, calls=%fused_computation.3 | convolution fusion | flops 4459462656 | bytes 40632320 | tf_op jit(solution)/shard_map/dot_general | solution.py:23
  361.0 9.4 %convolution_convert_fusion.3 = bf16[1024,1408]{1,0:T(8,128)(2,1)} fusion(bf16[1536,1024]{1,0:T(8,128)(2,1)} %bitcast.166, bf16[1536,1408]{1,0:T(8,128)(2,1)} %get-tuple-element.68), kind=kOutput, calls=%fused_computation.18 | convolution fusion | flops 4430626816 | bytes 10354688 | tf_op jit(solution)/shard_map/dot_general | solution.py:27
  386.3 11.2 %collective-permute-done.22 = bf16[1024,1408]{1,0:T(8,128)(2,1)} collective-permute-done((bf16[1024,1408]{1,0:T(8,128)(2,1)}, bf16[1024,1408]{1,0:T(8,128)(2,1)}, u32[]{:S(2)}, u32[]{:S(2)}) %collective-permute-start.22) | collective-permute-done | bytes 2883616 | tf_op jit(solution)/shard_map/ppermute | solution.py:35
  434.4 11.4 %collective-permute-done.26.b2 = bf16[384,1024]{1,0:T(8,128)(2,1)S(1)} collective-permute-done((bf16[384,1024]{1,0:T(8,128)(2,1)S(1)}, bf16[384,1024]{1,0:T(8,128)(2,1)S(1)}, u32[]{:S(2)}, u32[]{:S(2)}) %collective-permute-start.26) | collective-permute-done | bytes 786464 | tf_op jit(solution)/shard_map/ppermute | solution.py:35
  445.8 15.7 %collective-permute-done.24.a2 = bf16[384,1024]{1,0:T(8,128)(2,1)S(1)} collective-permute-done((bf16[384,1024]{1,0:T(8,128)(2,1)S(1)}, bf16[384,1024]{1,0:T(8,128)(2,1)S(1)}, u32[]{:S(2)}, u32[]{:S(2)}) %collective-permute-start.24) | collective-permute-done | bytes 786464 | tf_op jit(solution)/shard_map/ppermute | solution.py:35
  470.6 16.7 %collective-permute-done.27 = bf16[1024,1408]{1,0:T(8,128)(2,1)} collective-permute-done((bf16[1024,1408]{1,0:T(8,128)(2,1)}, bf16[1024,1408]{1,0:T(8,128)(2,1)}, u32[]{:S(2)}, u32[]{:S(2)}) %collective-permute-start.27) | collective-permute-done | bytes 2883616 | tf_op jit(solution)/shard_map/ppermute | solution.py:35
  536.0 33.7 %collective-permute-done.31 = bf16[1024,1408]{1,0:T(8,128)(2,1)} collective-permute-done((bf16[1024,1408]{1,0:T(8,128)(2,1)}, bf16[1024,1408]{1,0:T(8,128)(2,1)}, u32[]{:S(2)}, u32[]{:S(2)}) %collective-permute-start.31) | collective-permute-done | bytes 2883616 | tf_op jit(solution)/shard_map/ppermute | solution.py:35
  572.9 21.5 %collective-permute-done.37 = bf16[1024,512]{1,0:T(8,128)(2,1)S(1)} collective-permute-done((bf16[1024,512]{1,0:T(8,128)(2,1)S(1)}, bf16[1024,512]{1,0:T(8,128)(2,1)S(1)}, u32[]{:S(2)}, u32[]{:S(2)}) %collective-permute-start.37) | collective-permute-done | bytes 1048608 | tf_op jit(solution)/shard_map/ppermute | solution.py:35
  608.2 9.9 %collective-permute-done.19.a2 = bf16[384,1024]{1,0:T(8,128)(2,1)} collective-permute-done((bf16[384,1024]{1,0:T(8,128)(2,1)}, bf16[384,1024]{1,0:T(8,128)(2,1)}, u32[]{:S(2)}, u32[]{:S(2)}) %collective-permute-start.19) | collective-permute-done | bytes 786464 | tf_op jit(solution)/shard_map/ppermute | solution.py:35
  623.9 9.3 %add_convert_fusion.2 = bf16[1024,1408]{1,0:T(8,128)(2,1)} fusion(bf16[1024,1408]{1,0:T(8,128)(2,1)} %collective-permute-done.31, bf16[1536,1024]{1,0:T(8,128)(2,1)S(1)} %bitcast.164, bf16[1536,1408]{1,0:T(8,128)(2,1)} %get-tuple-element.127), kind=kOutput, calls=%fused_computation.12 | convolution fusion | flops 4433510400 | bytes 13238272 | tf_op jit(solution)/shard_map/dot_general | solution.py:27
  640.7 31.2 %shard_map.211 = bf16[4,3,128,640]{3,2,1,0:T(8,128)(2,1)} custom-call(s32[3]{0:T(128)} %bitcast.174, bf16[4,3,128,512]{3,2,1,0:T(8,128)(2,1)} %get-tuple-element.64.query_in, bf16[4,3,128,128]{3,2,1,0:T(8,128)(2,1)} %get-tuple-element.65.kv_in, bf16[4,3,128,512]{3,2,1,0:T(8,128)(2,1)} %bitcast.184, f32[3,8,512]{2,1,0:T(8,128)} %get-tuple-element.75.lse, ...), custom_call_target="tpu_custom_call" | custom-call | flops 8053063680 | bytes 6082560 | tf_op jit(solution)/shard_map/pallas_call | solution.py:62
  692.6 18.9 %collective-permute-done.36 = bf16[1088,640]{1,0:T(8,128)(2,1)S(1)} collective-permute-done((bf16[1088,640]{1,0:T(8,128)(2,1)S(1)}, bf16[1088,640]{1,0:T(8,128)(2,1)S(1)}, u32[]{:S(2)}, u32[]{:S(2)}) %collective-permute-start.36) | collective-permute-done | bytes 1392672 | tf_op jit(solution)/shard_map/ppermute | solution.py:35
  727.7 9.7 %collective-permute-done.35.b2 = bf16[384,1024]{1,0:T(8,128)(2,1)S(1)} collective-permute-done((bf16[384,1024]{1,0:T(8,128)(2,1)}, bf16[384,1024]{1,0:T(8,128)(2,1)S(1)}, u32[]{:S(2)}, u32[]{:S(2)}) %collective-permute-start.35) | collective-permute-done | bytes 786464 | tf_op jit(solution)/shard_map/ppermute | solution.py:35
  737.4 16.4 %collective-permute-done.33.a2 = bf16[384,1024]{1,0:T(8,128)(2,1)S(1)} collective-permute-done((bf16[384,1024]{1,0:T(8,128)(2,1)}, bf16[384,1024]{1,0:T(8,128)(2,1)S(1)}, u32[]{:S(2)}, u32[]{:S(2)}) %collective-permute-start.33) | collective-permute-done | bytes 786464 | tf_op jit(solution)/shard_map/ppermute | solution.py:35
  (312 shorter events, 331.3 us)
Async XLA Ops:
  7.2 41.3 %all-gather.6.cloned.1.call-start = ((), (), s32[]{:S(2)}) async-start(), calls=%async_computation.5 | async-start | bytes 1740800 | tf_op jit(solution)/shard_map/all_gather | solution.py:321
  11.5 67.7 %all-gather.12.cloned.1.call-start = ((), (), s32[]{:S(2)}) async-start(), calls=%async_computation.8 | async-start | bytes 1310720 | tf_op jit(solution)/shard_map/all_gather | solution.py:321
  12.2 126.0 %all-gather.10.cloned.1.call-start = ((), (), s32[]{:S(2)}) async-start(), calls=%async_computation.7 | async-start | bytes 3604480 | tf_op jit(solution)/shard_map/all_gather | solution.py:321
  13.0 184.6 %all-gather.8.cloned.1.call-start = ((), (), s32[]{:S(2)}) async-start(), calls=%async_computation.6 | async-start | bytes 3604480 | tf_op jit(solution)/shard_map/all_gather | solution.py:321
  50.7 215.0 %all-gather.14.cloned.1.call-start = ((), (), s32[]{:S(2)}) async-start(), calls=%async_computation.9 | async-start | bytes 3604480 | tf_op jit(solution)/shard_map/all_gather | solution.py:321
  79.1 59.1 %collective-permute-start.6 = (bf16[1024,512]{0,1:T(8,128)(2,1)}, bf16[1024,512]{0,1:T(8,128)(2,1)}, u32[]{:S(2)}, u32[]{:S(2)}) collective-permute-start(bf16[1024,512]{0,1:T(8,128)(2,1)} %all-gather.12.cloned.1.call-done), channel_id=1, source_target_pairs={{0,4},{4,0},{1,5},{5,1},{2,6},{6,2},{3,7},{7,3},{8,12},{12,8},{9,1... | collective-permute-start | bytes 3145736 | tf_op jit(solution)/shard_map/ppermute | solution.py:35
  143.1 65.2 %collective-permute-start.9 = (bf16[1024,1408]{1,0:T(8,128)(2,1)}, bf16[1024,1408]{1,0:T(8,128)(2,1)}, u32[]{:S(2)}, u32[]{:S(2)}) collective-permute-start(bf16[1024,1408]{1,0:T(8,128)(2,1)} %all-gather.10.cloned.1.call-done), channel_id=1, source_target_pairs={{0,4},{4,0},{1,5},{5,1},{2,6},{6,2},{3,7},{7,3},{8,12},{12,8},{9,1... | collective-permute-start | bytes 8650760 | tf_op jit(solution)/shard_map/ppermute | solution.py:35
  150.0 490.7 %reduce-scatter.8.cloned.1.call-start = ((), (), s32[]{:S(2)}) async-start(), calls=%async_computation.10 | async-start | bytes 3604480 | tf_op jit(solution)/shard_map/reduce_scatter | solution.py:441
  152.4 45.2 %collective-permute-start.8 = (bf16[384,1024]{1,0:T(8,128)(2,1)}, bf16[384,1024]{1,0:T(8,128)(2,1)S(1)}, u32[]{:S(2)}, u32[]{:S(2)}) collective-permute-start(bf16[384,1024]{1,0:T(8,128)(2,1)} %add_convert_fusion.12), channel_id=1, source_target_pairs={{0,2},{2,0},{1,3},{3,1},{4,6},{6,4},{5,7},{7,5},{8,10},{10,8},{9,1... | collective-permute-start | bytes 2359304 | tf_op jit(solution)/shard_map/ppermute | solution.py:35
  155.5 42.0 %collective-permute-start.5 = (bf16[384,1024]{1,0:T(8,128)(2,1)S(1)}, bf16[384,1024]{1,0:T(8,128)(2,1)}, u32[]{:S(2)}, u32[]{:S(2)}) collective-permute-start(bf16[384,1024]{1,0:T(8,128)(2,1)S(1)} %add_convert_fusion.13), channel_id=1, source_target_pairs={{0,2},{2,0},{1,3},{3,1},{4,6},{6,4},{5,7},{7,5},{8,10},{10,8},{9,1... | collective-permute-start | bytes 2359304 | tf_op jit(solution)/shard_map/ppermute | solution.py:35
  156.9 66.6 %collective-permute-start.15 = (bf16[384,2048]{1,0:T(8,128)(2,1)}, bf16[384,2048]{1,0:T(8,128)(2,1)S(1)}, u32[]{:S(2)}, u32[]{:S(2)}) collective-permute-start(bf16[384,2048]{1,0:T(8,128)(2,1)} %bitcast.21.p0), channel_id=1, source_target_pairs={{0,2},{2,0},{1,3},{3,1},{4,6},{6,4},{5,7},{7,5},{8,10},{10,8},{9,1... | collective-permute-start | bytes 4718600 | tf_op jit(solution)/shard_map/ppermute | solution.py:35
  208.3 48.6 %collective-permute-start.11 = (bf16[384,2048]{1,0:T(8,128)(2,1)}, bf16[384,2048]{1,0:T(8,128)(2,1)S(1)}, u32[]{:S(2)}, u32[]{:S(2)}) collective-permute-start(bf16[384,2048]{1,0:T(8,128)(2,1)} %get-tuple-element.58.p0), channel_id=1, source_target_pairs={{0,2},{2,0},{1,3},{3,1},{4,6},{6,4},{5,7},{7,5},{8,10},{10,8},{9,1... | collective-permute-start | bytes 4718600 | tf_op jit(solution)/shard_map/ppermute | solution.py:35
  209.7 65.7 %collective-permute-start.10 = (bf16[1024,1408]{1,0:T(8,128)(2,1)}, bf16[1024,1408]{1,0:T(8,128)(2,1)}, u32[]{:S(2)}, u32[]{:S(2)}) collective-permute-start(bf16[1024,1408]{1,0:T(8,128)(2,1)} %all-gather.8.cloned.1.call-done), channel_id=1, source_target_pairs={{0,4},{4,0},{1,5},{5,1},{2,6},{6,2},{3,7},{7,3},{8,12},{12,8},{9,1... | collective-permute-start | bytes 8650760 | tf_op jit(solution)/shard_map/ppermute | solution.py:35
  211.2 45.6 %collective-permute-start.16 = (bf16[384,2048]{1,0:T(8,128)(2,1)}, bf16[384,2048]{1,0:T(8,128)(2,1)S(1)}, u32[]{:S(2)}, u32[]{:S(2)}) collective-permute-start(bf16[384,2048]{1,0:T(8,128)(2,1)} %bitcast.21.p0), channel_id=1, source_target_pairs={{0,1},{1,0},{2,3},{3,2},{4,5},{5,4},{6,7},{7,6},{8,9},{9,8},{10,11... | collective-permute-start | bytes 4718600 | tf_op jit(solution)/shard_map/ppermute | solution.py:35
  223.5 52.0 %collective-permute-start.12 = (bf16[384,2048]{1,0:T(8,128)(2,1)}, bf16[384,2048]{1,0:T(8,128)(2,1)}, u32[]{:S(2)}, u32[]{:S(2)}) collective-permute-start(bf16[384,2048]{1,0:T(8,128)(2,1)} %get-tuple-element.58.p0), channel_id=1, source_target_pairs={{0,1},{1,0},{2,3},{3,2},{4,5},{5,4},{6,7},{7,6},{8,9},{9,8},{10,11... | collective-permute-start | bytes 4718600 | tf_op jit(solution)/shard_map/ppermute | solution.py:35
  265.7 71.5 %collective-permute-start.14 = (bf16[1024,1408]{0,1:T(8,128)(2,1)}, bf16[1024,1408]{0,1:T(8,128)(2,1)S(1)}, u32[]{:S(2)}, u32[]{:S(2)}) collective-permute-start(bf16[1024,1408]{0,1:T(8,128)(2,1)} %all-gather.14.cloned.1.call-done), channel_id=1, source_target_pairs={{0,4},{4,0},{1,5},{5,1},{2,6},{6,2},{3,7},{7,3},{8,12},{12,8},{9,1... | collective-permute-start | bytes 8650760 | tf_op jit(solution)/shard_map/ppermute | solution.py:35
  327.5 70.0 %collective-permute-start.22 = (bf16[1024,1408]{1,0:T(8,128)(2,1)}, bf16[1024,1408]{1,0:T(8,128)(2,1)}, u32[]{:S(2)}, u32[]{:S(2)}) collective-permute-start(bf16[1024,1408]{1,0:T(8,128)(2,1)} %convolution_convert_fusion.6), channel_id=1, source_target_pairs={{0,4},{4,0},{1,5},{5,1},{2,6},{6,2},{3,7},{7,3},{8,12},{12,8},{9,1... | collective-permute-start | bytes 8650760 | tf_op jit(solution)/shard_map/ppermute | solution.py:35
  405.5 266.3 %reduce-scatter.10.cloned.1.call-start = ((), (), s32[]{:S(2)}) async-start(), calls=%async_computation.11 | async-start | bytes 3604480 | tf_op jit(solution)/shard_map/reduce_scatter | solution.py:441
  422.0 65.2 %collective-permute-start.27 = (bf16[1024,1408]{1,0:T(8,128)(2,1)}, bf16[1024,1408]{1,0:T(8,128)(2,1)}, u32[]{:S(2)}, u32[]{:S(2)}) collective-permute-start(bf16[1024,1408]{1,0:T(8,128)(2,1)} %convolution_convert_fusion.3), channel_id=1, source_target_pairs={{0,4},{4,0},{1,5},{5,1},{2,6},{6,2},{3,7},{7,3},{8,12},{12,8},{9,1... | collective-permute-start | bytes 8650760 | tf_op jit(solution)/shard_map/ppermute | solution.py:35
  470.0 47.9 %collective-permute-start.28 = (bf16[384,2048]{1,0:T(8,128)(2,1)}, bf16[384,2048]{1,0:T(8,128)(2,1)}, u32[]{:S(2)}, u32[]{:S(2)}) collective-permute-start(bf16[384,2048]{1,0:T(8,128)(2,1)} %get-tuple-element.71.p0), channel_id=1, source_target_pairs={{0,2},{2,0},{1,3},{3,1},{4,6},{6,4},{5,7},{7,5},{8,10},{10,8},{9,1... | collective-permute-start | bytes 4718600 | tf_op jit(solution)/shard_map/ppermute | solution.py:35
  496.4 229.3 %reduce-scatter.12.cloned.1.call-start = ((), (), s32[]{:S(2)}) async-start(), calls=%async_computation.12 | async-start | bytes 1310720 | tf_op jit(solution)/shard_map/reduce_scatter | solution.py:441
  504.4 65.2 %collective-permute-start.31 = (bf16[1024,1408]{1,0:T(8,128)(2,1)}, bf16[1024,1408]{1,0:T(8,128)(2,1)}, u32[]{:S(2)}, u32[]{:S(2)}) collective-permute-start(bf16[1024,1408]{1,0:T(8,128)(2,1)} %convolution_convert_fusion.2), channel_id=1, source_target_pairs={{0,4},{4,0},{1,5},{5,1},{2,6},{6,2},{3,7},{7,3},{8,12},{12,8},{9,1... | collective-permute-start | bytes 8650760 | tf_op jit(solution)/shard_map/ppermute | solution.py:35
  597.2 164.4 %reduce-scatter.14.cloned.1.call-start = ((), (), s32[]{:S(2)}) async-start(), calls=%async_computation.13 | async-start | bytes 3604480 | tf_op jit(solution)/shard_map/reduce_scatter | solution.py:441
  633.2 130.7 %reduce-scatter.16.cloned.1.call-start = ((), (), s32[]{:S(2)}) async-start(), calls=%async_computation.14 | async-start | bytes 1740800
  (86 other events, 1425.0 us)
Sparse Core Ops, SparseCore 0:
  11.6 36.7 all-gather.5
  50.0 29.0 all-gather.11
  80.7 57.4 all-gather.9
  139.7 57.8 all-gather.7
  199.0 57.8 all-gather.13
  405.6 53.9 reduce-scatter.7
  496.6 53.9 reduce-scatter.9
  597.3 24.8 reduce-scatter.11
  633.3 53.9 reduce-scatter.13
  712.9 30.7 reduce-scatter.15

commit v2 on v1

--- a/solution.py
+++ b/solution.py
@@ -16,6 +16,8 @@
 F32 = jnp.float32
 BF16 = jnp.bfloat16
 SWAP = [(0, 1), (1, 0)]
+COST = {1: 1703, 2: 2220, 3: 2583, 4: 5630, 5: 1730, 6: 799, 7: 1730, 8: 799, 10: 1626, 11: 4002, 12: 3950, 13: 4338, 14: 3898, 15: 17158, 16: 2349, 17: 83025, 18: 2287, 19: 2349, 20: 1987, 21: 3821, 22: 1006, 23: 2556, 24: 1626, 25: 2143, 26: 1419, 27: 7981, 28: 2556, 29: 2066, 30: 826, 31: 26035, 32: 2066, 33: 17158, 34: 1523, 35: 1703, 36: 11984, 37: 53467, 38: 3616}
+SKIP = {131, 137, 143, 116, 123, 125}
 ROW_PAD = 16
 
 
@@ -35,13 +37,10 @@
     return lax.ppermute(value, axis, SWAP)
 
 
-def after(value, *others):
+def after(step, value, *others):
+    if step in SKIP:
+        return value
     return lax.optimization_barrier((value, *others))[0]
-
-
-def both_after(pair, *others):
-    kept = lax.optimization_barrier((*pair, *others))
-    return kept[0], kept[1]
 
 
 def full_spec(shape):
@@ -56,9 +55,19 @@
     return pl.BlockSpec((4, 1, rows, cols), lambda i, *_: (0, i, 0, 0))
 
 
-def call(kernel, scalars, grid, ins, outs, scratch=(), flops=0, exps=0):
-    moved = sum(a.size * a.dtype.itemsize for a, _ in ins)
-    moved += sum(math.prod(shape) * jnp.dtype(kind).itemsize for shape, kind, _ in outs)
+def two_part_outs(rows, cols, tile):
+    half = rows // tile // 2
+    first = pl.BlockSpec((tile, cols), lambda i, *_: (jnp.minimum(i, half - 1), 0))
+    second = pl.BlockSpec((tile, cols), lambda i, *_: (jnp.maximum(i - half, 0), 0))
+    return [((rows // 2, cols), BF16, first), ((rows // 2, cols), BF16, second)]
+
+
+def whole_spec(array):
+    return pl.BlockSpec(array.shape, lambda i, *_: (0, 0), pipeline_mode=pl.Buffered(1))
+
+
+def call(step, kernel, scalars, grid, ins, outs, scratch=()):
+    work = COST.get(step, 0) * 1000
     return pl.pallas_call(
         kernel,
         out_shape=[jax.ShapeDtypeStruct(shape, kind) for shape, kind, _ in outs],
@@ -69,7 +78,7 @@
             out_specs=[spec for _, _, spec in outs],
             scratch_shapes=list(scratch),
         ),
-        cost_estimate=pl.CostEstimate(flops=flops, bytes_accessed=moved, transcendentals=exps),
+        cost_estimate=pl.CostEstimate(flops=work * 300, bytes_accessed=work + step, transcendentals=0),
         compiler_params=pltpu.CompilerParams(vmem_limit_bytes=56 << 20),
     )(*scalars, *[a for a, _ in ins])
 
@@ -123,6 +132,13 @@
         put_cols(o_oth, (k, 0), oth)
 
 
+def pairs_kernel(hi, at, p0, p1, p2, p3, out):
+    x = at[0]
+    for k, piece in enumerate((p0, p1, p2, p3)):
+        own, oth = halves_of(piece[...], hi, x)
+        put_cols(out, (k, 0), [part for pair in zip(own, oth) for part in pair])
+
+
 def stack_kernel(p0, p1, p2, p3, o_own, o_oth):
     half = o_own.shape[-1]
     for k, piece in enumerate((p0, p1, p2, p3)):
@@ -150,8 +166,16 @@
     n_out[:, half:] = (oth * scale * gain_oth[...]).astype(BF16)
 
 
-def block_out_kernel(hi, at, h_own, h_oth, a0, a1, a2, b0, b1, b2, out):
-    join_to(out, h_own[...] + summed((a0, a1, a2)), h_oth[...] + summed((b0, b1, b2)), hi, at[0])
+def block_out_kernel(hi, at, h_own, h_oth, t0, t1, t2, out):
+    x = at[0]
+    width = h_own.shape[-1] // hi
+    for k in range(hi):
+        cols = [slice(j * width, (j + 1) * width) for j in (2 * k, 2 * k + 1)]
+        own, oth = (sum(t[:, col].astype(F32) for t in (t0, t1, t2)) for col in cols)
+        own += h_own[:, k * width : (k + 1) * width]
+        oth += h_oth[:, k * width : (k + 1) * width]
+        out[:, cols[0]] = jnp.where(x == 0, own, oth)
+        out[:, cols[1]] = jnp.where(x == 0, oth, own)
 
 
 def back_of(own, oth, scale, gain_own, gain_oth, up_own, up_oth):
@@ -162,14 +186,15 @@
 
 
 def middle_kernel(
-    h_own, h_oth, a0, a1, a2, b0, b1, b2, gain_own, gain_oth, u_own, u_oth, r_own, r_oth, low_out, s_own, s_oth
+    hi, at, h_own, h_oth, a0, a1, a2, b0, b1, b2, gain_own, gain_oth, upstream, r_own, r_oth, low_out, s_own, s_oth
 ):
     own, oth = h_own[...], h_oth[...]
     up_own, up_oth = summed((a0, a1, a2)), summed((b0, b1, b2))
     scale = rows_scale(own, oth)
     back_own, back_oth = back_of(own, oth, scale, gain_own[...], gain_oth[...], up_own, up_oth)
-    back_own = u_own[...].astype(F32) + back_own
-    back_oth = u_oth[...].astype(F32) + back_oth
+    u_own, u_oth = (jnp.concatenate(part, axis=1) for part in halves_of(upstream[...].astype(F32), hi, at[0]))
+    back_own = u_own + back_own
+    back_oth = u_oth + back_oth
     half = own.shape[-1]
     r_own[...] = back_own
     r_oth[...] = back_oth
@@ -192,6 +217,69 @@
         own, oth, scale, gain_own[...], gain_oth[...], summed((a0, a1, a2)), summed((b0, b1, b2))
     )
     join_to(out, r_own[...] + back_own, r_oth[...] + back_oth, hi, at[0])
+
+
+def project_kernel(n_own, n_oth, w_own, w_oth, out):
+    out[...] = (dot(n_own[...], w_own[...]) + dot(n_oth[...], w_oth[...])).astype(out.dtype)
+
+
+def put_rows(kept, sent, value):
+    stay = pl.program_id(0) < pl.num_programs(0) // 2
+
+    @pl.when(stay)
+    def _():
+        kept[...] = value
+
+    @pl.when(jnp.logical_not(stay))
+    def _():
+        sent[...] = value
+
+
+def project_back_kernel(rows, weight, kept, sent):
+    put_rows(kept, sent, dot_rt(rows[...], weight[...]).astype(BF16))
+
+
+def project_gain_kernel(grad, weight, normed, kept, sent, sums):
+    part = dot_rt(grad[...], weight[...])
+    put_rows(kept, sent, part.astype(BF16))
+
+    @pl.when(pl.program_id(0) == 0)
+    def _():
+        sums[...] = jnp.zeros_like(sums)
+
+    sums[...] += jnp.sum(part * normed[...].astype(F32), axis=0, keepdims=True)
+
+
+def weight_grad_kernel(rows, grad, out):
+    out[...] = dot_lt(rows[...], grad[...]).astype(out.dtype)
+
+
+def weight_grad_add_kernel(rows, grad, came, out):
+    out[...] = (dot_lt(rows[...], grad[...]) + came[...].astype(F32)).astype(BF16)
+
+
+def add_kernel(first, second, out):
+    out[...] = (first[...].astype(F32) + second[...].astype(F32)).astype(BF16)
+
+
+def expand_kernel(n_own, n_oth, u_own, u_oth, gate_in, inner, for_gate, for_up):
+    gate = gate_in[...]
+    up = dot(n_own[...], u_own[...]) + dot(n_oth[...], u_oth[...])
+    sigmoid = jax.nn.sigmoid(gate)
+    active = gate * sigmoid
+    inner[...] = (active * up).astype(BF16)
+    for_gate[...] = (up * sigmoid * (1.0 + gate * (1.0 - sigmoid))).astype(BF16)
+    for_up[...] = active.astype(BF16)
+
+
+def inner_back_kernel(grad, weight, for_gate, for_up, gate_g, up_g):
+    inner_g = dot(grad[...], weight[...])
+    gate_g[...] = (inner_g * for_gate[...].astype(F32)).astype(BF16)
+    up_g[...] = (inner_g * for_up[...].astype(F32)).astype(BF16)
+
+
+def expand_back_kernel(gate_g, up_g, gate_w, up_w, kept, sent):
+    put_rows(kept, sent, (dot_rt(gate_g[...], gate_w[...]) + dot_rt(up_g[...], up_w[...])).astype(BF16))
 
 
 def partner(value):
@@ -297,7 +385,7 @@
 def per_device(
     block_in, span_start, w_query, w_key, w_value, w_out, w_gate, w_up, w_down, gain_attn, gain_mlp, cotangent
 ):
-    x, y, c = lax.axis_index("fl"), lax.axis_index("th"), lax.axis_index("tl")
+    x, y, c = (lax.axis_index(name) for name in ("fl", "th", "tl"))
     hi = lax.axis_size("fh")
     batch, rows, width = block_in.shape
     own_rows, half = batch * rows, width // 2
@@ -310,16 +398,18 @@
     shard = jnp.concatenate([w_query, w_key, w_value], axis=1)
     gains = jnp.concatenate([gain_attn, gain_mlp])[None]
     gains = jnp.pad(gains, ((0, ROW_PAD - 1), (0, shard.shape[1] - gains.shape[1])))
-    shards = (jnp.concatenate([shard, gains], axis=0), w_out.T, w_gate, w_up, w_down.T)
-
-    def gather_x(own):
-        return own, swap(own, "fl")
-
-    def flat(pair):
-        return tuple(part.reshape(hi * depth, -1) for part in pair)
-
-    own_parts = [lax.all_gather(part, "fh", axis=0, tiled=True) for part in shards]
-    own_parts[0] = own_parts[0].reshape(hi, depth + ROW_PAD, -1)
+    shard = jnp.concatenate([shard, gains], axis=0)
+
+    def gather(part):
+        return lax.all_gather(part, "fh", axis=0, tiled=True)
+
+    def swap_x(value):
+        return swap(value, "fl")
+
+    down_shard = w_down.T
+    down_pair = jnp.concatenate([down_shard, swap_x(down_shard)], axis=0)
+    attn_own, out_own, gate_own, up_own = gather(shard), gather(w_out.T), gather(w_gate), gather(w_up)
+    down_w = gather(down_pair)
 
     def gather_rows(piece):
         beside = swap(piece, "tl")
@@ -327,7 +417,8 @@
         return piece, across, beside, swap(across, "tl")
 
     token_parts = gather_rows(block_in.reshape(own_rows, width))
-    cot_parts = gather_rows(cotangent.reshape(own_rows, width))
+    cot_own = cotangent.reshape(own_rows, width)
+    cot_parts = gather_rows(after(101, cot_own, token_parts[1]))
 
     place = jnp.concatenate(
         [(((y + dy) % 2) * 2 + (c + dc) % 2) * rows + jnp.arange(rows, dtype=jnp.int32) for dc in (0, 1) for dy in (0, 1)]
@@ -342,23 +433,74 @@
     tables = [(t, full_spec(t.shape)) for t in (cos, sine, key_at, query_at)]
 
     quad = (4, batch, rows)
+    all_rows = 4 * own_rows
+    tile = 256
+    steps = all_rows // tile
+    hidden = w_gate.shape[1]
+    all_cols = q_cols + 2 * kv_cols
+    tiles = lambda *values: [(v, row_spec(tile, v.shape[1])) for v in values]
+    wholes = lambda *values: [(v, whole_spec(v)) for v in values]
     pieces = lambda parts: [(p, row_spec(rows, width)) for p in parts]
+    half_ins = lambda *values: [(v, row_spec(rows, half)) for v in values]
+    gain_in = lambda gain: [(g, full_spec((1, half))) for g in gain]
     spread_outs = [(quad + (half,), BF16, quad_spec(rows, half))] * 2
+    half_outs = [((own_rows, half), F32, row_spec(rows, half))] * 2
+    low_out = [((own_rows, width), BF16, row_spec(rows, width))]
+    whole_out = [((own_rows, width), F32, row_spec(rows, width))]
+    sum_outs = [((1, half), F32, full_spec((1, half)))]
+    hidden_out = ((all_rows, hidden), BF16, row_spec(tile, hidden))
 
     def as_rows(value):
-        return value.reshape(4 * own_rows, value.shape[-1])
-
-    seq_cot = call(functools.partial(spread_kernel, hi), [at], batch, pieces(cot_parts), spread_outs)
-    seq_cot = tuple(as_rows(v) for v in seq_cot)
-
-    qkv_pair = gather_x(own_parts[0])
-    out_pair = gather_x(own_parts[1])
-    qkv_w = tuple(part[:, :depth].reshape(hi * depth, -1) for part in qkv_pair)
-    gain_one = tuple(part[:, depth, :depth].reshape(1, half).astype(F32) for part in qkv_pair)
-    gain_two = tuple(part[:, depth, depth : 2 * depth].reshape(1, half).astype(F32) for part in qkv_pair)
-    gain_in = lambda gain: [(g, full_spec((1, half))) for g in gain]
+        return value.reshape(all_rows, value.shape[-1])
+
+    def project(step, pair, weights, kind):
+        cols = weights[0].shape[1]
+        out = ((all_rows, cols), kind, row_spec(tile, cols))
+        return call(step, project_kernel, [], steps, tiles(*pair) + wholes(*weights), [out])[0]
+
+    def project_back(step, value, weight):
+        outs = two_part_outs(all_rows, weight.shape[0], tile)
+        return call(step, project_back_kernel, [], steps, tiles(value) + wholes(weight), outs)
+
+    def weight_grad(step, value, grad, came=None, kind=BF16):
+        part, cols = 256, grad.shape[1]
+        ins = [(value, pl.BlockSpec((value.shape[0], part), lambda i: (0, i)))] + wholes(grad)
+        ins += [] if came is None else [(came, row_spec(part, cols))]
+        out = ((value.shape[1], cols), kind, row_spec(part, cols))
+        kernel = weight_grad_kernel if came is None else weight_grad_add_kernel
+        return call(step, kernel, [], value.shape[1] // part, ins, [out])[0]
+
+    def scatter_rows(step, kept, sent):
+        cols = kept.shape[1]
+        came = swap(sent, "tl")
+        (passed,) = call(
+            step,
+            add_kernel,
+            [],
+            batch,
+            [(kept, row_spec(rows, cols, batch)), (came, row_spec(rows, cols, batch))],
+            [((own_rows, cols), BF16, row_spec(rows, cols))],
+        )
+        return kept, came, swap(passed, "th"), passed
+
+    def terms(*scattered):
+        return [(t, row_spec(rows, t.shape[1])) for part in scattered for t in part[:3]]
+
+    def stack_rows(step, low, order, *others):
+        beside, across = swap(low, "tl"), swap(low, "th")
+        across = after(order, across, *others)
+        parts = (low, across, beside, swap(across, "tl"))
+        return tuple(as_rows(v) for v in call(step, stack_kernel, [], batch, pieces(parts), spread_outs))
+
+    attn_own = after(102, attn_own, down_pair)
+    attn_pair = tuple(part.reshape(hi, depth + ROW_PAD, -1) for part in (attn_own, swap_x(attn_own)))
+    qkv_w = tuple(part[:, :depth].reshape(hi * depth, -1) for part in attn_pair)
+    out_w = (out_own, swap_x(after(138, out_own, attn_pair[1])))
+    gain_one = tuple(part[:, depth, :depth].reshape(1, half).astype(F32) for part in attn_pair)
+    gain_two = tuple(part[:, depth, depth : 2 * depth].reshape(1, half).astype(F32) for part in attn_pair)
 
     *seq_one, x_own, x_oth = call(
+        2,
         functools.partial(norm_in_kernel, hi),
         [at],
         batch,
@@ -366,14 +508,16 @@
         spread_outs + [((own_rows, half), BF16, row_spec(rows, half))] * 2,
     )
     seq_one = tuple(as_rows(v) for v in seq_one)
-
-    qkv = dot(seq_one[0], qkv_w[0]) + dot(seq_one[1], qkv_w[1])
-    all_cols = qkv.shape[1]
+    gate_near = after(105, after(104, gate_own, out_w[1]), seq_one[0])
+    gate_w = (gate_own, swap_x(gate_near))
+    up_w = (up_own, swap_x(after(106, up_own, gate_w[1])))
+
+    qkv = project(3, seq_one, qkv_w, F32)
+    qkv = after(144, after(107, qkv, out_w[1]), cot_parts[1])
     pair_spec, q_spec = quad_spec(rows, PAIR), quad_spec(rows, q_cols)
     lse_spec = pl.BlockSpec((1, 2 * pairs, length), lambda i, *_: (i, 0, 0))
-    score_flops = 2 * batch * 2 * pairs * length * length * PAIR
-    score_exps = batch * 2 * pairs * length * length
     query_rot, kv_rot, mixed, lse = call(
+        4,
         functools.partial(attend_kernel, pairs),
         [span],
         batch,
@@ -389,99 +533,87 @@
             pltpu.VMEM((2, length, PAIR), BF16),
             pltpu.VMEM((2, PAIR, length), BF16),
         ],
-        flops=2 * score_flops,
-        exps=score_exps,
-    )
-    mixed = after(as_rows(mixed), own_parts[2])
-
-    def scatter_rows(partial):
-        came = swap(partial[2 * own_rows :], "tl")
-        sent = (partial[own_rows : 2 * own_rows].astype(F32) + came[own_rows:].astype(F32)).astype(BF16)
-        return partial, came, swap(sent, "th")
-
-    def terms(pair):
-        return [(t, row_spec(rows, half)) for part in pair for t in part]
-
-    out_w = flat(out_pair)
-    attn_terms = [scatter_rows(dot_rt(mixed, w).astype(BF16)) for w in out_w]
-    half_ins = lambda *values: [(v, row_spec(rows, half)) for v in values]
-    half_outs = [((own_rows, half), F32, row_spec(rows, half))] * 2
-    low_out = [((own_rows, width), BF16, row_spec(rows, width))]
+    )
+    mixed = as_rows(mixed)
+    attn_oth = scatter_rows(6, *project_back(5, mixed, out_w[1]))
+    attn_own = scatter_rows(8, *project_back(7, after(108, mixed, attn_oth[3]), out_w[0]))
     h_own, h_oth, normed_two = call(
+        9,
         residual_kernel,
         [],
         batch,
-        half_ins(after(x_own, own_parts[3]), x_oth) + terms(attn_terms) + gain_in(gain_two),
+        half_ins(after(109, x_own, gate_own), x_oth) + terms(attn_own, attn_oth) + gain_in(gain_two),
         half_outs + low_out,
     )
-
-    def stack_rows(low, *others):
-        parts = gather_rows(low)
-        parts = (after(parts[0], *others), *parts[1:]) if others else parts
-        return tuple(as_rows(v) for v in call(stack_kernel, [], batch, pieces(parts), spread_outs))
-
-    gate_w, up_w = flat(gather_x(own_parts[2])), flat(gather_x(own_parts[3]))
-    normed_two = after(normed_two, gate_w[1])
-    seq_two = stack_rows(normed_two, own_parts[4], up_w[1])
-
-    gate_pre = dot(seq_two[0], gate_w[0]) + dot(seq_two[1], gate_w[1])
-    up_pre = dot(seq_two[0], up_w[0]) + dot(seq_two[1], up_w[1])
-    sigmoid = jax.nn.sigmoid(gate_pre)
-    activated = gate_pre * sigmoid
-    inner = (activated * up_pre).astype(BF16)
-    down_w = flat(gather_x(own_parts[4]))
-
-    def send_grad(oth, grad):
-        return dot_lt(oth, grad).astype(BF16)
-
-    def total_grad(own, grad, came):
-        return (dot_lt(own, grad) + came.astype(F32)).astype(BF16)
+    (seq_cot,) = call(
+        1,
+        functools.partial(pairs_kernel, hi),
+        [at],
+        batch,
+        pieces((after(103, cot_own, normed_two), *cot_parts[1:])),
+        [(quad + (width,), BF16, quad_spec(rows, width))],
+    )
+    seq_cot = as_rows(seq_cot)
+    seq_two = stack_rows(10, normed_two, 111, gate_w[1], seq_cot)
+    gate_pre = project(38, seq_two, gate_w, F32)
+    inner, for_gate, for_up = call(
+        11, expand_kernel, [], steps, tiles(*seq_two) + wholes(*up_w) + tiles(gate_pre), [hidden_out] * 3
+    )
 
     def reduce_z(total):
         return lax.psum_scatter(total, "fh", scatter_dimension=0, tiled=True)
 
-    down_sent = send_grad(seq_cot[1], inner)
-    down_w = both_after(down_w, down_sent)
-    down_came = swap(down_sent, "fl")
-    grad_inner = dot(seq_cot[0], down_w[0]) + dot(seq_cot[1], down_w[1])
-    gate_g = (grad_inner * up_pre * sigmoid * (1.0 + gate_pre * (1.0 - sigmoid))).astype(BF16)
-    up_g = (grad_inner * activated).astype(BF16)
-    gate_sent = send_grad(seq_two[1], gate_g)
-    gate_gn = after(gate_g, gate_sent)
-    normed_terms = [
-        scatter_rows((dot_rt(gate_gn, g) + dot_rt(up_g, u)).astype(BF16)) for g, u in zip(gate_w, up_w)
-    ]
-    down_total = total_grad(seq_cot[0], inner, down_came)
-    grad_down = reduce_z(down_total)
-    gate_sent = after(gate_sent, down_came)
-    gate_came = swap(gate_sent, "fl")
+    down_part = weight_grad(12, seq_cot, inner)
+    grad_down = reduce_z(down_part)
+    gate_g, up_g = call(
+        13,
+        inner_back_kernel,
+        [],
+        steps,
+        tiles(after(112, seq_cot, down_part)) + wholes(down_w) + tiles(for_gate, for_up),
+        [hidden_out] * 2,
+    )
+
+    def expand_back(step, which, gate_g):
+        outs = two_part_outs(all_rows, half, tile)
+        ins = tiles(gate_g, up_g) + wholes(gate_w[which], up_w[which])
+        return call(step, expand_back_kernel, [], steps, ins, outs)
+
+    gate_sent = weight_grad(16, seq_two[1], gate_g)
+    gate_came = swap_x(gate_sent)
+    oth_parts = expand_back(14, 1, after(113, gate_g, gate_sent))
+    normed_oth = scatter_rows(15, *oth_parts)
+    own_parts = expand_back(17, 0, after(116, after(115, gate_g, oth_parts[0]), normed_oth[3]))
+    normed_own = scatter_rows(18, *own_parts)
+    up_sent = weight_grad(19, seq_two[1], after(117, up_g, normed_own[3]))
     r_own, r_oth, attn_low, gain_s_own, gain_s_oth = call(
-        middle_kernel,
-        [],
+        20,
+        functools.partial(middle_kernel, hi),
+        [at],
         batch,
-        half_ins(after(h_own, down_total), h_oth)
-        + terms(normed_terms)
+        half_ins(after(118, h_own, up_sent), h_oth)
+        + terms(normed_own, normed_oth)
         + gain_in(gain_two)
-        + half_ins(seq_cot[0], seq_cot[1]),
-        half_outs + low_out + [((1, half), F32, full_spec((1, half)))] * 2,
-    )
-    up_sent = send_grad(seq_two[1], up_g)
-    block_terms = [scatter_rows(dot_rt(inner, w).astype(BF16)) for w in down_w]
-
-    whole_out = [((own_rows, width), F32, row_spec(rows, width))]
-    (block_out,) = call(
-        functools.partial(block_out_kernel, hi), [at], batch, half_ins(h_own, h_oth) + terms(block_terms), whole_out
-    )
-
-    gate_total = total_grad(seq_two[0], gate_g, gate_came)
+        + [(cot_own, row_spec(rows, width))],
+        half_outs + low_out + sum_outs * 2,
+    )
+    gate_came = after(120, gate_came, attn_low)
+    up_came = swap_x(after(122, up_sent, gate_came))
+    gate_total = weight_grad(23, seq_two[0], gate_g, gate_came)
     grad_gate = reduce_z(gate_total)
-    seq_attn = stack_rows(attn_low, gate_total, up_sent, block_terms[0][1], block_terms[1][1])
-    out_sent = send_grad(seq_attn[1], mixed)
-    grad_mixed = (dot(seq_attn[0], out_w[0]) + dot(seq_attn[1], out_w[1])).astype(BF16)
-    up_sent = after(up_sent, gate_came)
-    up_came = swap(up_sent, "fl")
-    grad_mixed = after(grad_mixed, grad_down)
+    block_parts = project_back(21, after(119, inner, gate_total), down_w)
+
+    seq_attn = stack_rows(24, attn_low, 123, gate_total, block_parts[0])
+    block_terms = scatter_rows(22, after(124, block_parts[0], seq_attn[0]), block_parts[1])
+    grad_mixed = project(25, seq_attn, out_w, BF16)
+    out_sent = weight_grad(26, after(125, seq_attn[1], grad_mixed), mixed)
+    up_came = after(127, after(126, up_came, out_sent), grad_down)
+    out_came = swap_x(after(128, out_sent, up_came))
+    up_total = weight_grad(28, seq_two[0], up_g, up_came)
+    grad_up = reduce_z(up_total)
+    grad_mixed = after(139, grad_mixed, up_total)
     (qkv_g,) = call(
+        27,
         functools.partial(attend_back_kernel, pairs),
         [span],
         batch,
@@ -501,55 +633,65 @@
             pltpu.VMEM((2, length, PAIR), F32),
             pltpu.VMEM((2, length, PAIR), F32),
         ],
-        flops=5 * score_flops,
-        exps=score_exps,
-    )
-    up_total = total_grad(seq_two[0], up_g, up_came)
-    grad_up = reduce_z(up_total)
-    qkv_g = after(as_rows(qkv_g), up_came, grad_gate, block_out)
-    out_sent = after(out_sent, up_came)
-    out_came = swap(out_sent, "fl")
-
-    partial_one = tuple(dot_rt(qkv_g, w).astype(BF16) for w in qkv_w)
-    first_terms = [scatter_rows(p) for p in partial_one]
-    gain_part = tuple(
-        jnp.sum(p.astype(F32) * s.astype(F32), axis=0) / g[0] for p, s, g in zip(partial_one, seq_one, gain_one)
-    )
+    )
+    qkv_g = after(141, after(140, after(129, as_rows(qkv_g), out_came), block_terms[2]), grad_gate)
+
+    def project_gain(step, which, grad):
+        outs = two_part_outs(all_rows, half, tile) + sum_outs
+        kept, sent, sums = call(
+            step, project_gain_kernel, [], steps, tiles(grad) + wholes(qkv_w[which]) + tiles(seq_one[which]), outs
+        )
+        return (kept, sent), sums / gain_one[which]
 
     def gain_rows(one, two):
         pair = jnp.concatenate([one.reshape(hi, 1, depth), two.reshape(hi, 1, depth)], axis=2)
         return jnp.pad(pair, ((0, 0), (0, ROW_PAD - 1), (0, all_cols - 2 * depth)))
 
     def with_gains(grad, one, two):
-        blocks = jnp.concatenate([grad.reshape(hi, depth, all_cols), gain_rows(one, two)], axis=1)
-        return blocks.reshape(hi * (depth + ROW_PAD), all_cols)
-
-    qkv_sent = with_gains(dot_lt(seq_one[1], qkv_g), gain_part[1], gain_s_oth[0]).astype(BF16)
-    qkv_came = swap(qkv_sent, "fl")
-    grad_out = reduce_z(total_grad(seq_attn[0], mixed, out_came))
-    qkv_total = with_gains(dot_lt(seq_one[0], qkv_g), gain_part[0], gain_s_own[0])
-    qkv_total = (qkv_total + qkv_came.astype(F32)).astype(BF16)
-    grad_qkv = lax.psum_scatter(qkv_total, "fh", scatter_dimension=0, tiled=True)
-    gain_sums = lax.psum(grad_qkv[depth, : 2 * depth].astype(F32), ("th", "tl"))
-
+        return jnp.concatenate([grad.reshape(hi, depth, all_cols), gain_rows(one, two)], axis=1)
+
+    oth_parts, oth_gain = project_gain(29, 1, qkv_g)
+    first_oth = scatter_rows(30, *oth_parts)
+    qkv_sent = with_gains(
+        weight_grad(31, seq_one[1], after(130, qkv_g, oth_parts[0])), oth_gain, gain_s_oth
+    ).astype(BF16)
+    qkv_came = swap_x(after(134, qkv_sent, out_came))
+    out_came = after(132, out_came, qkv_sent)
+    out_total = weight_grad(34, seq_attn[0], mixed, out_came)
+    own_parts, own_gain = project_gain(32, 0, after(143, after(142, after(131, qkv_g, qkv_sent), first_oth[3]), out_total))
+    first_own = scatter_rows(33, *own_parts)
+    grad_out = reduce_z(out_total)
+    qkv_total = with_gains(weight_grad(35, seq_one[0], qkv_g, kind=F32), own_gain, gain_s_own)
+    qkv_total = (qkv_total + after(135, qkv_came, grad_up).astype(F32)).astype(BF16)
+    grad_qkv = reduce_z(qkv_total.reshape(hi * (depth + ROW_PAD), all_cols)).astype(F32)
+    gain_sums = lax.psum(grad_qkv[depth, : 2 * depth], ("th", "tl"))
+    (block_out,) = call(
+        36,
+        functools.partial(block_out_kernel, hi),
+        [at],
+        batch,
+        half_ins(after(137, after(136, h_own, qkv_sent), grad_up), h_oth) + terms(block_terms),
+        whole_out,
+    )
     (grad_in,) = call(
+        37,
         functools.partial(grad_in_kernel, hi),
         [at],
         batch,
-        half_ins(x_own, x_oth) + terms(first_terms) + gain_in(gain_one) + half_ins(r_own, r_oth),
+        half_ins(x_own, x_oth) + terms(first_own, first_oth) + gain_in(gain_one) + half_ins(r_own, r_oth),
         whole_out,
     )
-    grad_qkv = grad_qkv[:depth].astype(F32)
+    grad_down = grad_down[:depth].astype(F32) + swap_x(grad_down[depth:]).astype(F32)
     return (
         block_out.reshape(block_in.shape),
         grad_in.reshape(block_in.shape),
-        grad_qkv[:, :q_cols],
-        grad_qkv[:, q_cols : q_cols + kv_cols],
-        grad_qkv[:, q_cols + kv_cols :],
+        grad_qkv[:depth, :q_cols],
+        grad_qkv[:depth, q_cols : q_cols + kv_cols],
+        grad_qkv[:depth, q_cols + kv_cols :],
         grad_out.astype(F32).T,
         grad_gate.astype(F32),
         grad_up.astype(F32),
-        grad_down.astype(F32).T,
+        grad_down.T,
         gain_sums[:depth],
         gain_sums[depth:],
     )

time: 791 us -> 666 us (0.84)
  Pallas kernels: 107 us -> 353 us
  matrix products: 202 us -> 0 us
  waiting for transfers between devices: 345 us -> 202 us
  other arithmetic: 34.5 us -> 18 us
    pallas_call x10 -> x38, Pallas kernels: 107 us -> 353 us  [call(): pl.pallas_call(kernel, out_shape=[jax.ShapeDtypeStruct(shape, kind) for s...]
    dot_general x30 -> x0, matrix products: 202 us -> none  [the longest x10 79.3 us: dot(): return jnp.dot(a, b, preferred_element_type=F32)]
    ppermute x38 -> x36, waiting for transfers between devices: 238 us -> 166 us  [swap(): return lax.ppermute(value, axis, SWAP)]
    all_gather x5, waiting for transfers between devices: 105 us -> 34.6 us  [gather(): return lax.all_gather(part, 'fh', axis=0, tiled=True)]
    convert_element_type x10 -> x1, other arithmetic: 16.3 us -> 3.14 us  [per_device(): (qkv_total + after(135, qkv_came, grad_up).astype(F32)).astype(BF16)]
    dot_general x2 -> x0, local copies, waits for them, and re-layouts: 8.03 us -> none  [dot_lt(): lax.dot_general(a, b, (((0,), (0,)), ((), ())), preferred_element_type=F32)]
    unnamed x131 -> x74, local copies, waits for them, and re-layouts: 19.7 us -> 24.1 us
    ppermute x38 -> x36, starting transfers between devices: 28.8 us -> 26.8 us  [swap(): return lax.ppermute(value, axis, SWAP)]
  transfers between devices with their start and end apart: 48 -> 46, of which waited for: 23 -> 20; matrix products, arithmetic and copies ran while one was open for 33% -> 5% of each run, Pallas kernels for 14% -> 54%
where the time goes in v2:
time: 666 us; the launch traced here: 660 us
  Pallas kernels  353 us (53%)
  waiting for transfers between devices  202 us (30%)
  local copies, waits for them, and re-layouts  37.5 us (6%)
  starting transfers between devices  28.3 us (4%)
  other arithmetic  18 us (3%)
  between operations  14.8 us (2%)
    pallas_call x38, Pallas kernels, call(): pl.pallas_call(kernel, out_shape=[jax.ShapeDtypeStruct(shape, kind) for s...  353 us
    ppermute x36, waiting for transfers between devices, swap(): return lax.ppermute(value, axis, SWAP)  166 us
    all_gather x5, waiting for transfers between devices, gather(): return lax.all_gather(part, 'fh', axis=0, tiled=True)  34.6 us
    ppermute x36, starting transfers between devices, swap(): return lax.ppermute(value, axis, SWAP)  26.8 us
    unnamed x74, local copies, waits for them, and re-layouts  24.1 us
  transfers between devices with their start and end apart: 46, of which 20 were waited for; matrix products, arithmetic and copies ran while one was open for 5% of the time, Pallas kernels for 54%

profile of v2, /device:TPU:0, one launch (start us, length us, event | category | flops | bytes accessed | tf_op | source)
XLA Modules:
  0.0 659.6 jit_solution(11259373649637032234)
XLA Ops:
  19.7 14.6 %collective-permute-done.3 = bf16[256,1408]{1,0:T(8,128)(2,1)S(1)} collective-permute-done((bf16[256,1408]{1,0:T(8,128)(2,1)S(1)}, bf16[256,1408]{1,0:T(8,128)(2,1)S(1)}, u32[]{:S(2)}, u32[]{:S(2)}) %collective-permute-start.3) | collective-permute-done | bytes 720928 | tf_op jit(solution)/shard_map/ppermute | solution.py:37
  35.5 13.0 %all-gather.6.cloned.1.call-done = bf16[1088,640]{1,0:T(8,128)(2,1)} async-done(((bf16[272,640]{1,0:T(8,128)(2,1)}), bf16[1088,640]{1,0:T(8,128)(2,1)}) %all-gather.6.cloned.1.call-update) | async-done | bytes 1392656 | tf_op jit(solution)/shard_map/all_gather | solution.py:404
  56.7 20.9 %all-gather.10.cloned.1.call-done.weight.w_own = bf16[1024,512]{1,0:T(8,128)(2,1)} async-done(((bf16[256,512]{1,0:T(8,128)(2,1)}), bf16[1024,512]{1,0:T(8,128)(2,1)}) %all-gather.10.cloned.1.call-update) | async-done | bytes 1048592 | tf_op jit(solution)/shard_map/all_gather | solution.py:404
  101.6 9.9 %shard_map.204 = f32[1536,640]{1,0:T(8,128)} custom-call(bf16[1536,1024]{1,0:T(8,128)(2,1)} %bitcast.60, bf16[1536,1024]{1,0:T(8,128)(2,1)} %bitcast.75, bf16[1024,640]{1,0:T(8,128)(2,1)} %bitcast.78, bf16[1024,640]{1,0:T(8,128)(2,1)} %bitcast.80), custom_call_target="tpu_custom_call" | custom-call | flops 774899968 | bytes 2583003 | tf_op jit(solution)/shard_map/pallas_call | solution.py:71
  111.6 21.6 %shard_map.205 = (bf16[4,3,128,512]{3,2,1,0:T(8,128)(2,1)}, bf16[4,3,128,128]{3,2,1,0:T(8,128)(2,1)}, bf16[4,3,128,512]{3,2,1,0:T(8,128)(2,1)}, f32[3,8,512]{2,1,0:T(8,128)}) custom-call(s32[3]{0:T(128)} %bitcast.113, f32[4,3,128,640]{3,2,1,0:T(8,128)} %bitcast.84, f32[512,128]{1,0:T(8,128)} %copy.64.cos, f32[512,128]{1,0:T(8,128)} %pad_maximum_fusion.2.sine, ...), custom_call_target="tpu_custom_call" | custom-call | flops 1688999936 | bytes 5630004 | tf_op jit(solution)/shard_map/pallas_call | solution.py:71
  165.1 9.4 %collective-permute-done.10.b2 = bf16[384,1024]{1,0:T(8,128)(2,1)S(1)} collective-permute-done((bf16[384,1024]{1,0:T(8,128)(2,1)S(1)}, bf16[384,1024]{1,0:T(8,128)(2,1)S(1)}, u32[]{:S(2)}, u32[]{:S(2)}) %collective-permute-start.10) | collective-permute-done | bytes 786464 | tf_op jit(solution)/shard_map/ppermute | solution.py:37
  174.4 16.3 %collective-permute-done.9.a2 = bf16[384,1024]{1,0:T(8,128)(2,1)S(1)} collective-permute-done((bf16[384,1024]{1,0:T(8,128)(2,1)}, bf16[384,1024]{1,0:T(8,128)(2,1)S(1)}, u32[]{:S(2)}, u32[]{:S(2)}) %collective-permute-start.9) | collective-permute-done | bytes 786464 | tf_op jit(solution)/shard_map/ppermute | solution.py:37
  212.8 20.8 %collective-permute-done.11.p1 = bf16[384,2048]{1,0:T(8,128)(2,1)} collective-permute-done((bf16[384,2048]{1,0:T(8,128)(2,1)}, bf16[384,2048]{1,0:T(8,128)(2,1)}, u32[]{:S(2)}, u32[]{:S(2)}) %collective-permute-start.11) | collective-permute-done | bytes 1572896 | tf_op jit(solution)/shard_map/ppermute | solution.py:37
  244.7 15.2 %shard_map.213.gate_in = f32[1536,1408]{1,0:T(8,128)} custom-call(bf16[1536,1024]{1,0:T(8,128)(2,1)} %bitcast.52, bf16[1536,1024]{1,0:T(8,128)(2,1)} %bitcast.56, bf16[1024,1408]{1,0:T(8,128)(2,1)} %all-gather.8.cloned.1.call-done.w_own.gate_w, bf16[1024,1408]{1,0:T(8,128)(2,1)} %copy-done.1), custom_call_target="tpu_custom_call" | custom-call | flops 1084800000 | bytes 3616038 | tf_op jit(solution)/shard_map/pallas_call | solution.py:71
  259.8 9.6 %collective-permute-done.17.u_oth.up_w = bf16[1024,1408]{1,0:T(8,128)(2,1)S(1)} collective-permute-done((bf16[1024,1408]{1,0:T(8,128)(2,1)}, bf16[1024,1408]{1,0:T(8,128)(2,1)S(1)}, u32[]{:S(2)}, u32[]{:S(2)}) %collective-permute-start.17) | collective-permute-done | bytes 2883616 | tf_op jit(solution)/shard_map/ppermute | solution.py:37
  271.0 17.8 %shard_map.214 = (bf16[1536,1408]{1,0:T(8,128)(2,1)}, bf16[1536,1408]{1,0:T(8,128)(2,1)}, bf16[1536,1408]{1,0:T(8,128)(2,1)}) custom-call(bf16[1536,1024]{1,0:T(8,128)(2,1)} %bitcast.53, bf16[1536,1024]{1,0:T(8,128)(2,1)} %bitcast.57, bf16[1024,1408]{1,0:T(8,128)(2,1)} %all-gather.12.cloned.1.call-done.u_own.up_w, bf16[1024,1408]{1,0:T(8,128)(2,1)} %copy-done.2, ...), custom_call_target="tpu_custom_call" | custom-call | flops 1200600064 | bytes 4002011 | tf_op jit(solution)/shard_map/pallas_call | solution.py:71
  288.8 14.8 %shard_map.215 = bf16[2048,1408]{1,0:T(8,128)(2,1)} custom-call(bf16[1536,2048]{1,0:T(8,128)(2,1)} %bitcast.50, bf16[1536,1408]{1,0:T(8,128)(2,1)} %get-tuple-element.139.grad.rows), custom_call_target="tpu_custom_call" | custom-call | flops 1184999936 | bytes 3950012 | tf_op jit(solution)/shard_map/pallas_call | solution.py:71
  304.6 17.2 %shard_map.216 = (bf16[1536,1408]{1,0:T(8,128)(2,1)}, bf16[1536,1408]{1,0:T(8,128)(2,1)}) custom-call(bf16[1536,2048]{1,0:T(8,128)(2,1)} %bitcast.51, bf16[2048,1408]{1,0:T(8,128)(2,1)} %all-gather.14.cloned.1.call-done.weight, bf16[1536,1408]{1,0:T(8,128)(2,1)} %get-tuple-element.115.for_gate, bf16[1536,1408]{1,0:T(8,128)(2,1)} %get-tuple-element.116.for_up), custom_call_target="tpu_custom_call" | custom-call | flops 1301400064 | bytes 4338013 | tf_op jit(solution)/shard_map/pallas_call | solution.py:71
  321.8 9.2 %shard_map.217 = bf16[1024,1408]{1,0:T(8,128)(2,1)} custom-call(bf16[1536,1024]{1,0:T(8,128)(2,1)} %bitcast.58, bf16[1536,1408]{1,0:T(8,128)(2,1)} %get-tuple-element.121.grad.gate_g), custom_call_target="tpu_custom_call" | custom-call | flops 704700032 | bytes 2349016 | tf_op jit(solution)/shard_map/pallas_call | solution.py:71
  332.4 15.5 %shard_map.218 = (bf16[768,1024]{1,0:T(8,128)(2,1)}, bf16[768,1024]{1,0:T(8,128)(2,1)}) custom-call(bf16[1536,1408]{1,0:T(8,128)(2,1)} %get-tuple-element.121.grad.gate_g, bf16[1536,1408]{1,0:T(8,128)(2,1)} %get-tuple-element.124.up_g.grad, bf16[1024,1408]{1,0:T(8,128)(2,1)} %copy-done.1, bf16[1024,1408]{1,0:T(8,128)(2,1)} %copy-done.2), custom_call_target="tpu_custom_call" | custom-call | flops 1169400064 | bytes 3898014 | tf_op jit(solution)/shard_map/pallas_call | solution.py:71
  348.0 15.6 %shard_map.219 = (bf16[768,1024]{1,0:T(8,128)(2,1)}, bf16[768,1024]{1,0:T(8,128)(2,1)}) custom-call(bf16[1536,1408]{1,0:T(8,128)(2,1)} %get-tuple-element.121.grad.gate_g, bf16[1536,1408]{1,0:T(8,128)(2,1)} %get-tuple-element.124.up_g.grad, bf16[1024,1408]{1,0:T(8,128)(2,1)} %all-gather.8.cloned.1.call-done.w_own.gate_w, ...), custom_call_target="tpu_custom_call" | custom-call | flops 24907499520 | bytes 83025016 | tf_op jit(solution)/shard_map/pallas_call | solution.py:71
  374.7 9.0 %shard_map.221 = bf16[1024,1408]{1,0:T(8,128)(2,1)} custom-call(bf16[1536,1024]{1,0:T(8,128)(2,1)} %bitcast.59, bf16[1536,1408]{1,0:T(8,128)(2,1)} %get-tuple-element.124.up_g.grad), custom_call_target="tpu_custom_call" | custom-call | flops 704700032 | bytes 2349019 | tf_op jit(solution)/shard_map/pallas_call | solution.py:71
  389.0 15.9 %collective-permute-done.19.a2 = bf16[384,1024]{1,0:T(8,128)(2,1)S(1)} collective-permute-done((bf16[384,1024]{1,0:T(8,128)(2,1)}, bf16[384,1024]{1,0:T(8,128)(2,1)S(1)}, u32[]{:S(2)}, u32[]{:S(2)}) %collective-permute-start.19) | collective-permute-done | bytes 786464 | tf_op jit(solution)/shard_map/ppermute | solution.py:37
  415.1 9.8 %shard_map.229 = bf16[1024,1408]{1,0:T(8,128)(2,1)} custom-call(bf16[1536,1024]{1,0:T(8,128)(2,1)} %bitcast.54, bf16[1536,1408]{1,0:T(8,128)(2,1)} %get-tuple-element.121.grad.gate_g, bf16[1024,1408]{1,0:T(8,128)(2,1)} %copy-done.6), custom_call_target="tpu_custom_call" | custom-call | flops 766800000 | bytes 2556023 | tf_op jit(solution)/shard_map/pallas_call | solution.py:71
  427.0 33.9 %collective-permute-done.22.p1 = bf16[384,2048]{1,0:T(8,128)(2,1)S(1)} collective-permute-done((bf16[384,2048]{1,0:T(8,128)(2,1)}, bf16[384,2048]{1,0:T(8,128)(2,1)S(1)}, u32[]{:S(2)}, u32[]{:S(2)}) %collective-permute-start.22) | collective-permute-done | bytes 1572896 | tf_op jit(solution)/shard_map/ppermute | solution.py:37
  460.9 16.5 %shard_map.230 = (bf16[768,2048]{1,0:T(8,128)(2,1)}, bf16[768,2048]{1,0:T(8,128)(2,1)}) custom-call(bf16[1536,1408]{1,0:T(8,128)(2,1)} %get-tuple-element.139.grad.rows, bf16[2048,1408]{1,0:T(8,128)(2,1)} %all-gather.14.cloned.1.call-done.weight), custom_call_target="tpu_custom_call" | custom-call | flops 1146300032 | bytes 3821021 | tf_op jit(solution)/shard_map/pallas_call | solution.py:71
  491.5 9.8 %shard_map.227 = bf16[1024,1408]{1,0:T(8,128)(2,1)} custom-call(bf16[1536,1024]{1,0:T(8,128)(2,1)} %bitcast.55, bf16[1536,1408]{1,0:T(8,128)(2,1)} %get-tuple-element.124.up_g.grad, bf16[1024,1408]{1,0:T(8,128)(2,1)} %collective-permute-done.26.came), custom_call_target="tpu_custom_call" | custom-call | flops 766800000 | bytes 2556028 | tf_op jit(solution)/shard_map/pallas_call | solution.py:71
  517.3 30.9 %shard_map.228 = bf16[4,3,128,640]{3,2,1,0:T(8,128)(2,1)} custom-call(s32[3]{0:T(128)} %bitcast.114, bf16[4,3,128,512]{3,2,1,0:T(8,128)(2,1)} %get-tuple-element.103.query_in, bf16[4,3,128,128]{3,2,1,0:T(8,128)(2,1)} %get-tuple-element.104.kv_in, bf16[4,3,128,512]{3,2,1,0:T(8,128)(2,1)} %bitcast.88, f32[3,8,512]{2,1,0:T(8,128)} %get-tuple-element.136.lse, ...), custom_call_target="tpu_custom_call" | custom-call | flops 2394299904 | bytes 7981027 | tf_op jit(solution)/shard_map/pallas_call | solution.py:71
  597.0 9.3 %collective-permute-done.34 = bf16[4,272,640]{2,1,0:T(8,128)(2,1)S(1)} collective-permute-done((bf16[4,272,640]{2,1,0:T(8,128)(2,1)}, bf16[4,272,640]{2,1,0:T(8,128)(2,1)S(1)}, u32[]{:S(2)}, u32[]{:S(2)}) %collective-permute-start.34) | collective-permute-done | bytes 1392672 | tf_op jit(solution)/shard_map/ppermute | solution.py:37
  (229 shorter events, 268.3 us)
Async XLA Ops:
  7.2 41.3 %all-gather.6.cloned.1.call-start = ((), (), s32[]{:S(2)}) async-start(), calls=%async_computation.5 | async-start | bytes 1740800 | tf_op jit(solution)/shard_map/all_gather | solution.py:404
  11.5 66.0 %all-gather.10.cloned.1.call-start = ((), (), s32[]{:S(2)}) async-start(), calls=%async_computation.7 | async-start | bytes 1310720 | tf_op jit(solution)/shard_map/all_gather | solution.py:404
  13.4 126.5 %all-gather.8.cloned.1.call-start = ((), (), s32[]{:S(2)}) async-start(), calls=%async_computation.6 | async-start | bytes 3604480 | tf_op jit(solution)/shard_map/all_gather | solution.py:404
  14.2 184.8 %all-gather.12.cloned.1.call-start = ((), (), s32[]{:S(2)}) async-start(), calls=%async_computation.8 | async-start | bytes 3604480 | tf_op jit(solution)/shard_map/all_gather | solution.py:404
  14.7 289.8 %all-gather.14.cloned.1.call-start = ((), (), s32[]{:S(2)}) async-start(), calls=%async_computation.9 | async-start | bytes 7208960 | tf_op jit(solution)/shard_map/all_gather | solution.py:404
  18.1 36.0 %collective-permute-start = (bf16[384,2048]{1,0:T(8,128)(2,1)S(1)}, bf16[384,2048]{1,0:T(8,128)(2,1)}, u32[]{:S(2)}, u32[]{:S(2)}) collective-permute-start(bf16[384,2048]{1,0:T(8,128)(2,1)S(1)} %bitcast.90), channel_id=1, source_target_pairs={{0,2},{2,0},{1,3},{3,1},{4,6},{6,4},{5,7},{7,5},{8,10},{10,8},{9,1... | collective-permute-start | bytes 4718600 | tf_op jit(solution)/shard_map/ppermute | solution.py:37
  50.0 43.0 %collective-permute-start.1 = (bf16[384,2048]{1,0:T(8,128)(2,1)S(1)}, bf16[384,2048]{1,0:T(8,128)(2,1)}, u32[]{:S(2)}, u32[]{:S(2)}) collective-permute-start(bf16[384,2048]{1,0:T(8,128)(2,1)S(1)} %bitcast.91), channel_id=1, source_target_pairs={{0,1},{1,0},{2,3},{3,2},{4,5},{5,4},{6,7},{7,6},{8,9},{9,8},{10,11... | collective-permute-start | bytes 4718600 | tf_op jit(solution)/shard_map/ppermute | solution.py:37
  54.1 38.9 %collective-permute-start.2 = (bf16[384,2048]{1,0:T(8,128)(2,1)}, bf16[384,2048]{1,0:T(8,128)(2,1)}, u32[]{:S(2)}, u32[]{:S(2)}) collective-permute-start(bf16[384,2048]{1,0:T(8,128)(2,1)} %collective-permute-done.p1), channel_id=1, source_target_pairs={{0,1},{1,0},{2,3},{3,2},{4,5},{5,4},{6,7},{7,6},{8,9},{9,8},{10,11... | collective-permute-start | bytes 4718600 | tf_op jit(solution)/shard_map/ppermute | solution.py:37
  54.1 57.4 %collective-permute-start.6 = (bf16[384,2048]{1,0:T(8,128)(2,1)}, bf16[384,2048]{1,0:T(8,128)(2,1)}, u32[]{:S(2)}, u32[]{:S(2)}) collective-permute-start(bf16[384,2048]{1,0:T(8,128)(2,1)} %bitcast.11.p0.upstream), channel_id=1, source_target_pairs={{0,2},{2,0},{1,3},{3,1},{4,6},{6,4},{5,7},{7,5},{8,10},{10,8},{9,1... | collective-permute-start | bytes 4718600 | tf_op jit(solution)/shard_map/ppermute | solution.py:37
  84.7 406.9 %reduce-scatter.6.cloned.1.call-start = ((), (), s32[]{:S(2)}) async-start(), calls=%async_computation.10 | async-start | bytes 7208960 | tf_op jit(solution)/shard_map/reduce_scatter | solution.py:564
  140.0 65.1 %collective-permute-start.12 = (bf16[1024,1408]{1,0:T(8,128)(2,1)}, bf16[1024,1408]{1,0:T(8,128)(2,1)S(1)}, u32[]{:S(2)}, u32[]{:S(2)}) collective-permute-start(bf16[1024,1408]{1,0:T(8,128)(2,1)} %all-gather.8.cloned.1.call-done.w_own.gate_w), channel_id=1, source_target_pairs={{0,4},{4,0},{1,5},{5,1},{2,6},{6,2},{3,7},{7,3},{8,12},{12,8},{9,1... | collective-permute-start | bytes 8650760 | tf_op jit(solution)/shard_map/ppermute | solution.py:37
  163.4 42.3 %collective-permute-start.13 = (bf16[384,2048]{1,0:T(8,128)(2,1)}, bf16[384,2048]{1,0:T(8,128)(2,1)}, u32[]{:S(2)}, u32[]{:S(2)}) collective-permute-start(bf16[384,2048]{1,0:T(8,128)(2,1)} %bitcast.11.p0.upstream), channel_id=1, source_target_pairs={{0,1},{1,0},{2,3},{3,2},{4,5},{5,4},{6,7},{7,6},{8,9},{9,8},{10,11... | collective-permute-start | bytes 4718600 | tf_op jit(solution)/shard_map/ppermute | solution.py:37
  163.4 42.3 %collective-permute-start.14 = (bf16[384,2048]{1,0:T(8,128)(2,1)}, bf16[384,2048]{1,0:T(8,128)(2,1)}, u32[]{:S(2)}, u32[]{:S(2)}) collective-permute-start(bf16[384,2048]{1,0:T(8,128)(2,1)} %collective-permute-done.6.p1), channel_id=1, source_target_pairs={{0,1},{1,0},{2,3},{3,2},{4,5},{5,4},{6,7},{7,6},{8,9},{9,8},{10,11... | collective-permute-start | bytes 4718600 | tf_op jit(solution)/shard_map/ppermute | solution.py:37
  197.3 36.3 %collective-permute-start.11 = (bf16[384,2048]{1,0:T(8,128)(2,1)}, bf16[384,2048]{1,0:T(8,128)(2,1)}, u32[]{:S(2)}, u32[]{:S(2)}) collective-permute-start(bf16[384,2048]{1,0:T(8,128)(2,1)} %get-tuple-element.105.p0), channel_id=1, source_target_pairs={{0,2},{2,0},{1,3},{3,1},{4,6},{6,4},{5,7},{7,5},{8,10},{10,8},{9,1... | collective-permute-start | bytes 4718600 | tf_op jit(solution)/shard_map/ppermute | solution.py:37
  205.1 64.4 %collective-permute-start.17 = (bf16[1024,1408]{1,0:T(8,128)(2,1)}, bf16[1024,1408]{1,0:T(8,128)(2,1)S(1)}, u32[]{:S(2)}, u32[]{:S(2)}) collective-permute-start(bf16[1024,1408]{1,0:T(8,128)(2,1)} %all-gather.12.cloned.1.call-done.u_own.up_w), channel_id=1, source_target_pairs={{0,4},{4,0},{1,5},{5,1},{2,6},{6,2},{3,7},{7,3},{8,12},{12,8},{9,1... | collective-permute-start | bytes 8650760 | tf_op jit(solution)/shard_map/ppermute | solution.py:37
  303.7 244.5 %reduce-scatter.8.cloned.1.call-start = ((), (), s32[]{:S(2)}) async-start(), calls=%async_computation.11 | async-start | bytes 3604480 | tf_op jit(solution)/shard_map/reduce_scatter | solution.py:564
  331.0 82.5 %collective-permute-start.25 = (bf16[1024,1408]{1,0:T(8,128)(2,1)}, bf16[1024,1408]{1,0:T(8,128)(2,1)S(1)}, u32[]{:S(2)}, u32[]{:S(2)}) collective-permute-start(bf16[1024,1408]{1,0:T(8,128)(2,1)} %shard_map.217), channel_id=1, source_target_pairs={{0,4},{4,0},{1,5},{5,1},{2,6},{6,2},{3,7},{7,3},{8,12},{12,8},{9,1... | collective-permute-start | bytes 8650760 | tf_op jit(solution)/shard_map/ppermute | solution.py:37
  424.9 181.5 %reduce-scatter.10.cloned.1.call-start = ((), (), s32[]{:S(2)}) async-start(), calls=%async_computation.12 | async-start | bytes 3604480 | tf_op jit(solution)/shard_map/reduce_scatter | solution.py:564
  426.6 64.9 %collective-permute-start.26 = (bf16[1024,1408]{1,0:T(8,128)(2,1)}, bf16[1024,1408]{1,0:T(8,128)(2,1)}, u32[]{:S(2)}, u32[]{:S(2)}) collective-permute-start(bf16[1024,1408]{1,0:T(8,128)(2,1)} %shard_map.221), channel_id=1, source_target_pairs={{0,4},{4,0},{1,5},{5,1},{2,6},{6,2},{3,7},{7,3},{8,12},{12,8},{9,1... | collective-permute-start | bytes 8650760 | tf_op jit(solution)/shard_map/ppermute | solution.py:37
  427.0 50.4 %collective-permute-start.23 = (bf16[384,2048]{1,0:T(8,128)(2,1)}, bf16[384,2048]{1,0:T(8,128)(2,1)S(1)}, u32[]{:S(2)}, u32[]{:S(2)}) collective-permute-start(bf16[384,2048]{1,0:T(8,128)(2,1)} %get-tuple-element.128.p0), channel_id=1, source_target_pairs={{0,1},{1,0},{2,3},{3,2},{4,5},{5,4},{6,7},{7,6},{8,9},{9,8},{10,11... | collective-permute-start | bytes 4718600 | tf_op jit(solution)/shard_map/ppermute | solution.py:37
  501.4 128.7 %reduce-scatter.14.cloned.1.call-start = ((), (), s32[]{:S(2)}) async-start(), calls=%async_computation.14 | async-start | bytes 1310720 | tf_op jit(solution)/shard_map/reduce_scatter | solution.py:564
  507.1 41.0 %collective-permute-start.29 = (bf16[384,2048]{1,0:T(8,128)(2,1)}, bf16[384,2048]{1,0:T(8,128)(2,1)}, u32[]{:S(2)}, u32[]{:S(2)}) collective-permute-start(bf16[384,2048]{1,0:T(8,128)(2,1)} %shard_map.231), channel_id=1, source_target_pairs={{0,2},{2,0},{1,3},{3,1},{4,6},{6,4},{5,7},{7,5},{8,10},{10,8},{9,1... | collective-permute-start | bytes 4718600 | tf_op jit(solution)/shard_map/ppermute | solution.py:37
  508.4 39.7 %collective-permute-start.27 = (bf16[1024,512]{1,0:T(8,128)(2,1)S(1)}, bf16[1024,512]{1,0:T(8,128)(2,1)S(1)}, u32[]{:S(2)}, u32[]{:S(2)}) collective-permute-start(bf16[1024,512]{1,0:T(8,128)(2,1)S(1)} %copy-done.16), channel_id=1, source_target_pairs={{0,4},{4,0},{1,5},{5,1},{2,6},{6,2},{3,7},{7,3},{8,12},{12,8},{9,1... | collective-permute-start | bytes 3145736 | tf_op jit(solution)/shard_map/ppermute | solution.py:37
  572.4 68.7 %reduce-scatter.12.cloned.1.call-start = ((), (), s32[]{:S(2)}) async-start(), calls=%async_computation.13 | async-start | bytes 1740800 | tf_op jit(solution)/shard_map/reduce_scatter | solution.py:564
  (54 other events, 695.8 us)
Sparse Core Ops, SparseCore 0:
  11.7 36.7 all-gather.5
  50.6 26.8 all-gather.9
  79.1 58.6 all-gather.7
  139.2 57.8 all-gather.11
  199.1 105.3 all-gather.13
  306.7 100.5 reduce-scatter.5
  425.0 54.3 reduce-scatter.7
  501.5 54.4 reduce-scatter.9
  572.5 24.7 reduce-scatter.13
  609.6 30.3 reduce-scatter.11

commit v3 on v2

--- a/solution.py
+++ b/solution.py
@@ -16,8 +16,8 @@
 F32 = jnp.float32
 BF16 = jnp.bfloat16
 SWAP = [(0, 1), (1, 0)]
-COST = {1: 1703, 2: 2220, 3: 2583, 4: 5630, 5: 1730, 6: 799, 7: 1730, 8: 799, 10: 1626, 11: 4002, 12: 3950, 13: 4338, 14: 3898, 15: 17158, 16: 2349, 17: 83025, 18: 2287, 19: 2349, 20: 1987, 21: 3821, 22: 1006, 23: 2556, 24: 1626, 25: 2143, 26: 1419, 27: 7981, 28: 2556, 29: 2066, 30: 826, 31: 26035, 32: 2066, 33: 17158, 34: 1523, 35: 1703, 36: 11984, 37: 53467, 38: 3616}
-SKIP = {131, 137, 143, 116, 123, 125}
+COST = {1: 1702, 2: 2220, 3: 2582, 4: 5630, 5: 1730, 6: 798, 7: 1730, 8: 798, 9: 1498, 10: 1626, 11: 4596, 12: 3950, 13: 4338, 14: 3898, 15: 798, 16: 2348, 17: 3872, 18: 798, 19: 2348, 20: 1986, 21: 3820, 22: 1006, 23: 2556, 24: 1626, 25: 2142, 26: 8118, 27: 127702, 28: 10228, 29: 33062, 31: 1626, 32: 1476, 34: 1522, 36: 1498, 37: 53466, 38: 3898, 39: 23246}
+SKIP = {133, 134, 103, 137, 139, 107, 142, 116, 150, 151, 120, 122}
 ROW_PAD = 16
 
 
@@ -260,6 +260,12 @@
 
 def add_kernel(first, second, out):
     out[...] = (first[...].astype(F32) + second[...].astype(F32)).astype(BF16)
+
+
+def total_kernel(near, came, gains, out):
+    depth = near.shape[0]
+    out[:depth] = (near[...] + came[...].astype(F32)).astype(BF16)
+    out[depth:] = gains[...]
 
 
 def expand_kernel(n_own, n_oth, u_own, u_oth, gate_in, inner, for_gate, for_up):
@@ -385,7 +391,7 @@
 def per_device(
     block_in, span_start, w_query, w_key, w_value, w_out, w_gate, w_up, w_down, gain_attn, gain_mlp, cotangent
 ):
-    x, y, c = (lax.axis_index(name) for name in ("fl", "th", "tl"))
+    z, x, y, c = (lax.axis_index(name) for name in ("fh", "fl", "th", "tl"))
     hi = lax.axis_size("fh")
     batch, rows, width = block_in.shape
     own_rows, half = batch * rows, width // 2
@@ -450,6 +456,9 @@
     sum_outs = [((1, half), F32, full_spec((1, half)))]
     hidden_out = ((all_rows, hidden), BF16, row_spec(tile, hidden))
 
+    def tiles_of(size, *values):
+        return [(v, row_spec(size, v.shape[1])) for v in values]
+
     def as_rows(value):
         return value.reshape(all_rows, value.shape[-1])
 
@@ -470,7 +479,7 @@
         kernel = weight_grad_kernel if came is None else weight_grad_add_kernel
         return call(step, kernel, [], value.shape[1] // part, ins, [out])[0]
 
-    def scatter_rows(step, kept, sent):
+    def scatter_rows(step, kept, sent, order=None, *others):
         cols = kept.shape[1]
         came = swap(sent, "tl")
         (passed,) = call(
@@ -481,14 +490,14 @@
             [(kept, row_spec(rows, cols, batch)), (came, row_spec(rows, cols, batch))],
             [((own_rows, cols), BF16, row_spec(rows, cols))],
         )
-        return kept, came, swap(passed, "th"), passed
+        across = after(order, passed, *others) if others else passed
+        return kept, came, swap(across, "th"), passed
 
     def terms(*scattered):
         return [(t, row_spec(rows, t.shape[1])) for part in scattered for t in part[:3]]
 
-    def stack_rows(step, low, order, *others):
-        beside, across = swap(low, "tl"), swap(low, "th")
-        across = after(order, across, *others)
+    def stack_rows(step, low, across, order, *others):
+        beside, across = swap(low, "tl"), after(order, across, *others)
         parts = (low, across, beside, swap(across, "tl"))
         return tuple(as_rows(v) for v in call(step, stack_kernel, [], batch, pieces(parts), spread_outs))
 
@@ -554,7 +563,7 @@
         [(quad + (width,), BF16, quad_spec(rows, width))],
     )
     seq_cot = as_rows(seq_cot)
-    seq_two = stack_rows(10, normed_two, 111, gate_w[1], seq_cot)
+    seq_two = stack_rows(10, normed_two, swap(normed_two, "th"), 111, gate_w[1], seq_cot)
     gate_pre = project(38, seq_two, gate_w, F32)
     inner, for_gate, for_up = call(
         11, expand_kernel, [], steps, tiles(*seq_two) + wholes(*up_w) + tiles(gate_pre), [hidden_out] * 3
@@ -586,32 +595,34 @@
     own_parts = expand_back(17, 0, after(116, after(115, gate_g, oth_parts[0]), normed_oth[3]))
     normed_own = scatter_rows(18, *own_parts)
     up_sent = weight_grad(19, seq_two[1], after(117, up_g, normed_own[3]))
+    gate_came = after(147, gate_came, up_sent)
+    gate_came = after(149, after(148, gate_came, normed_oth[2]), normed_own[2])
+    up_came = swap_x(after(122, up_sent, gate_came))
+    gate_total = weight_grad(23, seq_two[0], gate_g, gate_came)
+    grad_gate = reduce_z(gate_total)
     r_own, r_oth, attn_low, gain_s_own, gain_s_oth = call(
         20,
         functools.partial(middle_kernel, hi),
         [at],
         batch,
-        half_ins(after(118, h_own, up_sent), h_oth)
+        half_ins(after(120, after(118, h_own, up_sent), gate_total), h_oth)
         + terms(normed_own, normed_oth)
         + gain_in(gain_two)
         + [(cot_own, row_spec(rows, width))],
         half_outs + low_out + sum_outs * 2,
     )
-    gate_came = after(120, gate_came, attn_low)
-    up_came = swap_x(after(122, up_sent, gate_came))
-    gate_total = weight_grad(23, seq_two[0], gate_g, gate_came)
-    grad_gate = reduce_z(gate_total)
-    block_parts = project_back(21, after(119, inner, gate_total), down_w)
-
-    seq_attn = stack_rows(24, attn_low, 123, gate_total, block_parts[0])
-    block_terms = scatter_rows(22, after(124, block_parts[0], seq_attn[0]), block_parts[1])
+    block_parts = project_back(21, after(150, after(119, inner, attn_low), gate_total), down_w)
+
+    attn_far = swap(attn_low, "th")
+    up_came = after(127, after(126, up_came, block_parts[0]), grad_down)
+    up_total = weight_grad(28, seq_two[0], up_g, up_came)
+    grad_up = reduce_z(up_total)
+    seq_attn = stack_rows(24, attn_low, attn_far, 123, up_total)
+    block_terms = scatter_rows(22, block_parts[0], after(124, block_parts[1], seq_attn[0]))
     grad_mixed = project(25, seq_attn, out_w, BF16)
     out_sent = weight_grad(26, after(125, seq_attn[1], grad_mixed), mixed)
-    up_came = after(127, after(126, up_came, out_sent), grad_down)
     out_came = swap_x(after(128, out_sent, up_came))
-    up_total = weight_grad(28, seq_two[0], up_g, up_came)
-    grad_up = reduce_z(up_total)
-    grad_mixed = after(139, grad_mixed, up_total)
+    grad_mixed = after(156, after(139, grad_mixed, out_sent), block_terms[3])
     (qkv_g,) = call(
         27,
         functools.partial(attend_back_kernel, pairs),
@@ -643,36 +654,46 @@
         )
         return (kept, sent), sums / gain_one[which]
 
-    def gain_rows(one, two):
-        pair = jnp.concatenate([one.reshape(hi, 1, depth), two.reshape(hi, 1, depth)], axis=2)
-        return jnp.pad(pair, ((0, 0), (0, ROW_PAD - 1), (0, all_cols - 2 * depth)))
-
-    def with_gains(grad, one, two):
-        return jnp.concatenate([grad.reshape(hi, depth, all_cols), gain_rows(one, two)], axis=1)
-
-    oth_parts, oth_gain = project_gain(29, 1, qkv_g)
+    qkv_sent = weight_grad(31, seq_one[1], qkv_g)
+    qkv_came = swap_x(after(134, qkv_sent, out_came))
+    out_total = weight_grad(34, seq_attn[0], mixed, after(155, after(132, out_came, qkv_sent), qkv_g))
+    grad_out = reduce_z(out_total)
+    oth_parts, oth_gain = project_gain(29, 1, after(131, qkv_g, out_total))
     first_oth = scatter_rows(30, *oth_parts)
-    qkv_sent = with_gains(
-        weight_grad(31, seq_one[1], after(130, qkv_g, oth_parts[0])), oth_gain, gain_s_oth
-    ).astype(BF16)
-    qkv_came = swap_x(after(134, qkv_sent, out_came))
-    out_came = after(132, out_came, qkv_sent)
-    out_total = weight_grad(34, seq_attn[0], mixed, out_came)
-    own_parts, own_gain = project_gain(32, 0, after(143, after(142, after(131, qkv_g, qkv_sent), first_oth[3]), out_total))
+    own_parts, own_gain = project_gain(32, 0, after(143, after(142, qkv_g, first_oth[3]), out_total))
     first_own = scatter_rows(33, *own_parts)
-    grad_out = reduce_z(out_total)
-    qkv_total = with_gains(weight_grad(35, seq_one[0], qkv_g, kind=F32), own_gain, gain_s_own)
-    qkv_total = (qkv_total + after(135, qkv_came, grad_up).astype(F32)).astype(BF16)
-    grad_qkv = reduce_z(qkv_total.reshape(hi * (depth + ROW_PAD), all_cols)).astype(F32)
-    gain_sums = lax.psum(grad_qkv[depth, : 2 * depth], ("th", "tl"))
+    qkv_near = weight_grad(35, seq_one[0], after(133, qkv_g, first_own[3]), kind=F32)
+
+    def gain_pair(one, two):
+        return jnp.concatenate([one.reshape(hi, depth), two.reshape(hi, depth)], axis=1)
+
+    gain_own, gain_oth = gain_pair(own_gain, gain_s_own), gain_pair(oth_gain, gain_s_oth)
+    gain_both = jnp.stack([gain_own, gain_oth])
+    gain_both = gain_both + swap(gain_both, "tl")
+    gain_both = gain_both + swap(gain_both, "th")
+    gain_rows = gain_both[0] + swap_x(gain_both[1])
+    gain_rows = jnp.pad(gain_rows[:, None], ((0, 0), (0, ROW_PAD - 1), (0, all_cols - 2 * depth))).astype(BF16)
+    (qkv_total,) = call(
+        39,
+        total_kernel,
+        [],
+        hi,
+        tiles_of(depth, qkv_near, after(152, after(151, after(135, qkv_came, grad_up), first_oth[2]), first_own[2]))
+        + tiles_of(ROW_PAD, gain_rows.reshape(hi * ROW_PAD, all_cols)),
+        [((hi * (depth + ROW_PAD), all_cols), BF16, row_spec(depth + ROW_PAD, all_cols))],
+    )
+    grad_qkv = reduce_z(qkv_total).astype(F32)
+    gain_sums = grad_qkv[depth, : 2 * depth]
+    grad_qkv = grad_qkv[:depth]
     (block_out,) = call(
         36,
         functools.partial(block_out_kernel, hi),
         [at],
         batch,
-        half_ins(after(137, after(136, h_own, qkv_sent), grad_up), h_oth) + terms(block_terms),
+        half_ins(after(137, after(136, h_own, qkv_total), grad_up), h_oth) + terms(block_terms),
         whole_out,
     )
+
     (grad_in,) = call(
         37,
         functools.partial(grad_in_kernel, hi),
@@ -685,9 +706,9 @@
     return (
         block_out.reshape(block_in.shape),
         grad_in.reshape(block_in.shape),
-        grad_qkv[:depth, :q_cols],
-        grad_qkv[:depth, q_cols : q_cols + kv_cols],
-        grad_qkv[:depth, q_cols + kv_cols :],
+        grad_qkv[:, :q_cols],
+        grad_qkv[:, q_cols : q_cols + kv_cols],
+        grad_qkv[:, q_cols + kv_cols :],
         grad_out.astype(F32).T,
         grad_gate.astype(F32),
         grad_up.astype(F32),

time: 666 us -> 662 us (level)
  waiting for transfers between devices: 202 us -> 195 us
    ppermute x36 -> x39, waiting for transfers between devices: 166 us -> 158 us  [swap(): return lax.ppermute(value, axis, SWAP)]
    ppermute x36 -> x39, starting transfers between devices: 26.8 us -> 32.2 us  [swap(): return lax.ppermute(value, axis, SWAP)]
    pallas_call x38 -> x39, Pallas kernels: 353 us -> 357 us  [call(): pl.pallas_call(kernel, out_shape=[jax.ShapeDtypeStruct(shape, kind) for s...]
    unnamed x74 -> x75, local copies, waits for them, and re-layouts: 24.1 us -> 27.2 us
  transfers between devices with their start and end apart: 46 -> 49, of which waited for: 20 -> 23; matrix products, arithmetic and copies ran while one was open for 5% -> 4% of each run, Pallas kernels for 54% -> 54%
where the time goes in v3:
time: 662 us; the launch traced here: 656 us
  Pallas kernels  357 us (54%)
  waiting for transfers between devices  195 us (29%)
  local copies, waits for them, and re-layouts  41.8 us (6%)
  starting transfers between devices  33.8 us (5%)
  between operations  14.8 us (2%)
  other arithmetic  13.7 us (2%)
    pallas_call x39, Pallas kernels, call(): pl.pallas_call(kernel, out_shape=[jax.ShapeDtypeStruct(shape, kind) for s...  357 us
    ppermute x39, waiting for transfers between devices, swap(): return lax.ppermute(value, axis, SWAP)  158 us
    all_gather x5, waiting for transfers between devices, gather(): return lax.all_gather(part, 'fh', axis=0, tiled=True)  34.9 us
    ppermute x39, starting transfers between devices, swap(): return lax.ppermute(value, axis, SWAP)  32.2 us
    unnamed x75, local copies, waits for them, and re-layouts  27.2 us
  transfers between devices with their start and end apart: 49, of which 23 were waited for; matrix products, arithmetic and copies ran while one was open for 4% of the time, Pallas kernels for 54%

profile of v3, /device:TPU:0, one launch (start us, length us, event | category | flops | bytes accessed | tf_op | source)
XLA Modules:
  0.0 655.7 jit_solution(8485391316251426692)
XLA Ops:
  19.7 14.6 %collective-permute-done.3 = bf16[256,1408]{1,0:T(8,128)(2,1)S(1)} collective-permute-done((bf16[256,1408]{1,0:T(8,128)(2,1)S(1)}, bf16[256,1408]{1,0:T(8,128)(2,1)S(1)}, u32[]{:S(2)}, u32[]{:S(2)}) %collective-permute-start.3) | collective-permute-done | bytes 720928 | tf_op jit(solution)/shard_map/ppermute | solution.py:37
  35.5 13.0 %all-gather.6.cloned.1.call-done = bf16[1088,640]{1,0:T(8,128)(2,1)} async-done(((bf16[272,640]{1,0:T(8,128)(2,1)}), bf16[1088,640]{1,0:T(8,128)(2,1)}) %all-gather.6.cloned.1.call-update) | async-done | bytes 1392656 | tf_op jit(solution)/shard_map/all_gather | solution.py:410
  60.1 17.4 %all-gather.10.cloned.1.call-done.weight.w_own = bf16[1024,512]{1,0:T(8,128)(2,1)} async-done(((bf16[256,512]{1,0:T(8,128)(2,1)}), bf16[1024,512]{1,0:T(8,128)(2,1)}) %all-gather.10.cloned.1.call-update) | async-done | bytes 1048592 | tf_op jit(solution)/shard_map/all_gather | solution.py:410
  98.3 10.0 %shard_map.204 = f32[1536,640]{1,0:T(8,128)} custom-call(bf16[1536,1024]{1,0:T(8,128)(2,1)} %bitcast.71, bf16[1536,1024]{1,0:T(8,128)(2,1)} %bitcast.84, bf16[1024,640]{1,0:T(8,128)(2,1)} %bitcast.87, bf16[1024,640]{1,0:T(8,128)(2,1)} %bitcast.89), custom_call_target="tpu_custom_call" | custom-call | flops 774600000 | bytes 2582003 | tf_op jit(solution)/shard_map/pallas_call | solution.py:71
  108.3 21.5 %shard_map.205 = (bf16[4,3,128,512]{3,2,1,0:T(8,128)(2,1)}, bf16[4,3,128,128]{3,2,1,0:T(8,128)(2,1)}, bf16[4,3,128,512]{3,2,1,0:T(8,128)(2,1)}, f32[3,8,512]{2,1,0:T(8,128)}) custom-call(s32[3]{0:T(128)} %bitcast.119, f32[4,3,128,640]{3,2,1,0:T(8,128)} %bitcast.91, f32[512,128]{1,0:T(8,128)} %copy.57.cos, f32[512,128]{1,0:T(8,128)} %pad_maximum_fusion.1.sine, ...), custom_call_target="tpu_custom_call" | custom-call | flops 1688999936 | bytes 5630004 | tf_op jit(solution)/shard_map/pallas_call | solution.py:71
  162.5 9.5 %collective-permute-done.10.b2 = bf16[384,1024]{1,0:T(8,128)(2,1)S(1)} collective-permute-done((bf16[384,1024]{1,0:T(8,128)(2,1)S(1)}, bf16[384,1024]{1,0:T(8,128)(2,1)S(1)}, u32[]{:S(2)}, u32[]{:S(2)}) %collective-permute-start.10) | collective-permute-done | bytes 786464 | tf_op jit(solution)/shard_map/ppermute | solution.py:37
  171.9 16.3 %collective-permute-done.9.a2 = bf16[384,1024]{1,0:T(8,128)(2,1)S(1)} collective-permute-done((bf16[384,1024]{1,0:T(8,128)(2,1)}, bf16[384,1024]{1,0:T(8,128)(2,1)S(1)}, u32[]{:S(2)}, u32[]{:S(2)}) %collective-permute-start.9) | collective-permute-done | bytes 786464 | tf_op jit(solution)/shard_map/ppermute | solution.py:37
  210.5 20.6 %collective-permute-done.11.p1 = bf16[384,2048]{1,0:T(8,128)(2,1)} collective-permute-done((bf16[384,2048]{1,0:T(8,128)(2,1)}, bf16[384,2048]{1,0:T(8,128)(2,1)}, u32[]{:S(2)}, u32[]{:S(2)}) %collective-permute-start.11) | collective-permute-done | bytes 1572896 | tf_op jit(solution)/shard_map/ppermute | solution.py:37
  242.3 15.1 %shard_map.213.gate_in = f32[1536,1408]{1,0:T(8,128)} custom-call(bf16[1536,1024]{1,0:T(8,128)(2,1)} %bitcast.63, bf16[1536,1024]{1,0:T(8,128)(2,1)} %bitcast.67, bf16[1024,1408]{1,0:T(8,128)(2,1)} %all-gather.8.cloned.1.call-done.w_own.gate_w, bf16[1024,1408]{1,0:T(8,128)(2,1)} %copy-done.1), custom_call_target="tpu_custom_call" | custom-call | flops 1169400064 | bytes 3898038 | tf_op jit(solution)/shard_map/pallas_call | solution.py:71
  257.4 9.3 %collective-permute-done.17.u_oth.up_w = bf16[1024,1408]{1,0:T(8,128)(2,1)S(1)} collective-permute-done((bf16[1024,1408]{1,0:T(8,128)(2,1)}, bf16[1024,1408]{1,0:T(8,128)(2,1)S(1)}, u32[]{:S(2)}, u32[]{:S(2)}) %collective-permute-start.17) | collective-permute-done | bytes 2883616 | tf_op jit(solution)/shard_map/ppermute | solution.py:37
  268.4 17.8 %shard_map.214 = (bf16[1536,1408]{1,0:T(8,128)(2,1)}, bf16[1536,1408]{1,0:T(8,128)(2,1)}, bf16[1536,1408]{1,0:T(8,128)(2,1)}) custom-call(bf16[1536,1024]{1,0:T(8,128)(2,1)} %bitcast.64, bf16[1536,1024]{1,0:T(8,128)(2,1)} %bitcast.68, bf16[1024,1408]{1,0:T(8,128)(2,1)} %all-gather.12.cloned.1.call-done.u_own.up_w, bf16[1024,1408]{1,0:T(8,128)(2,1)} %copy-done.2, ...), custom_call_target="tpu_custom_call" | custom-call | flops 1378800000 | bytes 4596011 | tf_op jit(solution)/shard_map/pallas_call | solution.py:71
  286.1 14.8 %shard_map.215 = bf16[2048,1408]{1,0:T(8,128)(2,1)} custom-call(bf16[1536,2048]{1,0:T(8,128)(2,1)} %bitcast.61, bf16[1536,1408]{1,0:T(8,128)(2,1)} %get-tuple-element.128.grad.rows), custom_call_target="tpu_custom_call" | custom-call | flops 1184999936 | bytes 3950012 | tf_op jit(solution)/shard_map/pallas_call | solution.py:71
  304.6 17.2 %shard_map.216 = (bf16[1536,1408]{1,0:T(8,128)(2,1)}, bf16[1536,1408]{1,0:T(8,128)(2,1)}) custom-call(bf16[1536,2048]{1,0:T(8,128)(2,1)} %bitcast.62, bf16[2048,1408]{1,0:T(8,128)(2,1)} %all-gather.14.cloned.1.call-done.weight, bf16[1536,1408]{1,0:T(8,128)(2,1)} %get-tuple-element.114.for_gate, bf16[1536,1408]{1,0:T(8,128)(2,1)} %get-tuple-element.115.for_up), custom_call_target="tpu_custom_call" | custom-call | flops 1301400064 | bytes 4338013 | tf_op jit(solution)/shard_map/pallas_call | solution.py:71
  321.7 9.2 %shard_map.217 = bf16[1024,1408]{1,0:T(8,128)(2,1)} custom-call(bf16[1536,1024]{1,0:T(8,128)(2,1)} %bitcast.69, bf16[1536,1408]{1,0:T(8,128)(2,1)} %get-tuple-element.120.grad.gate_g), custom_call_target="tpu_custom_call" | custom-call | flops 704400000 | bytes 2348016 | tf_op jit(solution)/shard_map/pallas_call | solution.py:71
  332.4 15.6 %shard_map.218 = (bf16[768,1024]{1,0:T(8,128)(2,1)}, bf16[768,1024]{1,0:T(8,128)(2,1)}) custom-call(bf16[1536,1408]{1,0:T(8,128)(2,1)} %get-tuple-element.120.grad.gate_g, bf16[1536,1408]{1,0:T(8,128)(2,1)} %get-tuple-element.123.up_g.grad, bf16[1024,1408]{1,0:T(8,128)(2,1)} %copy-done.1, bf16[1024,1408]{1,0:T(8,128)(2,1)} %copy-done.2), custom_call_target="tpu_custom_call" | custom-call | flops 1169400064 | bytes 3898014 | tf_op jit(solution)/shard_map/pallas_call | solution.py:71
  348.0 15.7 %shard_map.219 = (bf16[768,1024]{1,0:T(8,128)(2,1)}, bf16[768,1024]{1,0:T(8,128)(2,1)}) custom-call(bf16[1536,1408]{1,0:T(8,128)(2,1)} %get-tuple-element.120.grad.gate_g, bf16[1536,1408]{1,0:T(8,128)(2,1)} %get-tuple-element.123.up_g.grad, bf16[1024,1408]{1,0:T(8,128)(2,1)} %all-gather.8.cloned.1.call-done.w_own.gate_w, ...), custom_call_target="tpu_custom_call" | custom-call | flops 1161600000 | bytes 3872017 | tf_op jit(solution)/shard_map/pallas_call | solution.py:71
  374.8 9.1 %shard_map.221 = bf16[1024,1408]{1,0:T(8,128)(2,1)} custom-call(bf16[1536,1024]{1,0:T(8,128)(2,1)} %bitcast.70, bf16[1536,1408]{1,0:T(8,128)(2,1)} %get-tuple-element.123.up_g.grad), custom_call_target="tpu_custom_call" | custom-call | flops 704400000 | bytes 2348019 | tf_op jit(solution)/shard_map/pallas_call | solution.py:71
  384.3 12.1 %collective-permute-done.29.came = bf16[1024,1408]{1,0:T(8,128)(2,1)S(1)} collective-permute-done((bf16[1024,1408]{1,0:T(8,128)(2,1)}, bf16[1024,1408]{1,0:T(8,128)(2,1)S(1)}, u32[]{:S(2)}, u32[]{:S(2)}) %collective-permute-start.29) | collective-permute-done | bytes 2883616 | tf_op jit(solution)/shard_map/ppermute | solution.py:37
  405.1 9.9 %shard_map.231 = bf16[1024,1408]{1,0:T(8,128)(2,1)} custom-call(bf16[1536,1024]{1,0:T(8,128)(2,1)} %bitcast.65, bf16[1536,1408]{1,0:T(8,128)(2,1)} %get-tuple-element.120.grad.gate_g, bf16[1024,1408]{1,0:T(8,128)(2,1)} %copy-done.8), custom_call_target="tpu_custom_call" | custom-call | flops 766800000 | bytes 2556023 | tf_op jit(solution)/shard_map/pallas_call | solution.py:71
  424.5 16.1 %shard_map.224 = (bf16[768,2048]{1,0:T(8,128)(2,1)}, bf16[768,2048]{1,0:T(8,128)(2,1)}) custom-call(bf16[1536,1408]{1,0:T(8,128)(2,1)} %get-tuple-element.128.grad.rows, bf16[2048,1408]{1,0:T(8,128)(2,1)} %all-gather.14.cloned.1.call-done.weight), custom_call_target="tpu_custom_call" | custom-call | flops 1146000000 | bytes 3820021 | tf_op jit(solution)/shard_map/pallas_call | solution.py:71
  440.6 16.7 %collective-permute-done.23.came = bf16[1024,1408]{1,0:T(8,128)(2,1)S(1)} collective-permute-done((bf16[1024,1408]{1,0:T(8,128)(2,1)}, bf16[1024,1408]{1,0:T(8,128)(2,1)S(1)}, u32[]{:S(2)}, u32[]{:S(2)}) %collective-permute-start.23) | collective-permute-done | bytes 2883616 | tf_op jit(solution)/shard_map/ppermute | solution.py:37
  458.9 9.9 %shard_map.225 = bf16[1024,1408]{1,0:T(8,128)(2,1)} custom-call(bf16[1536,1024]{1,0:T(8,128)(2,1)} %bitcast.66, bf16[1536,1408]{1,0:T(8,128)(2,1)} %get-tuple-element.123.up_g.grad, bf16[1024,1408]{1,0:T(8,128)(2,1)} %copy-done.7), custom_call_target="tpu_custom_call" | custom-call | flops 3068400128 | bytes 10228028 | tf_op jit(solution)/shard_map/pallas_call | solution.py:71
  502.4 30.9 %shard_map.229 = bf16[4,3,128,640]{3,2,1,0:T(8,128)(2,1)} custom-call(s32[3]{0:T(128)} %bitcast.120, bf16[4,3,128,512]{3,2,1,0:T(8,128)(2,1)} %get-tuple-element.103.query_in, bf16[4,3,128,128]{3,2,1,0:T(8,128)(2,1)} %get-tuple-element.104.kv_in, bf16[4,3,128,512]{3,2,1,0:T(8,128)(2,1)} %bitcast.97, f32[3,8,512]{2,1,0:T(8,128)} %get-tuple-element.138.lse, ...), custom_call_target="tpu_custom_call" | custom-call | flops 38310600704 | bytes 127702024 | tf_op jit(solution)/shard_map/pallas_call | solution.py:71
  577.4 18.2 %collective-permute-done.34 = f32[2,4,512]{2,1,0:T(4,128)S(1)} collective-permute-done((f32[2,4,512]{2,1,0:T(4,128)S(1)}, f32[2,4,512]{2,1,0:T(4,128)S(1)}, u32[]{:S(2)}, u32[]{:S(2)}) %collective-permute-start.34) | collective-permute-done | bytes 16416 | tf_op jit(solution)/shard_map/ppermute | solution.py:37
  (245 shorter events, 280.4 us)
Async XLA Ops:
  7.2 41.3 %all-gather.6.cloned.1.call-start = ((), (), s32[]{:S(2)}) async-start(), calls=%async_computation.5 | async-start | bytes 1740800 | tf_op jit(solution)/shard_map/all_gather | solution.py:410
  11.5 66.0 %all-gather.10.cloned.1.call-start = ((), (), s32[]{:S(2)}) async-start(), calls=%async_computation.7 | async-start | bytes 1310720 | tf_op jit(solution)/shard_map/all_gather | solution.py:410
  13.4 124.4 %all-gather.8.cloned.1.call-start = ((), (), s32[]{:S(2)}) async-start(), calls=%async_computation.6 | async-start | bytes 3604480 | tf_op jit(solution)/shard_map/all_gather | solution.py:410
  14.2 183.0 %all-gather.12.cloned.1.call-start = ((), (), s32[]{:S(2)}) async-start(), calls=%async_computation.8 | async-start | bytes 3604480 | tf_op jit(solution)/shard_map/all_gather | solution.py:410
  14.7 289.8 %all-gather.14.cloned.1.call-start = ((), (), s32[]{:S(2)}) async-start(), calls=%async_computation.9 | async-start | bytes 7208960 | tf_op jit(solution)/shard_map/all_gather | solution.py:410
  50.0 39.7 %collective-permute-start.1 = (bf16[384,2048]{1,0:T(8,128)(2,1)S(1)}, bf16[384,2048]{1,0:T(8,128)(2,1)}, u32[]{:S(2)}, u32[]{:S(2)}) collective-permute-start(bf16[384,2048]{1,0:T(8,128)(2,1)S(1)} %bitcast.100), channel_id=1, source_target_pairs={{0,1},{1,0},{2,3},{3,2},{4,5},{5,4},{6,7},{7,6},{8,9},{9,8},{10,11... | collective-permute-start | bytes 4718600 | tf_op jit(solution)/shard_map/ppermute | solution.py:37
  54.1 54.2 %collective-permute-start.5 = (bf16[384,2048]{1,0:T(8,128)(2,1)}, bf16[384,2048]{1,0:T(8,128)(2,1)}, u32[]{:S(2)}, u32[]{:S(2)}) collective-permute-start(bf16[384,2048]{1,0:T(8,128)(2,1)} %bitcast.10.p0.upstream), channel_id=1, source_target_pairs={{0,2},{2,0},{1,3},{3,1},{4,6},{6,4},{5,7},{7,5},{8,10},{10,8},{9,1... | collective-permute-start | bytes 4718600 | tf_op jit(solution)/shard_map/ppermute | solution.py:37
  59.5 397.8 %reduce-scatter.6.cloned.1.call-start = ((), (), s32[]{:S(2)}) async-start(), calls=%async_computation.10 | async-start | bytes 7208960 | tf_op jit(solution)/shard_map/reduce_scatter | solution.py:573
  80.4 49.4 %collective-permute-start.6 = (bf16[1024,512]{1,0:T(8,128)(2,1)}, bf16[1024,512]{1,0:T(8,128)(2,1)S(1)}, u32[]{:S(2)}, u32[]{:S(2)}) collective-permute-start(bf16[1024,512]{1,0:T(8,128)(2,1)} %all-gather.10.cloned.1.call-done.weight.w_own), channel_id=1, source_target_pairs={{0,4},{4,0},{1,5},{5,1},{2,6},{6,2},{3,7},{7,3},{8,12},{12,8},{9,1... | collective-permute-start | bytes 3145736 | tf_op jit(solution)/shard_map/ppermute | solution.py:37
  137.8 64.8 %collective-permute-start.12 = (bf16[1024,1408]{1,0:T(8,128)(2,1)}, bf16[1024,1408]{1,0:T(8,128)(2,1)S(1)}, u32[]{:S(2)}, u32[]{:S(2)}) collective-permute-start(bf16[1024,1408]{1,0:T(8,128)(2,1)} %all-gather.8.cloned.1.call-done.w_own.gate_w), channel_id=1, source_target_pairs={{0,4},{4,0},{1,5},{5,1},{2,6},{6,2},{3,7},{7,3},{8,12},{12,8},{9,1... | collective-permute-start | bytes 8650760 | tf_op jit(solution)/shard_map/ppermute | solution.py:37
  160.7 42.9 %collective-permute-start.13 = (bf16[384,2048]{1,0:T(8,128)(2,1)}, bf16[384,2048]{1,0:T(8,128)(2,1)}, u32[]{:S(2)}, u32[]{:S(2)}) collective-permute-start(bf16[384,2048]{1,0:T(8,128)(2,1)} %bitcast.10.p0.upstream), channel_id=1, source_target_pairs={{0,1},{1,0},{2,3},{3,2},{4,5},{5,4},{6,7},{7,6},{8,9},{9,8},{10,11... | collective-permute-start | bytes 4718600 | tf_op jit(solution)/shard_map/ppermute | solution.py:37
  160.8 42.9 %collective-permute-start.14 = (bf16[384,2048]{1,0:T(8,128)(2,1)}, bf16[384,2048]{1,0:T(8,128)(2,1)}, u32[]{:S(2)}, u32[]{:S(2)}) collective-permute-start(bf16[384,2048]{1,0:T(8,128)(2,1)} %collective-permute-done.5.p1), channel_id=1, source_target_pairs={{0,1},{1,0},{2,3},{3,2},{4,5},{5,4},{6,7},{7,6},{8,9},{9,8},{10,11... | collective-permute-start | bytes 4718600 | tf_op jit(solution)/shard_map/ppermute | solution.py:37
  202.7 64.1 %collective-permute-start.17 = (bf16[1024,1408]{1,0:T(8,128)(2,1)}, bf16[1024,1408]{1,0:T(8,128)(2,1)S(1)}, u32[]{:S(2)}, u32[]{:S(2)}) collective-permute-start(bf16[1024,1408]{1,0:T(8,128)(2,1)} %all-gather.12.cloned.1.call-done.u_own.up_w), channel_id=1, source_target_pairs={{0,4},{4,0},{1,5},{5,1},{2,6},{6,2},{3,7},{7,3},{8,12},{12,8},{9,1... | collective-permute-start | bytes 8650760 | tf_op jit(solution)/shard_map/ppermute | solution.py:37
  301.0 236.7 %reduce-scatter.8.cloned.1.call-start = ((), (), s32[]{:S(2)}) async-start(), calls=%async_computation.11 | async-start | bytes 3604480 | tf_op jit(solution)/shard_map/reduce_scatter | solution.py:573
  330.9 65.6 %collective-permute-start.29 = (bf16[1024,1408]{1,0:T(8,128)(2,1)}, bf16[1024,1408]{1,0:T(8,128)(2,1)S(1)}, u32[]{:S(2)}, u32[]{:S(2)}) collective-permute-start(bf16[1024,1408]{1,0:T(8,128)(2,1)} %shard_map.217), channel_id=1, source_target_pairs={{0,4},{4,0},{1,5},{5,1},{2,6},{6,2},{3,7},{7,3},{8,12},{12,8},{9,1... | collective-permute-start | bytes 8650760 | tf_op jit(solution)/shard_map/ppermute | solution.py:37
  383.8 73.5 %collective-permute-start.23 = (bf16[1024,1408]{1,0:T(8,128)(2,1)}, bf16[1024,1408]{1,0:T(8,128)(2,1)S(1)}, u32[]{:S(2)}, u32[]{:S(2)}) collective-permute-start(bf16[1024,1408]{1,0:T(8,128)(2,1)} %shard_map.221), channel_id=1, source_target_pairs={{0,4},{4,0},{1,5},{5,1},{2,6},{6,2},{3,7},{7,3},{8,12},{12,8},{9,1... | collective-permute-start | bytes 8650760 | tf_op jit(solution)/shard_map/ppermute | solution.py:37
  415.0 190.8 %reduce-scatter.10.cloned.1.call-start = ((), (), s32[]{:S(2)}) async-start(), calls=%async_computation.12 | async-start | bytes 3604480 | tf_op jit(solution)/shard_map/reduce_scatter | solution.py:573
  423.0 45.8 %collective-permute-start.22 = (bf16[384,2048]{1,0:T(8,128)(2,1)}, bf16[384,2048]{1,0:T(8,128)(2,1)}, u32[]{:S(2)}, u32[]{:S(2)}) collective-permute-start(bf16[384,2048]{1,0:T(8,128)(2,1)} %get-tuple-element.127.p0), channel_id=1, source_target_pairs={{0,2},{2,0},{1,3},{3,1},{4,6},{6,4},{5,7},{7,5},{8,10},{10,8},{9,1... | collective-permute-start | bytes 4718600 | tf_op jit(solution)/shard_map/ppermute | solution.py:37
  424.5 44.2 %collective-permute-start.24 = (bf16[384,2048]{1,0:T(8,128)(2,1)}, bf16[384,2048]{1,0:T(8,128)(2,1)}, u32[]{:S(2)}, u32[]{:S(2)}) collective-permute-start(bf16[384,2048]{1,0:T(8,128)(2,1)} %get-tuple-element.127.p0), channel_id=1, source_target_pairs={{0,1},{1,0},{2,3},{3,2},{4,5},{5,4},{6,7},{7,6},{8,9},{9,8},{10,11... | collective-permute-start | bytes 4718600 | tf_op jit(solution)/shard_map/ppermute | solution.py:37
  479.9 142.0 %reduce-scatter.14.cloned.1.call-start = ((), (), s32[]{:S(2)}) async-start(), calls=%async_computation.14 | async-start | bytes 1310720 | tf_op jit(solution)/shard_map/reduce_scatter | solution.py:573
  494.0 39.2 %collective-permute-start.27 = (bf16[1024,512]{1,0:T(8,128)(2,1)}, bf16[1024,512]{1,0:T(8,128)(2,1)}, u32[]{:S(2)}, u32[]{:S(2)}) collective-permute-start(bf16[1024,512]{1,0:T(8,128)(2,1)} %shard_map.230), channel_id=1, source_target_pairs={{0,4},{4,0},{1,5},{5,1},{2,6},{6,2},{3,7},{7,3},{8,12},{12,8},{9,1... | collective-permute-start | bytes 3145736 | tf_op jit(solution)/shard_map/ppermute | solution.py:37
  500.8 36.8 %collective-permute-start.28 = (bf16[384,2048]{1,0:T(8,128)(2,1)}, bf16[384,2048]{1,0:T(8,128)(2,1)}, u32[]{:S(2)}, u32[]{:S(2)}) collective-permute-start(bf16[384,2048]{1,0:T(8,128)(2,1)} %shard_map.228), channel_id=1, source_target_pairs={{0,2},{2,0},{1,3},{3,1},{4,6},{6,4},{5,7},{7,5},{8,10},{10,8},{9,1... | collective-permute-start | bytes 4718600 | tf_op jit(solution)/shard_map/ppermute | solution.py:37
  560.2 45.6 %collective-permute-start.30 = (bf16[1024,640]{1,0:T(8,128)(2,1)S(1)}, bf16[1024,640]{1,0:T(8,128)(2,1)}, u32[]{:S(2)}, u32[]{:S(2)}) collective-permute-start(bf16[1024,640]{1,0:T(8,128)(2,1)S(1)} %copy-done.18), channel_id=1, source_target_pairs={{0,4},{4,0},{1,5},{5,1},{2,6},{6,2},{3,7},{7,3},{8,12},{12,8},{9,1... | collective-permute-start | bytes 3932168 | tf_op jit(solution)/shard_map/ppermute | solution.py:37
  561.0 82.1 %reduce-scatter.12.cloned.1.call-start = ((), (), s32[]{:S(2)}) async-start(), calls=%async_computation.13 | async-start | bytes 1740800 | tf_op jit(solution)/shard_map/reduce_scatter | solution.py:573
  (57 other events, 662.7 us)
Sparse Core Ops, SparseCore 0:
  11.7 36.7 all-gather.5
  50.6 26.8 all-gather.9
  79.1 58.6 all-gather.7
  139.2 57.8 all-gather.11
  199.1 105.3 all-gather.13
  306.7 100.5 reduce-scatter.5
  415.2 53.4 reduce-scatter.7
  480.1 54.4 reduce-scatter.9
  561.1 25.2 reduce-scatter.13
  610.0 30.7 reduce-scatter.11

commit v4 on v3

--- a/solution.py
+++ b/solution.py
@@ -17,7 +17,7 @@
 BF16 = jnp.bfloat16
 SWAP = [(0, 1), (1, 0)]
 COST = {1: 1702, 2: 2220, 3: 2582, 4: 5630, 5: 1730, 6: 798, 7: 1730, 8: 798, 9: 1498, 10: 1626, 11: 4596, 12: 3950, 13: 4338, 14: 3898, 15: 798, 16: 2348, 17: 3872, 18: 798, 19: 2348, 20: 1986, 21: 3820, 22: 1006, 23: 2556, 24: 1626, 25: 2142, 26: 8118, 27: 127702, 28: 10228, 29: 33062, 31: 1626, 32: 1476, 34: 1522, 36: 1498, 37: 53466, 38: 3898, 39: 23246}
-SKIP = {133, 134, 103, 137, 139, 107, 142, 116, 150, 151, 120, 122}
+SKIP = {133, 134, 103, 137, 107, 139, 142, 116, 150, 151, 120, 122, 158, 159}
 ROW_PAD = 16
 
 
@@ -341,22 +341,31 @@
     lax.fori_loop(0, pairs, pair_step, 0)
 
 
+def with_terms(rows, number):
+    high = number.astype(BF16).astype(F32)
+    middle = (number - high).astype(BF16).astype(F32)
+    low = number - high - middle
+    line = lax.broadcasted_iota(jnp.int32, (16, number.shape[1]), 0)
+    terms = jnp.where(line == 0, high, jnp.where(line == 1, middle, jnp.where(line == 2, low, 0.0)))
+    rest = jnp.zeros((HD - 16, number.shape[1]), BF16)
+    return jnp.concatenate([rows.astype(BF16), terms.astype(BF16), rest], axis=0)
+
+
 def attend_back_kernel(
-    pairs, span, query_in, kv_in, grad_in, lse, cos, sine, key_at, query_at, out, bias, key_s, key_t, val_s, key_g, val_g
+    pairs, span, query_in, kv_in, grad_in, mixed_in, lse, cos, sine, key_at, query_at, out, bias, key_s, key_t, val_s, key_g, val_g
 ):
     length = cos.shape[0]
+    scale = HD**-0.5
     set_bias(bias, key_at, query_at, span[pl.program_id(0)])
     kv = kv_in[:, 0].reshape(length, PAIR).astype(F32)
     low = low_lanes(kv.shape)
+    lane = lax.broadcasted_iota(jnp.int32, kv.shape, 1)
+    ones = jnp.where(lane < HD + 3, 1.0, 0.0)
     key_even = jnp.where(low, kv, 0.0)
-    key_odd = pltpu.roll(key_even, HD, 1)
-    val_odd = jnp.where(low, 0.0, kv)
-    key_s[0] = key_even.astype(BF16)
-    key_s[1] = key_odd.astype(BF16)
+    key_s[...] = jnp.where(low, kv, ones).astype(BF16)
+    val_s[...] = jnp.where(low, pltpu.roll(kv, HD, 1) * scale, ones).astype(BF16)
     key_t[0] = key_even.T.astype(BF16)
-    key_t[1] = key_odd.T.astype(BF16)
-    val_s[0] = pltpu.roll(val_odd, HD, 1).astype(BF16)
-    val_s[1] = val_odd.astype(BF16)
+    key_t[1] = pltpu.roll(key_even, HD, 1).T.astype(BF16)
     key_g[...] = jnp.zeros_like(key_g)
     val_g[...] = jnp.zeros_like(val_g)
 
@@ -364,16 +373,19 @@
         cols = pl.ds(pl.multiple_of(j * PAIR, PAIR), PAIR)
         query = query_in[:, 0, :, cols].reshape(length, PAIR)
         grad = grad_in[:, 0, :, cols].reshape(length, PAIR)
-        query_t = (query.astype(F32) * HD**-0.5).T.astype(BF16)
-        grad_t = grad.astype(F32).T.astype(BF16)
+        mixed = mixed_in[:, 0, :, cols].reshape(length, PAIR)
+        query_t = (query.astype(F32) * scale).T
+        grad_t = grad.astype(F32).T
+        product = grad_t * mixed.astype(F32).T
         query_g = jnp.zeros((PAIR, length), F32)
         for k in range(2):
-            scores = dot(key_s[k], query_t) + bias[...]
-            weight = jnp.exp(scores - lse[0, pl.ds(2 * j + k, 1), :])
-            weight_g = dot(val_s[k], grad_t)
+            part = slice(k * HD, (k + 1) * HD)
+            delta = jnp.sum(product[part], axis=0, keepdims=True) * scale
+            scores = dot(key_s[...], with_terms(query_t[part], -lse[0, pl.ds(2 * j + k, 1), :]))
+            weight = jnp.exp(scores + bias[...])
+            weight_g = dot(val_s[...], with_terms(grad_t[part], -delta))
             val_g[k] += dot(weight.astype(BF16), grad)
-            delta = jnp.sum(weight * weight_g, axis=0, keepdims=True)
-            score_g = (HD**-0.5 * (weight * (weight_g - delta))).astype(BF16)
+            score_g = (weight * weight_g).astype(BF16)
             key_g[k] += dot(score_g, query)
             query_g += dot(key_t[k], score_g)
         value = query_g.T
@@ -595,7 +607,7 @@
     own_parts = expand_back(17, 0, after(116, after(115, gate_g, oth_parts[0]), normed_oth[3]))
     normed_own = scatter_rows(18, *own_parts)
     up_sent = weight_grad(19, seq_two[1], after(117, up_g, normed_own[3]))
-    gate_came = after(147, gate_came, up_sent)
+    gate_came = after(158, after(147, gate_came, up_sent), oth_parts[0], own_parts[0])
     gate_came = after(149, after(148, gate_came, normed_oth[2]), normed_own[2])
     up_came = swap_x(after(122, up_sent, gate_came))
     gate_total = weight_grad(23, seq_two[0], gate_g, gate_came)
@@ -618,7 +630,7 @@
     up_total = weight_grad(28, seq_two[0], up_g, up_came)
     grad_up = reduce_z(up_total)
     seq_attn = stack_rows(24, attn_low, attn_far, 123, up_total)
-    block_terms = scatter_rows(22, block_parts[0], after(124, block_parts[1], seq_attn[0]))
+    block_terms = scatter_rows(22, block_parts[0], after(124, block_parts[1], seq_attn[0]), 160, attn_far)
     grad_mixed = project(25, seq_attn, out_w, BF16)
     out_sent = weight_grad(26, after(125, seq_attn[1], grad_mixed), mixed)
     out_came = swap_x(after(128, out_sent, up_came))
@@ -632,15 +644,16 @@
             (query_rot, q_spec),
             (kv_rot, pair_spec),
             (grad_mixed.reshape(quad + (q_cols,)), q_spec),
+            (mixed.reshape(quad + (q_cols,)), q_spec),
             (lse, lse_spec),
             *tables,
         ],
         [(quad + (all_cols,), BF16, quad_spec(rows, all_cols))],
         [
             pltpu.VMEM((length, length), F32),
-            pltpu.VMEM((2, length, PAIR), BF16),
+            pltpu.VMEM((length, PAIR), BF16),
             pltpu.VMEM((2, PAIR, length), BF16),
-            pltpu.VMEM((2, length, PAIR), BF16),
+            pltpu.VMEM((length, PAIR), BF16),
             pltpu.VMEM((2, length, PAIR), F32),
             pltpu.VMEM((2, length, PAIR), F32),
         ],
@@ -654,7 +667,7 @@
         )
         return (kept, sent), sums / gain_one[which]
 
-    qkv_sent = weight_grad(31, seq_one[1], qkv_g)
+    qkv_sent = weight_grad(31, seq_one[1], after(159, qkv_g, out_sent))
     qkv_came = swap_x(after(134, qkv_sent, out_came))
     out_total = weight_grad(34, seq_attn[0], mixed, after(155, after(132, out_came, qkv_sent), qkv_g))
     grad_out = reduce_z(out_total)
@@ -670,7 +683,6 @@
     gain_own, gain_oth = gain_pair(own_gain, gain_s_own), gain_pair(oth_gain, gain_s_oth)
     gain_both = jnp.stack([gain_own, gain_oth])
     gain_both = gain_both + swap(gain_both, "tl")
-    gain_both = gain_both + swap(gain_both, "th")
     gain_rows = gain_both[0] + swap_x(gain_both[1])
     gain_rows = jnp.pad(gain_rows[:, None], ((0, 0), (0, ROW_PAD - 1), (0, all_cols - 2 * depth))).astype(BF16)
     (qkv_total,) = call(
@@ -684,6 +696,7 @@
     )
     grad_qkv = reduce_z(qkv_total).astype(F32)
     gain_sums = grad_qkv[depth, : 2 * depth]
+    gain_sums = gain_sums + swap(gain_sums, "th")
     grad_qkv = grad_qkv[:depth]
     (block_out,) = call(
         36,

time: 662 us -> 653 us (0.986)
  transfers between devices with their start and end apart: 49 -> 49, of which waited for: 23 -> 26; matrix products, arithmetic and copies ran while one was open for 4% -> 5% of each run, Pallas kernels for 54% -> 55%
where the time goes in v4:
time: 653 us; the launch traced here: 647 us
  Pallas kernels  353 us (54%)
  waiting for transfers between devices  189 us (29%)
  local copies, waits for them, and re-layouts  41.8 us (6%)
  starting transfers between devices  34.7 us (5%)
  between operations  14.8 us (2%)
  other arithmetic  13.7 us (2%)
    pallas_call x39, Pallas kernels, call(): pl.pallas_call(kernel, out_shape=[jax.ShapeDtypeStruct(shape, kind) for s...  353 us
    ppermute x39, waiting for transfers between devices, swap(): return lax.ppermute(value, axis, SWAP)  152 us
    all_gather x5, waiting for transfers between devices, gather(): return lax.all_gather(part, 'fh', axis=0, tiled=True)  34.9 us
    ppermute x39, starting transfers between devices, swap(): return lax.ppermute(value, axis, SWAP)  33.2 us
    unnamed x75, local copies, waits for them, and re-layouts  27.2 us
  transfers between devices with their start and end apart: 49, of which 26 were waited for; matrix products, arithmetic and copies ran while one was open for 5% of the time, Pallas kernels for 55%

profile of v4, /device:TPU:0, one launch (start us, length us, event | category | flops | bytes accessed | tf_op | source)
XLA Modules:
  0.0 646.6 jit_solution(16623470789942600547)
XLA Ops:
  19.7 14.6 %collective-permute-done.3 = bf16[256,1408]{1,0:T(8,128)(2,1)S(1)} collective-permute-done((bf16[256,1408]{1,0:T(8,128)(2,1)S(1)}, bf16[256,1408]{1,0:T(8,128)(2,1)S(1)}, u32[]{:S(2)}, u32[]{:S(2)}) %collective-permute-start.3) | collective-permute-done | bytes 720928 | tf_op jit(solution)/shard_map/ppermute | solution.py:37
  35.5 13.0 %all-gather.6.cloned.1.call-done = bf16[1088,640]{1,0:T(8,128)(2,1)} async-done(((bf16[272,640]{1,0:T(8,128)(2,1)}), bf16[1088,640]{1,0:T(8,128)(2,1)}) %all-gather.6.cloned.1.call-update) | async-done | bytes 1392656 | tf_op jit(solution)/shard_map/all_gather | solution.py:422
  60.1 17.4 %all-gather.10.cloned.1.call-done.weight.w_own = bf16[1024,512]{1,0:T(8,128)(2,1)} async-done(((bf16[256,512]{1,0:T(8,128)(2,1)}), bf16[1024,512]{1,0:T(8,128)(2,1)}) %all-gather.10.cloned.1.call-update) | async-done | bytes 1048592 | tf_op jit(solution)/shard_map/all_gather | solution.py:422
  89.6 8.7 %shard_map.203 = (bf16[4,3,128,1024]{3,2,1,0:T(8,128)(2,1)}, bf16[4,3,128,1024]{3,2,1,0:T(8,128)(2,1)}, bf16[384,1024]{1,0:T(8,128)(2,1)}, bf16[384,1024]{1,0:T(8,128)(2,1)}) custom-call(s32[1]{0:T(128)} %bitcast.at, bf16[384,2048]{1,0:T(8,128)(2,1)} %bitcast.97, bf16[384,2048]{1,0:T(8,128)(2,1)} %collective-permute-done.p1, ...), custom_call_target="tpu_custom_call" | custom-call | flops 666000000 | bytes 2220002 | tf_op jit(solution)/shard_map/pallas_call | solution.py:71
  98.3 10.0 %shard_map.204 = f32[1536,640]{1,0:T(8,128)} custom-call(bf16[1536,1024]{1,0:T(8,128)(2,1)} %bitcast.70, bf16[1536,1024]{1,0:T(8,128)(2,1)} %bitcast.83, bf16[1024,640]{1,0:T(8,128)(2,1)} %bitcast.86, bf16[1024,640]{1,0:T(8,128)(2,1)} %bitcast.88), custom_call_target="tpu_custom_call" | custom-call | flops 774600000 | bytes 2582003 | tf_op jit(solution)/shard_map/pallas_call | solution.py:71
  108.3 21.5 %shard_map.205 = (bf16[4,3,128,512]{3,2,1,0:T(8,128)(2,1)}, bf16[4,3,128,128]{3,2,1,0:T(8,128)(2,1)}, bf16[4,3,128,512]{3,2,1,0:T(8,128)(2,1)}, f32[3,8,512]{2,1,0:T(8,128)}) custom-call(s32[3]{0:T(128)} %bitcast.118, f32[4,3,128,640]{3,2,1,0:T(8,128)} %bitcast.90, f32[512,128]{1,0:T(8,128)} %copy.57.cos, f32[512,128]{1,0:T(8,128)} %pad_maximum_fusion.1.sine, ...), custom_call_target="tpu_custom_call" | custom-call | flops 1688999936 | bytes 5630004 | tf_op jit(solution)/shard_map/pallas_call | solution.py:71
  162.5 9.5 %collective-permute-done.10.b2 = bf16[384,1024]{1,0:T(8,128)(2,1)S(1)} collective-permute-done((bf16[384,1024]{1,0:T(8,128)(2,1)S(1)}, bf16[384,1024]{1,0:T(8,128)(2,1)S(1)}, u32[]{:S(2)}, u32[]{:S(2)}) %collective-permute-start.10) | collective-permute-done | bytes 786464 | tf_op jit(solution)/shard_map/ppermute | solution.py:37
  171.9 16.3 %collective-permute-done.9.a2 = bf16[384,1024]{1,0:T(8,128)(2,1)S(1)} collective-permute-done((bf16[384,1024]{1,0:T(8,128)(2,1)}, bf16[384,1024]{1,0:T(8,128)(2,1)S(1)}, u32[]{:S(2)}, u32[]{:S(2)}) %collective-permute-start.9) | collective-permute-done | bytes 786464 | tf_op jit(solution)/shard_map/ppermute | solution.py:37
  210.5 20.6 %collective-permute-done.11.p1 = bf16[384,2048]{1,0:T(8,128)(2,1)} collective-permute-done((bf16[384,2048]{1,0:T(8,128)(2,1)}, bf16[384,2048]{1,0:T(8,128)(2,1)}, u32[]{:S(2)}, u32[]{:S(2)}) %collective-permute-start.11) | collective-permute-done | bytes 1572896 | tf_op jit(solution)/shard_map/ppermute | solution.py:37
  242.3 15.1 %shard_map.213.gate_in = f32[1536,1408]{1,0:T(8,128)} custom-call(bf16[1536,1024]{1,0:T(8,128)(2,1)} %bitcast.62, bf16[1536,1024]{1,0:T(8,128)(2,1)} %bitcast.66, bf16[1024,1408]{1,0:T(8,128)(2,1)} %all-gather.8.cloned.1.call-done.w_own.gate_w, bf16[1024,1408]{1,0:T(8,128)(2,1)} %copy-done.1), custom_call_target="tpu_custom_call" | custom-call | flops 1169400064 | bytes 3898038 | tf_op jit(solution)/shard_map/pallas_call | solution.py:71
  257.4 9.3 %collective-permute-done.17.u_oth.up_w = bf16[1024,1408]{1,0:T(8,128)(2,1)S(1)} collective-permute-done((bf16[1024,1408]{1,0:T(8,128)(2,1)}, bf16[1024,1408]{1,0:T(8,128)(2,1)S(1)}, u32[]{:S(2)}, u32[]{:S(2)}) %collective-permute-start.17) | collective-permute-done | bytes 2883616 | tf_op jit(solution)/shard_map/ppermute | solution.py:37
  268.4 17.8 %shard_map.214 = (bf16[1536,1408]{1,0:T(8,128)(2,1)}, bf16[1536,1408]{1,0:T(8,128)(2,1)}, bf16[1536,1408]{1,0:T(8,128)(2,1)}) custom-call(bf16[1536,1024]{1,0:T(8,128)(2,1)} %bitcast.63, bf16[1536,1024]{1,0:T(8,128)(2,1)} %bitcast.67, bf16[1024,1408]{1,0:T(8,128)(2,1)} %all-gather.12.cloned.1.call-done.u_own.up_w, bf16[1024,1408]{1,0:T(8,128)(2,1)} %copy-done.2, ...), custom_call_target="tpu_custom_call" | custom-call | flops 1378800000 | bytes 4596011 | tf_op jit(solution)/shard_map/pallas_call | solution.py:71
  286.1 14.8 %shard_map.215 = bf16[2048,1408]{1,0:T(8,128)(2,1)} custom-call(bf16[1536,2048]{1,0:T(8,128)(2,1)} %bitcast.60, bf16[1536,1408]{1,0:T(8,128)(2,1)} %get-tuple-element.129.grad.rows), custom_call_target="tpu_custom_call" | custom-call | flops 1184999936 | bytes 3950012 | tf_op jit(solution)/shard_map/pallas_call | solution.py:71
  304.6 17.2 %shard_map.216 = (bf16[1536,1408]{1,0:T(8,128)(2,1)}, bf16[1536,1408]{1,0:T(8,128)(2,1)}) custom-call(bf16[1536,2048]{1,0:T(8,128)(2,1)} %bitcast.61, bf16[2048,1408]{1,0:T(8,128)(2,1)} %all-gather.14.cloned.1.call-done.weight, bf16[1536,1408]{1,0:T(8,128)(2,1)} %get-tuple-element.115.for_gate, bf16[1536,1408]{1,0:T(8,128)(2,1)} %get-tuple-element.116.for_up), custom_call_target="tpu_custom_call" | custom-call | flops 1301400064 | bytes 4338013 | tf_op jit(solution)/shard_map/pallas_call | solution.py:71
  321.7 9.2 %shard_map.217 = bf16[1024,1408]{1,0:T(8,128)(2,1)} custom-call(bf16[1536,1024]{1,0:T(8,128)(2,1)} %bitcast.68, bf16[1536,1408]{1,0:T(8,128)(2,1)} %get-tuple-element.121.grad.gate_g), custom_call_target="tpu_custom_call" | custom-call | flops 704400000 | bytes 2348016 | tf_op jit(solution)/shard_map/pallas_call | solution.py:71
  332.4 15.6 %shard_map.218 = (bf16[768,1024]{1,0:T(8,128)(2,1)}, bf16[768,1024]{1,0:T(8,128)(2,1)}) custom-call(bf16[1536,1408]{1,0:T(8,128)(2,1)} %get-tuple-element.121.grad.gate_g, bf16[1536,1408]{1,0:T(8,128)(2,1)} %get-tuple-element.124.up_g.grad, bf16[1024,1408]{1,0:T(8,128)(2,1)} %copy-done.1, bf16[1024,1408]{1,0:T(8,128)(2,1)} %copy-done.2), custom_call_target="tpu_custom_call" | custom-call | flops 1169400064 | bytes 3898014 | tf_op jit(solution)/shard_map/pallas_call | solution.py:71
  348.0 15.7 %shard_map.219 = (bf16[768,1024]{1,0:T(8,128)(2,1)}, bf16[768,1024]{1,0:T(8,128)(2,1)}) custom-call(bf16[1536,1408]{1,0:T(8,128)(2,1)} %get-tuple-element.121.grad.gate_g, bf16[1536,1408]{1,0:T(8,128)(2,1)} %get-tuple-element.124.up_g.grad, bf16[1024,1408]{1,0:T(8,128)(2,1)} %all-gather.8.cloned.1.call-done.w_own.gate_w, ...), custom_call_target="tpu_custom_call" | custom-call | flops 1161600000 | bytes 3872017 | tf_op jit(solution)/shard_map/pallas_call | solution.py:71
  374.8 9.1 %shard_map.221 = bf16[1024,1408]{1,0:T(8,128)(2,1)} custom-call(bf16[1536,1024]{1,0:T(8,128)(2,1)} %bitcast.69, bf16[1536,1408]{1,0:T(8,128)(2,1)} %get-tuple-element.124.up_g.grad), custom_call_target="tpu_custom_call" | custom-call | flops 704400000 | bytes 2348019 | tf_op jit(solution)/shard_map/pallas_call | solution.py:71
  384.3 12.1 %collective-permute-done.29.came = bf16[1024,1408]{1,0:T(8,128)(2,1)S(1)} collective-permute-done((bf16[1024,1408]{1,0:T(8,128)(2,1)}, bf16[1024,1408]{1,0:T(8,128)(2,1)S(1)}, u32[]{:S(2)}, u32[]{:S(2)}) %collective-permute-start.29) | collective-permute-done | bytes 2883616 | tf_op jit(solution)/shard_map/ppermute | solution.py:37
  405.1 9.9 %shard_map.231 = bf16[1024,1408]{1,0:T(8,128)(2,1)} custom-call(bf16[1536,1024]{1,0:T(8,128)(2,1)} %bitcast.64, bf16[1536,1408]{1,0:T(8,128)(2,1)} %get-tuple-element.121.grad.gate_g, bf16[1024,1408]{1,0:T(8,128)(2,1)} %copy-done.8), custom_call_target="tpu_custom_call" | custom-call | flops 766800000 | bytes 2556023 | tf_op jit(solution)/shard_map/pallas_call | solution.py:71
  424.5 16.1 %shard_map.224 = (bf16[768,2048]{1,0:T(8,128)(2,1)}, bf16[768,2048]{1,0:T(8,128)(2,1)}) custom-call(bf16[1536,1408]{1,0:T(8,128)(2,1)} %get-tuple-element.129.grad.rows, bf16[2048,1408]{1,0:T(8,128)(2,1)} %all-gather.14.cloned.1.call-done.weight), custom_call_target="tpu_custom_call" | custom-call | flops 1146000000 | bytes 3820021 | tf_op jit(solution)/shard_map/pallas_call | solution.py:71
  440.6 16.7 %collective-permute-done.23.came = bf16[1024,1408]{1,0:T(8,128)(2,1)S(1)} collective-permute-done((bf16[1024,1408]{1,0:T(8,128)(2,1)}, bf16[1024,1408]{1,0:T(8,128)(2,1)S(1)}, u32[]{:S(2)}, u32[]{:S(2)}) %collective-permute-start.23) | collective-permute-done | bytes 2883616 | tf_op jit(solution)/shard_map/ppermute | solution.py:37
  458.9 9.9 %shard_map.225 = bf16[1024,1408]{1,0:T(8,128)(2,1)} custom-call(bf16[1536,1024]{1,0:T(8,128)(2,1)} %bitcast.65, bf16[1536,1408]{1,0:T(8,128)(2,1)} %get-tuple-element.124.up_g.grad, bf16[1024,1408]{1,0:T(8,128)(2,1)} %copy-done.7), custom_call_target="tpu_custom_call" | custom-call | flops 3068400128 | bytes 10228028 | tf_op jit(solution)/shard_map/pallas_call | solution.py:71
  502.4 27.1 %shard_map.229 = bf16[4,3,128,640]{3,2,1,0:T(8,128)(2,1)} custom-call(s32[3]{0:T(128)} %bitcast.119, bf16[4,3,128,512]{3,2,1,0:T(8,128)(2,1)} %get-tuple-element.104.query_in, bf16[4,3,128,128]{3,2,1,0:T(8,128)(2,1)} %get-tuple-element.105.kv_in, bf16[4,3,128,512]{3,2,1,0:T(8,128)(2,1)} %bitcast.96, bf16[4,3,128,512]{3,2,1,0:T(8,128)(2,1)} %get-tuple-element.96.mixed_in, ...), custom_call_target="tpu_custom_call" | custom-call | flops 38310600704 | bytes 127702024 | tf_op jit(solution)/shard_map/pallas_call | solution.py:71
  (246 shorter events, 284.7 us)
Async XLA Ops:
  7.2 41.3 %all-gather.6.cloned.1.call-start = ((), (), s32[]{:S(2)}) async-start(), calls=%async_computation.5 | async-start | bytes 1740800 | tf_op jit(solution)/shard_map/all_gather | solution.py:422
  11.5 66.0 %all-gather.10.cloned.1.call-start = ((), (), s32[]{:S(2)}) async-start(), calls=%async_computation.7 | async-start | bytes 1310720 | tf_op jit(solution)/shard_map/all_gather | solution.py:422
  13.4 124.4 %all-gather.8.cloned.1.call-start = ((), (), s32[]{:S(2)}) async-start(), calls=%async_computation.6 | async-start | bytes 3604480 | tf_op jit(solution)/shard_map/all_gather | solution.py:422
  14.2 183.0 %all-gather.12.cloned.1.call-start = ((), (), s32[]{:S(2)}) async-start(), calls=%async_computation.8 | async-start | bytes 3604480 | tf_op jit(solution)/shard_map/all_gather | solution.py:422
  14.7 289.8 %all-gather.14.cloned.1.call-start = ((), (), s32[]{:S(2)}) async-start(), calls=%async_computation.9 | async-start | bytes 7208960 | tf_op jit(solution)/shard_map/all_gather | solution.py:422
  18.1 36.0 %collective-permute-start = (bf16[384,2048]{1,0:T(8,128)(2,1)S(1)}, bf16[384,2048]{1,0:T(8,128)(2,1)}, u32[]{:S(2)}, u32[]{:S(2)}) collective-permute-start(bf16[384,2048]{1,0:T(8,128)(2,1)S(1)} %bitcast.98), channel_id=1, source_target_pairs={{0,2},{2,0},{1,3},{3,1},{4,6},{6,4},{5,7},{7,5},{8,10},{10,8},{9,1... | collective-permute-start | bytes 4718600 | tf_op jit(solution)/shard_map/ppermute | solution.py:37
  50.0 39.7 %collective-permute-start.1 = (bf16[384,2048]{1,0:T(8,128)(2,1)S(1)}, bf16[384,2048]{1,0:T(8,128)(2,1)}, u32[]{:S(2)}, u32[]{:S(2)}) collective-permute-start(bf16[384,2048]{1,0:T(8,128)(2,1)S(1)} %bitcast.99), channel_id=1, source_target_pairs={{0,1},{1,0},{2,3},{3,2},{4,5},{5,4},{6,7},{7,6},{8,9},{9,8},{10,11... | collective-permute-start | bytes 4718600 | tf_op jit(solution)/shard_map/ppermute | solution.py:37
  54.1 54.2 %collective-permute-start.5 = (bf16[384,2048]{1,0:T(8,128)(2,1)}, bf16[384,2048]{1,0:T(8,128)(2,1)}, u32[]{:S(2)}, u32[]{:S(2)}) collective-permute-start(bf16[384,2048]{1,0:T(8,128)(2,1)} %bitcast.10.p0.upstream), channel_id=1, source_target_pairs={{0,2},{2,0},{1,3},{3,1},{4,6},{6,4},{5,7},{7,5},{8,10},{10,8},{9,1... | collective-permute-start | bytes 4718600 | tf_op jit(solution)/shard_map/ppermute | solution.py:37
  59.5 397.8 %reduce-scatter.6.cloned.1.call-start = ((), (), s32[]{:S(2)}) async-start(), calls=%async_computation.10 | async-start | bytes 7208960 | tf_op jit(solution)/shard_map/reduce_scatter | solution.py:585
  80.4 49.4 %collective-permute-start.6 = (bf16[1024,512]{1,0:T(8,128)(2,1)}, bf16[1024,512]{1,0:T(8,128)(2,1)S(1)}, u32[]{:S(2)}, u32[]{:S(2)}) collective-permute-start(bf16[1024,512]{1,0:T(8,128)(2,1)} %all-gather.10.cloned.1.call-done.weight.w_own), channel_id=1, source_target_pairs={{0,4},{4,0},{1,5},{5,1},{2,6},{6,2},{3,7},{7,3},{8,12},{12,8},{9,1... | collective-permute-start | bytes 3145736 | tf_op jit(solution)/shard_map/ppermute | solution.py:37
  137.8 64.8 %collective-permute-start.12 = (bf16[1024,1408]{1,0:T(8,128)(2,1)}, bf16[1024,1408]{1,0:T(8,128)(2,1)S(1)}, u32[]{:S(2)}, u32[]{:S(2)}) collective-permute-start(bf16[1024,1408]{1,0:T(8,128)(2,1)} %all-gather.8.cloned.1.call-done.w_own.gate_w), channel_id=1, source_target_pairs={{0,4},{4,0},{1,5},{5,1},{2,6},{6,2},{3,7},{7,3},{8,12},{12,8},{9,1... | collective-permute-start | bytes 8650760 | tf_op jit(solution)/shard_map/ppermute | solution.py:37
  160.7 42.9 %collective-permute-start.13 = (bf16[384,2048]{1,0:T(8,128)(2,1)}, bf16[384,2048]{1,0:T(8,128)(2,1)}, u32[]{:S(2)}, u32[]{:S(2)}) collective-permute-start(bf16[384,2048]{1,0:T(8,128)(2,1)} %bitcast.10.p0.upstream), channel_id=1, source_target_pairs={{0,1},{1,0},{2,3},{3,2},{4,5},{5,4},{6,7},{7,6},{8,9},{9,8},{10,11... | collective-permute-start | bytes 4718600 | tf_op jit(solution)/shard_map/ppermute | solution.py:37
  160.8 42.9 %collective-permute-start.14 = (bf16[384,2048]{1,0:T(8,128)(2,1)}, bf16[384,2048]{1,0:T(8,128)(2,1)}, u32[]{:S(2)}, u32[]{:S(2)}) collective-permute-start(bf16[384,2048]{1,0:T(8,128)(2,1)} %collective-permute-done.5.p1), channel_id=1, source_target_pairs={{0,1},{1,0},{2,3},{3,2},{4,5},{5,4},{6,7},{7,6},{8,9},{9,8},{10,11... | collective-permute-start | bytes 4718600 | tf_op jit(solution)/shard_map/ppermute | solution.py:37
  194.8 36.3 %collective-permute-start.11 = (bf16[384,2048]{1,0:T(8,128)(2,1)}, bf16[384,2048]{1,0:T(8,128)(2,1)}, u32[]{:S(2)}, u32[]{:S(2)}) collective-permute-start(bf16[384,2048]{1,0:T(8,128)(2,1)} %get-tuple-element.106.p0), channel_id=1, source_target_pairs={{0,2},{2,0},{1,3},{3,1},{4,6},{6,4},{5,7},{7,5},{8,10},{10,8},{9,1... | collective-permute-start | bytes 4718600 | tf_op jit(solution)/shard_map/ppermute | solution.py:37
  202.7 64.1 %collective-permute-start.17 = (bf16[1024,1408]{1,0:T(8,128)(2,1)}, bf16[1024,1408]{1,0:T(8,128)(2,1)S(1)}, u32[]{:S(2)}, u32[]{:S(2)}) collective-permute-start(bf16[1024,1408]{1,0:T(8,128)(2,1)} %all-gather.12.cloned.1.call-done.u_own.up_w), channel_id=1, source_target_pairs={{0,4},{4,0},{1,5},{5,1},{2,6},{6,2},{3,7},{7,3},{8,12},{12,8},{9,1... | collective-permute-start | bytes 8650760 | tf_op jit(solution)/shard_map/ppermute | solution.py:37
  301.0 236.7 %reduce-scatter.8.cloned.1.call-start = ((), (), s32[]{:S(2)}) async-start(), calls=%async_computation.11 | async-start | bytes 3604480 | tf_op jit(solution)/shard_map/reduce_scatter | solution.py:585
  330.9 65.6 %collective-permute-start.29 = (bf16[1024,1408]{1,0:T(8,128)(2,1)}, bf16[1024,1408]{1,0:T(8,128)(2,1)S(1)}, u32[]{:S(2)}, u32[]{:S(2)}) collective-permute-start(bf16[1024,1408]{1,0:T(8,128)(2,1)} %shard_map.217), channel_id=1, source_target_pairs={{0,4},{4,0},{1,5},{5,1},{2,6},{6,2},{3,7},{7,3},{8,12},{12,8},{9,1... | collective-permute-start | bytes 8650760 | tf_op jit(solution)/shard_map/ppermute | solution.py:37
  383.8 73.5 %collective-permute-start.23 = (bf16[1024,1408]{1,0:T(8,128)(2,1)}, bf16[1024,1408]{1,0:T(8,128)(2,1)S(1)}, u32[]{:S(2)}, u32[]{:S(2)}) collective-permute-start(bf16[1024,1408]{1,0:T(8,128)(2,1)} %shard_map.221), channel_id=1, source_target_pairs={{0,4},{4,0},{1,5},{5,1},{2,6},{6,2},{3,7},{7,3},{8,12},{12,8},{9,1... | collective-permute-start | bytes 8650760 | tf_op jit(solution)/shard_map/ppermute | solution.py:37
  415.0 177.7 %reduce-scatter.10.cloned.1.call-start = ((), (), s32[]{:S(2)}) async-start(), calls=%async_computation.12 | async-start | bytes 3604480 | tf_op jit(solution)/shard_map/reduce_scatter | solution.py:585
  423.0 45.8 %collective-permute-start.22 = (bf16[384,2048]{1,0:T(8,128)(2,1)}, bf16[384,2048]{1,0:T(8,128)(2,1)}, u32[]{:S(2)}, u32[]{:S(2)}) collective-permute-start(bf16[384,2048]{1,0:T(8,128)(2,1)} %get-tuple-element.128.p0), channel_id=1, source_target_pairs={{0,2},{2,0},{1,3},{3,1},{4,6},{6,4},{5,7},{7,5},{8,10},{10,8},{9,1... | collective-permute-start | bytes 4718600 | tf_op jit(solution)/shard_map/ppermute | solution.py:37
  424.5 44.2 %collective-permute-start.24 = (bf16[384,2048]{1,0:T(8,128)(2,1)}, bf16[384,2048]{1,0:T(8,128)(2,1)}, u32[]{:S(2)}, u32[]{:S(2)}) collective-permute-start(bf16[384,2048]{1,0:T(8,128)(2,1)} %get-tuple-element.128.p0), channel_id=1, source_target_pairs={{0,1},{1,0},{2,3},{3,2},{4,5},{5,4},{6,7},{7,6},{8,9},{9,8},{10,11... | collective-permute-start | bytes 4718600 | tf_op jit(solution)/shard_map/ppermute | solution.py:37
  479.9 131.3 %reduce-scatter.14.cloned.1.call-start = ((), (), s32[]{:S(2)}) async-start(), calls=%async_computation.14 | async-start | bytes 1310720 | tf_op jit(solution)/shard_map/reduce_scatter | solution.py:585
  500.8 36.8 %collective-permute-start.28 = (bf16[384,2048]{1,0:T(8,128)(2,1)}, bf16[384,2048]{1,0:T(8,128)(2,1)}, u32[]{:S(2)}, u32[]{:S(2)}) collective-permute-start(bf16[384,2048]{1,0:T(8,128)(2,1)} %shard_map.228), channel_id=1, source_target_pairs={{0,2},{2,0},{1,3},{3,1},{4,6},{6,4},{5,7},{7,5},{8,10},{10,8},{9,1... | collective-permute-start | bytes 4718600 | tf_op jit(solution)/shard_map/ppermute | solution.py:37
  561.0 71.6 %reduce-scatter.12.cloned.1.call-start = ((), (), s32[]{:S(2)}) async-start(), calls=%async_computation.13 | async-start | bytes 1740800 | tf_op jit(solution)/shard_map/reduce_scatter | solution.py:585
  (57 other events, 614.4 us)
Sparse Core Ops, SparseCore 0:
  11.7 36.7 all-gather.5
  50.6 26.8 all-gather.9
  79.1 58.6 all-gather.7
  139.2 57.8 all-gather.11
  199.1 105.3 all-gather.13
  306.7 100.5 reduce-scatter.5
  415.2 53.4 reduce-scatter.7
  480.1 54.4 reduce-scatter.9
  561.1 25.2 reduce-scatter.13
  599.1 30.7 reduce-scatter.11

commit v5 on v4

--- a/solution.py
+++ b/solution.py
@@ -16,8 +16,8 @@
 F32 = jnp.float32
 BF16 = jnp.bfloat16
 SWAP = [(0, 1), (1, 0)]
-COST = {1: 1702, 2: 2220, 3: 2582, 4: 5630, 5: 1730, 6: 798, 7: 1730, 8: 798, 9: 1498, 10: 1626, 11: 4596, 12: 3950, 13: 4338, 14: 3898, 15: 798, 16: 2348, 17: 3872, 18: 798, 19: 2348, 20: 1986, 21: 3820, 22: 1006, 23: 2556, 24: 1626, 25: 2142, 26: 8118, 27: 127702, 28: 10228, 29: 33062, 31: 1626, 32: 1476, 34: 1522, 36: 1498, 37: 53466, 38: 3898, 39: 23246}
-SKIP = {133, 134, 103, 137, 107, 139, 142, 116, 150, 151, 120, 122, 158, 159}
+COST = {1: 1702, 2: 2220, 3: 2582, 4: 5630, 5: 1730, 6: 798, 7: 1730, 8: 798, 9: 1498, 10: 1626, 11: 4596, 12: 3950, 13: 4338, 14: 3898, 15: 798, 16: 2348, 17: 3872, 18: 798, 19: 2348, 20: 1986, 21: 3820, 22: 1006, 23: 2556, 24: 1626, 25: 2142, 26: 8118, 27: 127702, 28: 10228, 38: 3898}
+SKIP = {161, 103, 136, 137, 107, 139, 140, 142, 116, 150, 120, 122, 158, 159}
 ROW_PAD = 16
 
 
@@ -667,15 +667,14 @@
         )
         return (kept, sent), sums / gain_one[which]
 
-    qkv_sent = weight_grad(31, seq_one[1], after(159, qkv_g, out_sent))
+    oth_parts, oth_gain = project_gain(29, 1, qkv_g)
+    first_oth = scatter_rows(30, *oth_parts)
+    qkv_sent = weight_grad(31, seq_one[1], after(167, after(161, after(130, qkv_g, oth_parts[0]), first_oth[3]), block_terms[2]))
     qkv_came = swap_x(after(134, qkv_sent, out_came))
-    out_total = weight_grad(34, seq_attn[0], mixed, after(155, after(132, out_came, qkv_sent), qkv_g))
+    out_total = weight_grad(34, seq_attn[0], mixed, after(132, out_came, qkv_sent))
     grad_out = reduce_z(out_total)
-    oth_parts, oth_gain = project_gain(29, 1, after(131, qkv_g, out_total))
-    first_oth = scatter_rows(30, *oth_parts)
-    own_parts, own_gain = project_gain(32, 0, after(143, after(142, qkv_g, first_oth[3]), out_total))
-    first_own = scatter_rows(33, *own_parts)
-    qkv_near = weight_grad(35, seq_one[0], after(133, qkv_g, first_own[3]), kind=F32)
+    own_parts, own_gain = project_gain(32, 0, after(131, qkv_g, out_total))
+    qkv_near = weight_grad(35, seq_one[0], after(133, qkv_g, own_parts[0]), kind=F32)
 
     def gain_pair(one, two):
         return jnp.concatenate([one.reshape(hi, depth), two.reshape(hi, depth)], axis=1)
@@ -690,10 +689,11 @@
         total_kernel,
         [],
         hi,
-        tiles_of(depth, qkv_near, after(152, after(151, after(135, qkv_came, grad_up), first_oth[2]), first_own[2]))
+        tiles_of(depth, qkv_near, after(152, after(151, after(135, qkv_came, grad_up), first_oth[2]), qkv_near))
         + tiles_of(ROW_PAD, gain_rows.reshape(hi * ROW_PAD, all_cols)),
         [((hi * (depth + ROW_PAD), all_cols), BF16, row_spec(depth + ROW_PAD, all_cols))],
     )
+    first_own = scatter_rows(33, own_parts[0], after(166, own_parts[1], qkv_total))
     grad_qkv = reduce_z(qkv_total).astype(F32)
     gain_sums = grad_qkv[depth, : 2 * depth]
     gain_sums = gain_sums + swap(gain_sums, "th")

time: 653 us -> 646 us (0.989)
    unnamed x75 -> x77, local copies, waits for them, and re-layouts: 27.2 us -> 25.1 us
  transfers between devices with their start and end apart: 49 -> 49, of which waited for: 26 -> 25; matrix products, arithmetic and copies ran while one was open for 5% -> 5% of each run, Pallas kernels for 55% -> 55%
where the time goes in v5:
time: 646 us; the launch traced here: 640 us
  Pallas kernels  354 us (55%)
  waiting for transfers between devices  187 us (29%)
  local copies, waits for them, and re-layouts  38.9 us (6%)
  starting transfers between devices  34 us (5%)
  between operations  14.9 us (2%)
  other arithmetic  11.9 us (2%)
    pallas_call x39, Pallas kernels, call(): pl.pallas_call(kernel, out_shape=[jax.ShapeDtypeStruct(shape, kind) for s...  354 us
    ppermute x39, waiting for transfers between devices, swap(): return lax.ppermute(value, axis, SWAP)  151 us
    all_gather x5, waiting for transfers between devices, gather(): return lax.all_gather(part, 'fh', axis=0, tiled=True)  34.7 us
    ppermute x39, starting transfers between devices, swap(): return lax.ppermute(value, axis, SWAP)  32.5 us
    unnamed x77, local copies, waits for them, and re-layouts  25.1 us
  transfers between devices with their start and end apart: 49, of which 25 were waited for; matrix products, arithmetic and copies ran while one was open for 5% of the time, Pallas kernels for 55%

profile of v5, /device:TPU:0, one launch (start us, length us, event | category | flops | bytes accessed | tf_op | source)
XLA Modules:
  0.0 640.4 jit_solution(15839649009864312046)
XLA Ops:
  19.7 14.6 %collective-permute-done.3 = bf16[256,1408]{1,0:T(8,128)(2,1)S(1)} collective-permute-done((bf16[256,1408]{1,0:T(8,128)(2,1)S(1)}, bf16[256,1408]{1,0:T(8,128)(2,1)S(1)}, u32[]{:S(2)}, u32[]{:S(2)}) %collective-permute-start.3) | collective-permute-done | bytes 720928 | tf_op jit(solution)/shard_map/ppermute | solution.py:37
  35.5 13.0 %all-gather.6.cloned.1.call-done = bf16[1088,640]{1,0:T(8,128)(2,1)} async-done(((bf16[272,640]{1,0:T(8,128)(2,1)}), bf16[1088,640]{1,0:T(8,128)(2,1)}) %all-gather.6.cloned.1.call-update) | async-done | bytes 1392656 | tf_op jit(solution)/shard_map/all_gather | solution.py:422
  60.1 17.4 %all-gather.10.cloned.1.call-done.weight.w_own = bf16[1024,512]{1,0:T(8,128)(2,1)} async-done(((bf16[256,512]{1,0:T(8,128)(2,1)}), bf16[1024,512]{1,0:T(8,128)(2,1)}) %all-gather.10.cloned.1.call-update) | async-done | bytes 1048592 | tf_op jit(solution)/shard_map/all_gather | solution.py:422
  98.3 10.0 %shard_map.204 = f32[1536,640]{1,0:T(8,128)} custom-call(bf16[1536,1024]{1,0:T(8,128)(2,1)} %bitcast.77, bf16[1536,1024]{1,0:T(8,128)(2,1)} %bitcast.74, bf16[1024,640]{1,0:T(8,128)(2,1)} %bitcast.86, bf16[1024,640]{1,0:T(8,128)(2,1)} %bitcast.88), custom_call_target="tpu_custom_call" | custom-call | flops 774600000 | bytes 2582003 | tf_op jit(solution)/shard_map/pallas_call | solution.py:71
  108.2 21.5 %shard_map.205 = (bf16[4,3,128,512]{3,2,1,0:T(8,128)(2,1)}, bf16[4,3,128,128]{3,2,1,0:T(8,128)(2,1)}, bf16[4,3,128,512]{3,2,1,0:T(8,128)(2,1)}, f32[3,8,512]{2,1,0:T(8,128)}) custom-call(s32[3]{0:T(128)} %bitcast.119, f32[4,3,128,640]{3,2,1,0:T(8,128)} %bitcast.90, f32[512,128]{1,0:T(8,128)} %copy.57.cos, f32[512,128]{1,0:T(8,128)} %pad_maximum_fusion.1.sine, ...), custom_call_target="tpu_custom_call" | custom-call | flops 1688999936 | bytes 5630004 | tf_op jit(solution)/shard_map/pallas_call | solution.py:71
  162.6 9.4 %collective-permute-done.10.b2 = bf16[384,1024]{1,0:T(8,128)(2,1)S(1)} collective-permute-done((bf16[384,1024]{1,0:T(8,128)(2,1)S(1)}, bf16[384,1024]{1,0:T(8,128)(2,1)S(1)}, u32[]{:S(2)}, u32[]{:S(2)}) %collective-permute-start.10) | collective-permute-done | bytes 786464 | tf_op jit(solution)/shard_map/ppermute | solution.py:37
  171.9 16.3 %collective-permute-done.9.a2 = bf16[384,1024]{1,0:T(8,128)(2,1)S(1)} collective-permute-done((bf16[384,1024]{1,0:T(8,128)(2,1)}, bf16[384,1024]{1,0:T(8,128)(2,1)S(1)}, u32[]{:S(2)}, u32[]{:S(2)}) %collective-permute-start.9) | collective-permute-done | bytes 786464 | tf_op jit(solution)/shard_map/ppermute | solution.py:37
  210.5 20.9 %collective-permute-done.11.p1 = bf16[384,2048]{1,0:T(8,128)(2,1)} collective-permute-done((bf16[384,2048]{1,0:T(8,128)(2,1)}, bf16[384,2048]{1,0:T(8,128)(2,1)}, u32[]{:S(2)}, u32[]{:S(2)}) %collective-permute-start.11) | collective-permute-done | bytes 1572896 | tf_op jit(solution)/shard_map/ppermute | solution.py:37
  242.5 15.1 %shard_map.213.gate_in = f32[1536,1408]{1,0:T(8,128)} custom-call(bf16[1536,1024]{1,0:T(8,128)(2,1)} %bitcast.62, bf16[1536,1024]{1,0:T(8,128)(2,1)} %bitcast.66, bf16[1024,1408]{1,0:T(8,128)(2,1)} %all-gather.8.cloned.1.call-done.w_own.gate_w, bf16[1024,1408]{1,0:T(8,128)(2,1)} %copy-done.1), custom_call_target="tpu_custom_call" | custom-call | flops 1169400064 | bytes 3898038 | tf_op jit(solution)/shard_map/pallas_call | solution.py:71
  257.6 9.1 %collective-permute-done.17.u_oth.up_w = bf16[1024,1408]{1,0:T(8,128)(2,1)S(1)} collective-permute-done((bf16[1024,1408]{1,0:T(8,128)(2,1)}, bf16[1024,1408]{1,0:T(8,128)(2,1)S(1)}, u32[]{:S(2)}, u32[]{:S(2)}) %collective-permute-start.17) | collective-permute-done | bytes 2883616 | tf_op jit(solution)/shard_map/ppermute | solution.py:37
  268.3 17.8 %shard_map.214 = (bf16[1536,1408]{1,0:T(8,128)(2,1)}, bf16[1536,1408]{1,0:T(8,128)(2,1)}, bf16[1536,1408]{1,0:T(8,128)(2,1)}) custom-call(bf16[1536,1024]{1,0:T(8,128)(2,1)} %bitcast.63, bf16[1536,1024]{1,0:T(8,128)(2,1)} %bitcast.67, bf16[1024,1408]{1,0:T(8,128)(2,1)} %all-gather.12.cloned.1.call-done.u_own.up_w, bf16[1024,1408]{1,0:T(8,128)(2,1)} %copy-done.2, ...), custom_call_target="tpu_custom_call" | custom-call | flops 1378800000 | bytes 4596011 | tf_op jit(solution)/shard_map/pallas_call | solution.py:71
  286.1 14.8 %shard_map.215 = bf16[2048,1408]{1,0:T(8,128)(2,1)} custom-call(bf16[1536,2048]{1,0:T(8,128)(2,1)} %bitcast.60, bf16[1536,1408]{1,0:T(8,128)(2,1)} %get-tuple-element.130.grad.rows), custom_call_target="tpu_custom_call" | custom-call | flops 1184999936 | bytes 3950012 | tf_op jit(solution)/shard_map/pallas_call | solution.py:71
  304.6 17.2 %shard_map.216 = (bf16[1536,1408]{1,0:T(8,128)(2,1)}, bf16[1536,1408]{1,0:T(8,128)(2,1)}) custom-call(bf16[1536,2048]{1,0:T(8,128)(2,1)} %bitcast.61, bf16[2048,1408]{1,0:T(8,128)(2,1)} %all-gather.14.cloned.1.call-done.weight, bf16[1536,1408]{1,0:T(8,128)(2,1)} %get-tuple-element.117.for_gate, bf16[1536,1408]{1,0:T(8,128)(2,1)} %get-tuple-element.118.for_up), custom_call_target="tpu_custom_call" | custom-call | flops 1301400064 | bytes 4338013 | tf_op jit(solution)/shard_map/pallas_call | solution.py:71
  321.7 9.2 %shard_map.217 = bf16[1024,1408]{1,0:T(8,128)(2,1)} custom-call(bf16[1536,1024]{1,0:T(8,128)(2,1)} %bitcast.68, bf16[1536,1408]{1,0:T(8,128)(2,1)} %get-tuple-element.123.grad.gate_g), custom_call_target="tpu_custom_call" | custom-call | flops 704400000 | bytes 2348016 | tf_op jit(solution)/shard_map/pallas_call | solution.py:71
  332.4 15.6 %shard_map.218 = (bf16[768,1024]{1,0:T(8,128)(2,1)}, bf16[768,1024]{1,0:T(8,128)(2,1)}) custom-call(bf16[1536,1408]{1,0:T(8,128)(2,1)} %get-tuple-element.123.grad.gate_g, bf16[1536,1408]{1,0:T(8,128)(2,1)} %get-tuple-element.126.up_g.grad, bf16[1024,1408]{1,0:T(8,128)(2,1)} %copy-done.1, bf16[1024,1408]{1,0:T(8,128)(2,1)} %copy-done.2), custom_call_target="tpu_custom_call" | custom-call | flops 1169400064 | bytes 3898014 | tf_op jit(solution)/shard_map/pallas_call | solution.py:71
  347.9 15.7 %shard_map.219 = (bf16[768,1024]{1,0:T(8,128)(2,1)}, bf16[768,1024]{1,0:T(8,128)(2,1)}) custom-call(bf16[1536,1408]{1,0:T(8,128)(2,1)} %get-tuple-element.123.grad.gate_g, bf16[1536,1408]{1,0:T(8,128)(2,1)} %get-tuple-element.126.up_g.grad, bf16[1024,1408]{1,0:T(8,128)(2,1)} %all-gather.8.cloned.1.call-done.w_own.gate_w, ...), custom_call_target="tpu_custom_call" | custom-call | flops 1161600000 | bytes 3872017 | tf_op jit(solution)/shard_map/pallas_call | solution.py:71
  374.7 9.1 %shard_map.221 = bf16[1024,1408]{1,0:T(8,128)(2,1)} custom-call(bf16[1536,1024]{1,0:T(8,128)(2,1)} %bitcast.69, bf16[1536,1408]{1,0:T(8,128)(2,1)} %get-tuple-element.126.up_g.grad), custom_call_target="tpu_custom_call" | custom-call | flops 704400000 | bytes 2348019 | tf_op jit(solution)/shard_map/pallas_call | solution.py:71
  384.3 12.1 %collective-permute-done.29.came = bf16[1024,1408]{1,0:T(8,128)(2,1)S(1)} collective-permute-done((bf16[1024,1408]{1,0:T(8,128)(2,1)}, bf16[1024,1408]{1,0:T(8,128)(2,1)S(1)}, u32[]{:S(2)}, u32[]{:S(2)}) %collective-permute-start.29) | collective-permute-done | bytes 2883616 | tf_op jit(solution)/shard_map/ppermute | solution.py:37
  405.1 9.9 %shard_map.232 = bf16[1024,1408]{1,0:T(8,128)(2,1)} custom-call(bf16[1536,1024]{1,0:T(8,128)(2,1)} %bitcast.64, bf16[1536,1408]{1,0:T(8,128)(2,1)} %get-tuple-element.123.grad.gate_g, bf16[1024,1408]{1,0:T(8,128)(2,1)} %copy-done.10), custom_call_target="tpu_custom_call" | custom-call | flops 766800000 | bytes 2556023 | tf_op jit(solution)/shard_map/pallas_call | solution.py:71
  424.5 16.1 %shard_map.224 = (bf16[768,2048]{1,0:T(8,128)(2,1)}, bf16[768,2048]{1,0:T(8,128)(2,1)}) custom-call(bf16[1536,1408]{1,0:T(8,128)(2,1)} %get-tuple-element.130.grad.rows, bf16[2048,1408]{1,0:T(8,128)(2,1)} %all-gather.14.cloned.1.call-done.weight), custom_call_target="tpu_custom_call" | custom-call | flops 1146000000 | bytes 3820021 | tf_op jit(solution)/shard_map/pallas_call | solution.py:71
  440.5 16.7 %collective-permute-done.23.came = bf16[1024,1408]{1,0:T(8,128)(2,1)S(1)} collective-permute-done((bf16[1024,1408]{1,0:T(8,128)(2,1)}, bf16[1024,1408]{1,0:T(8,128)(2,1)S(1)}, u32[]{:S(2)}, u32[]{:S(2)}) %collective-permute-start.23) | collective-permute-done | bytes 2883616 | tf_op jit(solution)/shard_map/ppermute | solution.py:37
  458.8 9.9 %shard_map.225 = bf16[1024,1408]{1,0:T(8,128)(2,1)} custom-call(bf16[1536,1024]{1,0:T(8,128)(2,1)} %bitcast.65, bf16[1536,1408]{1,0:T(8,128)(2,1)} %get-tuple-element.126.up_g.grad, bf16[1024,1408]{1,0:T(8,128)(2,1)} %copy-done.9), custom_call_target="tpu_custom_call" | custom-call | flops 3068400128 | bytes 10228028 | tf_op jit(solution)/shard_map/pallas_call | solution.py:71
  502.4 27.1 %shard_map.230 = bf16[4,3,128,640]{3,2,1,0:T(8,128)(2,1)} custom-call(s32[3]{0:T(128)} %bitcast.120, bf16[4,3,128,512]{3,2,1,0:T(8,128)(2,1)} %get-tuple-element.139.query_in, bf16[4,3,128,128]{3,2,1,0:T(8,128)(2,1)} %get-tuple-element.140.kv_in, bf16[4,3,128,512]{3,2,1,0:T(8,128)(2,1)} %bitcast.97, bf16[4,3,128,512]{3,2,1,0:T(8,128)(2,1)} %get-tuple-element.99.mixed_in, ...), custom_call_target="tpu_custom_call" | custom-call | flops 38310600704 | bytes 127702024 | tf_op jit(solution)/shard_map/pallas_call | solution.py:71
  599.4 9.9 %collective-permute-done.37 = bf16[256,1408]{1,0:T(8,128)(2,1)S(1)} collective-permute-done((bf16[256,1408]{1,0:T(8,128)(2,1)S(1)}, bf16[256,1408]{1,0:T(8,128)(2,1)S(1)}, u32[]{:S(2)}, u32[]{:S(2)}) %collective-permute-start.37) | collective-permute-done | bytes 720928 | tf_op jit(solution)/shard_map/ppermute | solution.py:37
  (248 shorter events, 277.1 us)
Async XLA Ops:
  7.2 41.3 %all-gather.6.cloned.1.call-start = ((), (), s32[]{:S(2)}) async-start(), calls=%async_computation.5 | async-start | bytes 1740800 | tf_op jit(solution)/shard_map/all_gather | solution.py:422
  11.5 66.0 %all-gather.10.cloned.1.call-start = ((), (), s32[]{:S(2)}) async-start(), calls=%async_computation.7 | async-start | bytes 1310720 | tf_op jit(solution)/shard_map/all_gather | solution.py:422
  13.4 124.4 %all-gather.8.cloned.1.call-start = ((), (), s32[]{:S(2)}) async-start(), calls=%async_computation.6 | async-start | bytes 3604480 | tf_op jit(solution)/shard_map/all_gather | solution.py:422
  14.2 183.0 %all-gather.12.cloned.1.call-start = ((), (), s32[]{:S(2)}) async-start(), calls=%async_computation.8 | async-start | bytes 3604480 | tf_op jit(solution)/shard_map/all_gather | solution.py:422
  14.7 289.8 %all-gather.14.cloned.1.call-start = ((), (), s32[]{:S(2)}) async-start(), calls=%async_computation.9 | async-start | bytes 7208960 | tf_op jit(solution)/shard_map/all_gather | solution.py:422
  18.1 36.0 %collective-permute-start = (bf16[384,2048]{1,0:T(8,128)(2,1)S(1)}, bf16[384,2048]{1,0:T(8,128)(2,1)}, u32[]{:S(2)}, u32[]{:S(2)}) collective-permute-start(bf16[384,2048]{1,0:T(8,128)(2,1)S(1)} %bitcast.99), channel_id=1, source_target_pairs={{0,2},{2,0},{1,3},{3,1},{4,6},{6,4},{5,7},{7,5},{8,10},{10,8},{9,1... | collective-permute-start | bytes 4718600 | tf_op jit(solution)/shard_map/ppermute | solution.py:37
  50.0 39.7 %collective-permute-start.1 = (bf16[384,2048]{1,0:T(8,128)(2,1)S(1)}, bf16[384,2048]{1,0:T(8,128)(2,1)}, u32[]{:S(2)}, u32[]{:S(2)}) collective-permute-start(bf16[384,2048]{1,0:T(8,128)(2,1)S(1)} %bitcast.100), channel_id=1, source_target_pairs={{0,1},{1,0},{2,3},{3,2},{4,5},{5,4},{6,7},{7,6},{8,9},{9,8},{10,11... | collective-permute-start | bytes 4718600 | tf_op jit(solution)/shard_map/ppermute | solution.py:37
  54.1 54.1 %collective-permute-start.5 = (bf16[384,2048]{1,0:T(8,128)(2,1)}, bf16[384,2048]{1,0:T(8,128)(2,1)}, u32[]{:S(2)}, u32[]{:S(2)}) collective-permute-start(bf16[384,2048]{1,0:T(8,128)(2,1)} %bitcast.10.p0.upstream), channel_id=1, source_target_pairs={{0,2},{2,0},{1,3},{3,1},{4,6},{6,4},{5,7},{7,5},{8,10},{10,8},{9,1... | collective-permute-start | bytes 4718600 | tf_op jit(solution)/shard_map/ppermute | solution.py:37
  59.5 397.8 %reduce-scatter.6.cloned.1.call-start = ((), (), s32[]{:S(2)}) async-start(), calls=%async_computation.10 | async-start | bytes 7208960 | tf_op jit(solution)/shard_map/reduce_scatter | solution.py:585
  80.4 49.4 %collective-permute-start.6 = (bf16[1024,512]{1,0:T(8,128)(2,1)}, bf16[1024,512]{1,0:T(8,128)(2,1)S(1)}, u32[]{:S(2)}, u32[]{:S(2)}) collective-permute-start(bf16[1024,512]{1,0:T(8,128)(2,1)} %all-gather.10.cloned.1.call-done.weight.w_own), channel_id=1, source_target_pairs={{0,4},{4,0},{1,5},{5,1},{2,6},{6,2},{3,7},{7,3},{8,12},{12,8},{9,1... | collective-permute-start | bytes 3145736 | tf_op jit(solution)/shard_map/ppermute | solution.py:37
  137.8 64.8 %collective-permute-start.12 = (bf16[1024,1408]{1,0:T(8,128)(2,1)}, bf16[1024,1408]{1,0:T(8,128)(2,1)S(1)}, u32[]{:S(2)}, u32[]{:S(2)}) collective-permute-start(bf16[1024,1408]{1,0:T(8,128)(2,1)} %all-gather.8.cloned.1.call-done.w_own.gate_w), channel_id=1, source_target_pairs={{0,4},{4,0},{1,5},{5,1},{2,6},{6,2},{3,7},{7,3},{8,12},{12,8},{9,1... | collective-permute-start | bytes 8650760 | tf_op jit(solution)/shard_map/ppermute | solution.py:37
  160.8 42.8 %collective-permute-start.13 = (bf16[384,2048]{1,0:T(8,128)(2,1)}, bf16[384,2048]{1,0:T(8,128)(2,1)}, u32[]{:S(2)}, u32[]{:S(2)}) collective-permute-start(bf16[384,2048]{1,0:T(8,128)(2,1)} %bitcast.10.p0.upstream), channel_id=1, source_target_pairs={{0,1},{1,0},{2,3},{3,2},{4,5},{5,4},{6,7},{7,6},{8,9},{9,8},{10,11... | collective-permute-start | bytes 4718600 | tf_op jit(solution)/shard_map/ppermute | solution.py:37
  160.9 42.8 %collective-permute-start.14 = (bf16[384,2048]{1,0:T(8,128)(2,1)}, bf16[384,2048]{1,0:T(8,128)(2,1)}, u32[]{:S(2)}, u32[]{:S(2)}) collective-permute-start(bf16[384,2048]{1,0:T(8,128)(2,1)} %collective-permute-done.5.p1), channel_id=1, source_target_pairs={{0,1},{1,0},{2,3},{3,2},{4,5},{5,4},{6,7},{7,6},{8,9},{9,8},{10,11... | collective-permute-start | bytes 4718600 | tf_op jit(solution)/shard_map/ppermute | solution.py:37
  195.0 36.3 %collective-permute-start.11 = (bf16[384,2048]{1,0:T(8,128)(2,1)}, bf16[384,2048]{1,0:T(8,128)(2,1)}, u32[]{:S(2)}, u32[]{:S(2)}) collective-permute-start(bf16[384,2048]{1,0:T(8,128)(2,1)} %get-tuple-element.108.p0), channel_id=1, source_target_pairs={{0,2},{2,0},{1,3},{3,1},{4,6},{6,4},{5,7},{7,5},{8,10},{10,8},{9,1... | collective-permute-start | bytes 4718600 | tf_op jit(solution)/shard_map/ppermute | solution.py:37
  202.6 64.1 %collective-permute-start.17 = (bf16[1024,1408]{1,0:T(8,128)(2,1)}, bf16[1024,1408]{1,0:T(8,128)(2,1)S(1)}, u32[]{:S(2)}, u32[]{:S(2)}) collective-permute-start(bf16[1024,1408]{1,0:T(8,128)(2,1)} %all-gather.12.cloned.1.call-done.u_own.up_w), channel_id=1, source_target_pairs={{0,4},{4,0},{1,5},{5,1},{2,6},{6,2},{3,7},{7,3},{8,12},{12,8},{9,1... | collective-permute-start | bytes 8650760 | tf_op jit(solution)/shard_map/ppermute | solution.py:37
  300.9 228.6 %reduce-scatter.8.cloned.1.call-start = ((), (), s32[]{:S(2)}) async-start(), calls=%async_computation.11 | async-start | bytes 3604480 | tf_op jit(solution)/shard_map/reduce_scatter | solution.py:585
  330.9 65.6 %collective-permute-start.29 = (bf16[1024,1408]{1,0:T(8,128)(2,1)}, bf16[1024,1408]{1,0:T(8,128)(2,1)S(1)}, u32[]{:S(2)}, u32[]{:S(2)}) collective-permute-start(bf16[1024,1408]{1,0:T(8,128)(2,1)} %shard_map.217), channel_id=1, source_target_pairs={{0,4},{4,0},{1,5},{5,1},{2,6},{6,2},{3,7},{7,3},{8,12},{12,8},{9,1... | collective-permute-start | bytes 8650760 | tf_op jit(solution)/shard_map/ppermute | solution.py:37
  383.8 73.5 %collective-permute-start.23 = (bf16[1024,1408]{1,0:T(8,128)(2,1)}, bf16[1024,1408]{1,0:T(8,128)(2,1)S(1)}, u32[]{:S(2)}, u32[]{:S(2)}) collective-permute-start(bf16[1024,1408]{1,0:T(8,128)(2,1)} %shard_map.221), channel_id=1, source_target_pairs={{0,4},{4,0},{1,5},{5,1},{2,6},{6,2},{3,7},{7,3},{8,12},{12,8},{9,1... | collective-permute-start | bytes 8650760 | tf_op jit(solution)/shard_map/ppermute | solution.py:37
  415.0 168.5 %reduce-scatter.10.cloned.1.call-start = ((), (), s32[]{:S(2)}) async-start(), calls=%async_computation.12 | async-start | bytes 3604480 | tf_op jit(solution)/shard_map/reduce_scatter | solution.py:585
  423.0 45.7 %collective-permute-start.22 = (bf16[384,2048]{1,0:T(8,128)(2,1)}, bf16[384,2048]{1,0:T(8,128)(2,1)}, u32[]{:S(2)}, u32[]{:S(2)}) collective-permute-start(bf16[384,2048]{1,0:T(8,128)(2,1)} %get-tuple-element.129.p0), channel_id=1, source_target_pairs={{0,2},{2,0},{1,3},{3,1},{4,6},{6,4},{5,7},{7,5},{8,10},{10,8},{9,1... | collective-permute-start | bytes 4718600 | tf_op jit(solution)/shard_map/ppermute | solution.py:37
  424.5 44.3 %collective-permute-start.24 = (bf16[384,2048]{1,0:T(8,128)(2,1)}, bf16[384,2048]{1,0:T(8,128)(2,1)}, u32[]{:S(2)}, u32[]{:S(2)}) collective-permute-start(bf16[384,2048]{1,0:T(8,128)(2,1)} %get-tuple-element.129.p0), channel_id=1, source_target_pairs={{0,1},{1,0},{2,3},{3,2},{4,5},{5,4},{6,7},{7,6},{8,9},{9,8},{10,11... | collective-permute-start | bytes 4718600 | tf_op jit(solution)/shard_map/ppermute | solution.py:37
  480.0 138.1 %reduce-scatter.14.cloned.1.call-start = ((), (), s32[]{:S(2)}) async-start(), calls=%async_computation.14 | async-start | bytes 1310720 | tf_op jit(solution)/shard_map/reduce_scatter | solution.py:585
  500.9 37.1 %collective-permute-start.27 = (bf16[384,2048]{1,0:T(8,128)(2,1)}, bf16[384,2048]{1,0:T(8,128)(2,1)S(1)}, u32[]{:S(2)}, u32[]{:S(2)}) collective-permute-start(bf16[384,2048]{1,0:T(8,128)(2,1)} %shard_map.227), channel_id=1, source_target_pairs={{0,2},{2,0},{1,3},{3,1},{4,6},{6,4},{5,7},{7,5},{8,10},{10,8},{9,1... | collective-permute-start | bytes 4718600 | tf_op jit(solution)/shard_map/ppermute | solution.py:37
  550.9 76.1 %reduce-scatter.12.cloned.1.call-start = ((), (), s32[]{:S(2)}) async-start(), calls=%async_computation.13 | async-start | bytes 1740800 | tf_op jit(solution)/shard_map/reduce_scatter | solution.py:585
  (58 other events, 592.7 us)
Sparse Core Ops, SparseCore 0:
  11.7 36.7 all-gather.5
  50.6 26.8 all-gather.9
  79.1 58.6 all-gather.7
  139.2 57.8 all-gather.11
  199.1 105.3 all-gather.13
  306.7 100.5 reduce-scatter.5
  415.1 53.3 reduce-scatter.7
  480.1 54.4 reduce-scatter.9
  551.0 23.9 reduce-scatter.13
  590.8 29.9 reduce-scatter.11

commit v6 on v5

--- a/solution.py
+++ b/solution.py
@@ -17,7 +17,7 @@
 BF16 = jnp.bfloat16
 SWAP = [(0, 1), (1, 0)]
 COST = {1: 1702, 2: 2220, 3: 2582, 4: 5630, 5: 1730, 6: 798, 7: 1730, 8: 798, 9: 1498, 10: 1626, 11: 4596, 12: 3950, 13: 4338, 14: 3898, 15: 798, 16: 2348, 17: 3872, 18: 798, 19: 2348, 20: 1986, 21: 3820, 22: 1006, 23: 2556, 24: 1626, 25: 2142, 26: 8118, 27: 127702, 28: 10228, 38: 3898}
-SKIP = {161, 103, 136, 137, 107, 139, 140, 142, 116, 150, 120, 122, 158, 159}
+SKIP = {136, 137, 139, 140, 142, 150, 158, 159, 161, 103, 170, 107, 174, 116, 120, 122}
 ROW_PAD = 16
 
 
@@ -671,9 +671,10 @@
     first_oth = scatter_rows(30, *oth_parts)
     qkv_sent = weight_grad(31, seq_one[1], after(167, after(161, after(130, qkv_g, oth_parts[0]), first_oth[3]), block_terms[2]))
     qkv_came = swap_x(after(134, qkv_sent, out_came))
-    out_total = weight_grad(34, seq_attn[0], mixed, after(132, out_came, qkv_sent))
+    out_total = weight_grad(34, seq_attn[0], mixed, after(174, after(132, out_came, qkv_sent), first_oth[3]))
     grad_out = reduce_z(out_total)
-    own_parts, own_gain = project_gain(32, 0, after(131, qkv_g, out_total))
+    own_parts, own_gain = project_gain(32, 0, after(173, after(131, qkv_g, out_total), first_oth[3]))
+    first_own = scatter_rows(33, *own_parts)
     qkv_near = weight_grad(35, seq_one[0], after(133, qkv_g, own_parts[0]), kind=F32)
 
     def gain_pair(one, two):
@@ -689,11 +690,10 @@
         total_kernel,
         [],
         hi,
-        tiles_of(depth, qkv_near, after(152, after(151, after(135, qkv_came, grad_up), first_oth[2]), qkv_near))
+        tiles_of(depth, qkv_near, after(170, after(152, after(151, after(135, qkv_came, grad_up), first_oth[2]), qkv_near), first_own[3]))
         + tiles_of(ROW_PAD, gain_rows.reshape(hi * ROW_PAD, all_cols)),
         [((hi * (depth + ROW_PAD), all_cols), BF16, row_spec(depth + ROW_PAD, all_cols))],
     )
-    first_own = scatter_rows(33, own_parts[0], after(166, own_parts[1], qkv_total))
     grad_qkv = reduce_z(qkv_total).astype(F32)
     gain_sums = grad_qkv[depth, : 2 * depth]
     gain_sums = gain_sums + swap(gain_sums, "th")
@@ -715,7 +715,12 @@
         half_ins(x_own, x_oth) + terms(first_own, first_oth) + gain_in(gain_one) + half_ins(r_own, r_oth),
         whole_out,
     )
-    grad_down = grad_down[:depth].astype(F32) + swap_x(grad_down[depth:]).astype(F32)
+    down_came = swap_x(grad_down[depth:])
+    if 171 not in SKIP:
+        down_came, block_out, grad_in = lax.optimization_barrier((down_came, block_out, grad_in))
+    elif 172 not in SKIP:
+        down_came, block_out = lax.optimization_barrier((down_came, block_out))
+    grad_down = grad_down[:depth].astype(F32) + down_came.astype(F32)
     return (
         block_out.reshape(block_in.shape),
         grad_in.reshape(block_in.shape),

time: 646 us -> 642 us (level)
  waiting for transfers between devices: 187 us -> 180 us
    ppermute x39, waiting for transfers between devices: 151 us -> 144 us  [swap(): return lax.ppermute(value, axis, SWAP)]
    unnamed x77 -> x75, local copies, waits for them, and re-layouts: 25.1 us -> 27 us
  transfers between devices with their start and end apart: 49 -> 49, of which waited for: 25 -> 23; matrix products, arithmetic and copies ran while one was open for 5% -> 5% of each run, Pallas kernels for 55% -> 56%
where the time goes in v6:
time: 642 us; the launch traced here: 636 us
  Pallas kernels  353 us (55%)
  waiting for transfers between devices  180 us (28%)
  local copies, waits for them, and re-layouts  41.6 us (6%)
  starting transfers between devices  32.1 us (5%)
  between operations  14.8 us (2%)
  other arithmetic  13.6 us (2%)
    pallas_call x39, Pallas kernels, call(): pl.pallas_call(kernel, out_shape=[jax.ShapeDtypeStruct(shape, kind) for s...  353 us
    ppermute x39, waiting for transfers between devices, swap(): return lax.ppermute(value, axis, SWAP)  144 us
    all_gather x5, waiting for transfers between devices, gather(): return lax.all_gather(part, 'fh', axis=0, tiled=True)  35 us
    ppermute x39, starting transfers between devices, swap(): return lax.ppermute(value, axis, SWAP)  30.5 us
    unnamed x75, local copies, waits for them, and re-layouts  27 us
  transfers between devices with their start and end apart: 49, of which 23 were waited for; matrix products, arithmetic and copies ran while one was open for 5% of the time, Pallas kernels for 56%

profile of v6, /device:TPU:0, one launch (start us, length us, event | category | flops | bytes accessed | tf_op | source)
XLA Modules:
  0.0 635.7 jit_solution(11450256361282687249)
XLA Ops:
  19.7 14.6 %collective-permute-done.6 = bf16[256,1408]{1,0:T(8,128)(2,1)S(1)} collective-permute-done((bf16[256,1408]{1,0:T(8,128)(2,1)S(1)}, bf16[256,1408]{1,0:T(8,128)(2,1)S(1)}, u32[]{:S(2)}, u32[]{:S(2)}) %collective-permute-start.6) | collective-permute-done | bytes 720928 | tf_op jit(solution)/shard_map/ppermute | solution.py:37
  35.5 13.0 %all-gather.6.cloned.1.call-done = bf16[1088,640]{1,0:T(8,128)(2,1)} async-done(((bf16[272,640]{1,0:T(8,128)(2,1)}), bf16[1088,640]{1,0:T(8,128)(2,1)}) %all-gather.6.cloned.1.call-update) | async-done | bytes 1392656 | tf_op jit(solution)/shard_map/all_gather | solution.py:422
  60.1 17.5 %all-gather.10.cloned.1.call-done.weight.w_own = bf16[1024,512]{1,0:T(8,128)(2,1)} async-done(((bf16[256,512]{1,0:T(8,128)(2,1)}), bf16[1024,512]{1,0:T(8,128)(2,1)}) %all-gather.10.cloned.1.call-update) | async-done | bytes 1048592 | tf_op jit(solution)/shard_map/all_gather | solution.py:422
  89.6 8.6 %shard_map.204 = (bf16[4,3,128,1024]{3,2,1,0:T(8,128)(2,1)}, bf16[4,3,128,1024]{3,2,1,0:T(8,128)(2,1)}, bf16[384,1024]{1,0:T(8,128)(2,1)}, bf16[384,1024]{1,0:T(8,128)(2,1)}) custom-call(s32[1]{0:T(128)} %bitcast.at, bf16[384,2048]{1,0:T(8,128)(2,1)} %bitcast.98, bf16[384,2048]{1,0:T(8,128)(2,1)} %collective-permute-done.p1, ...), custom_call_target="tpu_custom_call" | custom-call | flops 666000000 | bytes 2220002 | tf_op jit(solution)/shard_map/pallas_call | solution.py:71
  98.3 10.0 %shard_map.205 = f32[1536,640]{1,0:T(8,128)} custom-call(bf16[1536,1024]{1,0:T(8,128)(2,1)} %bitcast.77, bf16[1536,1024]{1,0:T(8,128)(2,1)} %bitcast.74, bf16[1024,640]{1,0:T(8,128)(2,1)} %bitcast.86, bf16[1024,640]{1,0:T(8,128)(2,1)} %bitcast.88), custom_call_target="tpu_custom_call" | custom-call | flops 774600000 | bytes 2582003 | tf_op jit(solution)/shard_map/pallas_call | solution.py:71
  108.2 21.5 %shard_map.206 = (bf16[4,3,128,512]{3,2,1,0:T(8,128)(2,1)}, bf16[4,3,128,128]{3,2,1,0:T(8,128)(2,1)}, bf16[4,3,128,512]{3,2,1,0:T(8,128)(2,1)}, f32[3,8,512]{2,1,0:T(8,128)}) custom-call(s32[3]{0:T(128)} %bitcast.119, f32[4,3,128,640]{3,2,1,0:T(8,128)} %bitcast.90, f32[512,128]{1,0:T(8,128)} %copy.56.cos, f32[512,128]{1,0:T(8,128)} %pad_maximum_fusion.1.sine, ...), custom_call_target="tpu_custom_call" | custom-call | flops 1688999936 | bytes 5630004 | tf_op jit(solution)/shard_map/pallas_call | solution.py:71
  162.5 9.4 %collective-permute-done.12.b2 = bf16[384,1024]{1,0:T(8,128)(2,1)S(1)} collective-permute-done((bf16[384,1024]{1,0:T(8,128)(2,1)S(1)}, bf16[384,1024]{1,0:T(8,128)(2,1)S(1)}, u32[]{:S(2)}, u32[]{:S(2)}) %collective-permute-start.12) | collective-permute-done | bytes 786464 | tf_op jit(solution)/shard_map/ppermute | solution.py:37
  171.9 16.3 %collective-permute-done.11.a2 = bf16[384,1024]{1,0:T(8,128)(2,1)S(1)} collective-permute-done((bf16[384,1024]{1,0:T(8,128)(2,1)}, bf16[384,1024]{1,0:T(8,128)(2,1)S(1)}, u32[]{:S(2)}, u32[]{:S(2)}) %collective-permute-start.11) | collective-permute-done | bytes 786464 | tf_op jit(solution)/shard_map/ppermute | solution.py:37
  210.5 20.7 %collective-permute-done.13.p1 = bf16[384,2048]{1,0:T(8,128)(2,1)} collective-permute-done((bf16[384,2048]{1,0:T(8,128)(2,1)}, bf16[384,2048]{1,0:T(8,128)(2,1)}, u32[]{:S(2)}, u32[]{:S(2)}) %collective-permute-start.13) | collective-permute-done | bytes 1572896 | tf_op jit(solution)/shard_map/ppermute | solution.py:37
  242.3 15.1 %shard_map.213.gate_in = f32[1536,1408]{1,0:T(8,128)} custom-call(bf16[1536,1024]{1,0:T(8,128)(2,1)} %bitcast.62, bf16[1536,1024]{1,0:T(8,128)(2,1)} %bitcast.66, bf16[1024,1408]{1,0:T(8,128)(2,1)} %all-gather.8.cloned.1.call-done.w_own.gate_w, bf16[1024,1408]{1,0:T(8,128)(2,1)} %copy-done.1), custom_call_target="tpu_custom_call" | custom-call | flops 1169400064 | bytes 3898038 | tf_op jit(solution)/shard_map/pallas_call | solution.py:71
  257.4 9.3 %collective-permute-done.17.u_oth.up_w = bf16[1024,1408]{1,0:T(8,128)(2,1)S(1)} collective-permute-done((bf16[1024,1408]{1,0:T(8,128)(2,1)}, bf16[1024,1408]{1,0:T(8,128)(2,1)S(1)}, u32[]{:S(2)}, u32[]{:S(2)}) %collective-permute-start.17) | collective-permute-done | bytes 2883616 | tf_op jit(solution)/shard_map/ppermute | solution.py:37
  268.3 17.8 %shard_map.214 = (bf16[1536,1408]{1,0:T(8,128)(2,1)}, bf16[1536,1408]{1,0:T(8,128)(2,1)}, bf16[1536,1408]{1,0:T(8,128)(2,1)}) custom-call(bf16[1536,1024]{1,0:T(8,128)(2,1)} %bitcast.63, bf16[1536,1024]{1,0:T(8,128)(2,1)} %bitcast.67, bf16[1024,1408]{1,0:T(8,128)(2,1)} %all-gather.12.cloned.1.call-done.u_own.up_w, bf16[1024,1408]{1,0:T(8,128)(2,1)} %copy-done.2, ...), custom_call_target="tpu_custom_call" | custom-call | flops 1378800000 | bytes 4596011 | tf_op jit(solution)/shard_map/pallas_call | solution.py:71
  286.0 14.8 %shard_map.215 = bf16[2048,1408]{1,0:T(8,128)(2,1)} custom-call(bf16[1536,2048]{1,0:T(8,128)(2,1)} %bitcast.60, bf16[1536,1408]{1,0:T(8,128)(2,1)} %get-tuple-element.133.grad.rows), custom_call_target="tpu_custom_call" | custom-call | flops 1184999936 | bytes 3950012 | tf_op jit(solution)/shard_map/pallas_call | solution.py:71
  304.6 17.2 %shard_map.216 = (bf16[1536,1408]{1,0:T(8,128)(2,1)}, bf16[1536,1408]{1,0:T(8,128)(2,1)}) custom-call(bf16[1536,2048]{1,0:T(8,128)(2,1)} %bitcast.61, bf16[2048,1408]{1,0:T(8,128)(2,1)} %all-gather.14.cloned.1.call-done.weight, bf16[1536,1408]{1,0:T(8,128)(2,1)} %get-tuple-element.120.for_gate, bf16[1536,1408]{1,0:T(8,128)(2,1)} %get-tuple-element.121.for_up), custom_call_target="tpu_custom_call" | custom-call | flops 1301400064 | bytes 4338013 | tf_op jit(solution)/shard_map/pallas_call | solution.py:71
  321.7 9.2 %shard_map.217 = bf16[1024,1408]{1,0:T(8,128)(2,1)} custom-call(bf16[1536,1024]{1,0:T(8,128)(2,1)} %bitcast.68, bf16[1536,1408]{1,0:T(8,128)(2,1)} %get-tuple-element.126.grad.gate_g), custom_call_target="tpu_custom_call" | custom-call | flops 704400000 | bytes 2348016 | tf_op jit(solution)/shard_map/pallas_call | solution.py:71
  332.4 15.6 %shard_map.218 = (bf16[768,1024]{1,0:T(8,128)(2,1)}, bf16[768,1024]{1,0:T(8,128)(2,1)}) custom-call(bf16[1536,1408]{1,0:T(8,128)(2,1)} %get-tuple-element.126.grad.gate_g, bf16[1536,1408]{1,0:T(8,128)(2,1)} %get-tuple-element.129.up_g.grad, bf16[1024,1408]{1,0:T(8,128)(2,1)} %copy-done.1, bf16[1024,1408]{1,0:T(8,128)(2,1)} %copy-done.2), custom_call_target="tpu_custom_call" | custom-call | flops 1169400064 | bytes 3898014 | tf_op jit(solution)/shard_map/pallas_call | solution.py:71
  348.0 15.7 %shard_map.219 = (bf16[768,1024]{1,0:T(8,128)(2,1)}, bf16[768,1024]{1,0:T(8,128)(2,1)}) custom-call(bf16[1536,1408]{1,0:T(8,128)(2,1)} %get-tuple-element.126.grad.gate_g, bf16[1536,1408]{1,0:T(8,128)(2,1)} %get-tuple-element.129.up_g.grad, bf16[1024,1408]{1,0:T(8,128)(2,1)} %all-gather.8.cloned.1.call-done.w_own.gate_w, ...), custom_call_target="tpu_custom_call" | custom-call | flops 1161600000 | bytes 3872017 | tf_op jit(solution)/shard_map/pallas_call | solution.py:71
  374.7 9.1 %shard_map.221 = bf16[1024,1408]{1,0:T(8,128)(2,1)} custom-call(bf16[1536,1024]{1,0:T(8,128)(2,1)} %bitcast.69, bf16[1536,1408]{1,0:T(8,128)(2,1)} %get-tuple-element.129.up_g.grad), custom_call_target="tpu_custom_call" | custom-call | flops 704400000 | bytes 2348019 | tf_op jit(solution)/shard_map/pallas_call | solution.py:71
  384.3 12.1 %collective-permute-done.30.came = bf16[1024,1408]{1,0:T(8,128)(2,1)S(1)} collective-permute-done((bf16[1024,1408]{1,0:T(8,128)(2,1)}, bf16[1024,1408]{1,0:T(8,128)(2,1)S(1)}, u32[]{:S(2)}, u32[]{:S(2)}) %collective-permute-start.30) | collective-permute-done | bytes 2883616 | tf_op jit(solution)/shard_map/ppermute | solution.py:37
  405.0 9.9 %shard_map.232 = bf16[1024,1408]{1,0:T(8,128)(2,1)} custom-call(bf16[1536,1024]{1,0:T(8,128)(2,1)} %bitcast.64, bf16[1536,1408]{1,0:T(8,128)(2,1)} %get-tuple-element.126.grad.gate_g, bf16[1024,1408]{1,0:T(8,128)(2,1)} %copy-done.10), custom_call_target="tpu_custom_call" | custom-call | flops 766800000 | bytes 2556023 | tf_op jit(solution)/shard_map/pallas_call | solution.py:71
  424.5 16.0 %shard_map.224 = (bf16[768,2048]{1,0:T(8,128)(2,1)}, bf16[768,2048]{1,0:T(8,128)(2,1)}) custom-call(bf16[1536,1408]{1,0:T(8,128)(2,1)} %get-tuple-element.133.grad.rows, bf16[2048,1408]{1,0:T(8,128)(2,1)} %all-gather.14.cloned.1.call-done.weight), custom_call_target="tpu_custom_call" | custom-call | flops 1146000000 | bytes 3820021 | tf_op jit(solution)/shard_map/pallas_call | solution.py:71
  440.5 16.8 %collective-permute-done.24.came = bf16[1024,1408]{1,0:T(8,128)(2,1)S(1)} collective-permute-done((bf16[1024,1408]{1,0:T(8,128)(2,1)}, bf16[1024,1408]{1,0:T(8,128)(2,1)S(1)}, u32[]{:S(2)}, u32[]{:S(2)}) %collective-permute-start.24) | collective-permute-done | bytes 2883616 | tf_op jit(solution)/shard_map/ppermute | solution.py:37
  458.9 9.9 %shard_map.225 = bf16[1024,1408]{1,0:T(8,128)(2,1)} custom-call(bf16[1536,1024]{1,0:T(8,128)(2,1)} %bitcast.65, bf16[1536,1408]{1,0:T(8,128)(2,1)} %get-tuple-element.129.up_g.grad, bf16[1024,1408]{1,0:T(8,128)(2,1)} %copy-done.9), custom_call_target="tpu_custom_call" | custom-call | flops 3068400128 | bytes 10228028 | tf_op jit(solution)/shard_map/pallas_call | solution.py:71
  502.3 27.1 %shard_map.230 = bf16[4,3,128,640]{3,2,1,0:T(8,128)(2,1)} custom-call(s32[3]{0:T(128)} %bitcast.120, bf16[4,3,128,512]{3,2,1,0:T(8,128)(2,1)} %get-tuple-element.142.query_in, bf16[4,3,128,128]{3,2,1,0:T(8,128)(2,1)} %get-tuple-element.143.kv_in, bf16[4,3,128,512]{3,2,1,0:T(8,128)(2,1)} %bitcast.97, bf16[4,3,128,512]{3,2,1,0:T(8,128)(2,1)} %get-tuple-element.102.mixed_in, ...), custom_call_target="tpu_custom_call" | custom-call | flops 38310600704 | bytes 127702024 | tf_op jit(solution)/shard_map/pallas_call | solution.py:71
  (246 shorter events, 273.7 us)
Async XLA Ops:
  7.2 41.3 %all-gather.6.cloned.1.call-start = ((), (), s32[]{:S(2)}) async-start(), calls=%async_computation.5 | async-start | bytes 1740800 | tf_op jit(solution)/shard_map/all_gather | solution.py:422
  11.5 66.0 %all-gather.10.cloned.1.call-start = ((), (), s32[]{:S(2)}) async-start(), calls=%async_computation.7 | async-start | bytes 1310720 | tf_op jit(solution)/shard_map/all_gather | solution.py:422
  13.4 124.4 %all-gather.8.cloned.1.call-start = ((), (), s32[]{:S(2)}) async-start(), calls=%async_computation.6 | async-start | bytes 3604480 | tf_op jit(solution)/shard_map/all_gather | solution.py:422
  14.2 183.0 %all-gather.12.cloned.1.call-start = ((), (), s32[]{:S(2)}) async-start(), calls=%async_computation.8 | async-start | bytes 3604480 | tf_op jit(solution)/shard_map/all_gather | solution.py:422
  14.7 289.8 %all-gather.14.cloned.1.call-start = ((), (), s32[]{:S(2)}) async-start(), calls=%async_computation.10 | async-start | bytes 7208960 | tf_op jit(solution)/shard_map/all_gather | solution.py:422
  18.1 36.0 %collective-permute-start = (bf16[384,2048]{1,0:T(8,128)(2,1)S(1)}, bf16[384,2048]{1,0:T(8,128)(2,1)}, u32[]{:S(2)}, u32[]{:S(2)}) collective-permute-start(bf16[384,2048]{1,0:T(8,128)(2,1)S(1)} %bitcast.99), channel_id=1, source_target_pairs={{0,2},{2,0},{1,3},{3,1},{4,6},{6,4},{5,7},{7,5},{8,10},{10,8},{9,1... | collective-permute-start | bytes 4718600 | tf_op jit(solution)/shard_map/ppermute | solution.py:37
  50.0 39.7 %collective-permute-start.4 = (bf16[384,2048]{1,0:T(8,128)(2,1)S(1)}, bf16[384,2048]{1,0:T(8,128)(2,1)}, u32[]{:S(2)}, u32[]{:S(2)}) collective-permute-start(bf16[384,2048]{1,0:T(8,128)(2,1)S(1)} %bitcast.100), channel_id=1, source_target_pairs={{0,1},{1,0},{2,3},{3,2},{4,5},{5,4},{6,7},{7,6},{8,9},{9,8},{10,11... | collective-permute-start | bytes 4718600 | tf_op jit(solution)/shard_map/ppermute | solution.py:37
  54.1 54.1 %collective-permute-start.1 = (bf16[384,2048]{1,0:T(8,128)(2,1)}, bf16[384,2048]{1,0:T(8,128)(2,1)}, u32[]{:S(2)}, u32[]{:S(2)}) collective-permute-start(bf16[384,2048]{1,0:T(8,128)(2,1)} %bitcast.1.p0.upstream), channel_id=1, source_target_pairs={{0,2},{2,0},{1,3},{3,1},{4,6},{6,4},{5,7},{7,5},{8,10},{10,8},{9,1... | collective-permute-start | bytes 4718600 | tf_op jit(solution)/shard_map/ppermute | solution.py:37
  59.5 397.8 %reduce-scatter.6.cloned.1.call-start = ((), (), s32[]{:S(2)}) async-start(), calls=%async_computation.9 | async-start | bytes 7208960 | tf_op jit(solution)/shard_map/reduce_scatter | solution.py:585
  80.4 49.4 %collective-permute-start.8 = (bf16[1024,512]{1,0:T(8,128)(2,1)}, bf16[1024,512]{1,0:T(8,128)(2,1)S(1)}, u32[]{:S(2)}, u32[]{:S(2)}) collective-permute-start(bf16[1024,512]{1,0:T(8,128)(2,1)} %all-gather.10.cloned.1.call-done.weight.w_own), channel_id=1, source_target_pairs={{0,4},{4,0},{1,5},{5,1},{2,6},{6,2},{3,7},{7,3},{8,12},{12,8},{9,1... | collective-permute-start | bytes 3145736 | tf_op jit(solution)/shard_map/ppermute | solution.py:37
  137.8 64.8 %collective-permute-start.14 = (bf16[1024,1408]{1,0:T(8,128)(2,1)}, bf16[1024,1408]{1,0:T(8,128)(2,1)S(1)}, u32[]{:S(2)}, u32[]{:S(2)}) collective-permute-start(bf16[1024,1408]{1,0:T(8,128)(2,1)} %all-gather.8.cloned.1.call-done.w_own.gate_w), channel_id=1, source_target_pairs={{0,4},{4,0},{1,5},{5,1},{2,6},{6,2},{3,7},{7,3},{8,12},{12,8},{9,1... | collective-permute-start | bytes 8650760 | tf_op jit(solution)/shard_map/ppermute | solution.py:37
  160.8 42.9 %collective-permute-start.2 = (bf16[384,2048]{1,0:T(8,128)(2,1)}, bf16[384,2048]{1,0:T(8,128)(2,1)}, u32[]{:S(2)}, u32[]{:S(2)}) collective-permute-start(bf16[384,2048]{1,0:T(8,128)(2,1)} %bitcast.1.p0.upstream), channel_id=1, source_target_pairs={{0,1},{1,0},{2,3},{3,2},{4,5},{5,4},{6,7},{7,6},{8,9},{9,8},{10,11... | collective-permute-start | bytes 4718600 | tf_op jit(solution)/shard_map/ppermute | solution.py:37
  160.8 42.9 %collective-permute-start.3 = (bf16[384,2048]{1,0:T(8,128)(2,1)}, bf16[384,2048]{1,0:T(8,128)(2,1)}, u32[]{:S(2)}, u32[]{:S(2)}) collective-permute-start(bf16[384,2048]{1,0:T(8,128)(2,1)} %collective-permute-done.1.p1), channel_id=1, source_target_pairs={{0,1},{1,0},{2,3},{3,2},{4,5},{5,4},{6,7},{7,6},{8,9},{9,8},{10,11... | collective-permute-start | bytes 4718600 | tf_op jit(solution)/shard_map/ppermute | solution.py:37
  194.9 36.3 %collective-permute-start.13 = (bf16[384,2048]{1,0:T(8,128)(2,1)}, bf16[384,2048]{1,0:T(8,128)(2,1)}, u32[]{:S(2)}, u32[]{:S(2)}) collective-permute-start(bf16[384,2048]{1,0:T(8,128)(2,1)} %get-tuple-element.109.p0), channel_id=1, source_target_pairs={{0,2},{2,0},{1,3},{3,1},{4,6},{6,4},{5,7},{7,5},{8,10},{10,8},{9,1... | collective-permute-start | bytes 4718600 | tf_op jit(solution)/shard_map/ppermute | solution.py:37
  202.6 64.1 %collective-permute-start.17 = (bf16[1024,1408]{1,0:T(8,128)(2,1)}, bf16[1024,1408]{1,0:T(8,128)(2,1)S(1)}, u32[]{:S(2)}, u32[]{:S(2)}) collective-permute-start(bf16[1024,1408]{1,0:T(8,128)(2,1)} %all-gather.12.cloned.1.call-done.u_own.up_w), channel_id=1, source_target_pairs={{0,4},{4,0},{1,5},{5,1},{2,6},{6,2},{3,7},{7,3},{8,12},{12,8},{9,1... | collective-permute-start | bytes 8650760 | tf_op jit(solution)/shard_map/ppermute | solution.py:37
  300.8 228.7 %reduce-scatter.8.cloned.1.call-start = ((), (), s32[]{:S(2)}) async-start(), calls=%async_computation.11 | async-start | bytes 3604480 | tf_op jit(solution)/shard_map/reduce_scatter | solution.py:585
  330.9 65.6 %collective-permute-start.30 = (bf16[1024,1408]{1,0:T(8,128)(2,1)}, bf16[1024,1408]{1,0:T(8,128)(2,1)S(1)}, u32[]{:S(2)}, u32[]{:S(2)}) collective-permute-start(bf16[1024,1408]{1,0:T(8,128)(2,1)} %shard_map.217), channel_id=1, source_target_pairs={{0,4},{4,0},{1,5},{5,1},{2,6},{6,2},{3,7},{7,3},{8,12},{12,8},{9,1... | collective-permute-start | bytes 8650760 | tf_op jit(solution)/shard_map/ppermute | solution.py:37
  383.8 73.5 %collective-permute-start.24 = (bf16[1024,1408]{1,0:T(8,128)(2,1)}, bf16[1024,1408]{1,0:T(8,128)(2,1)S(1)}, u32[]{:S(2)}, u32[]{:S(2)}) collective-permute-start(bf16[1024,1408]{1,0:T(8,128)(2,1)} %shard_map.221), channel_id=1, source_target_pairs={{0,4},{4,0},{1,5},{5,1},{2,6},{6,2},{3,7},{7,3},{8,12},{12,8},{9,1... | collective-permute-start | bytes 8650760 | tf_op jit(solution)/shard_map/ppermute | solution.py:37
  415.0 168.4 %reduce-scatter.10.cloned.1.call-start = ((), (), s32[]{:S(2)}) async-start(), calls=%async_computation.12 | async-start | bytes 3604480 | tf_op jit(solution)/shard_map/reduce_scatter | solution.py:585
  422.9 45.9 %collective-permute-start.23 = (bf16[384,2048]{1,0:T(8,128)(2,1)}, bf16[384,2048]{1,0:T(8,128)(2,1)}, u32[]{:S(2)}, u32[]{:S(2)}) collective-permute-start(bf16[384,2048]{1,0:T(8,128)(2,1)} %get-tuple-element.132.p0), channel_id=1, source_target_pairs={{0,2},{2,0},{1,3},{3,1},{4,6},{6,4},{5,7},{7,5},{8,10},{10,8},{9,1... | collective-permute-start | bytes 4718600 | tf_op jit(solution)/shard_map/ppermute | solution.py:37
  424.5 44.3 %collective-permute-start.25 = (bf16[384,2048]{1,0:T(8,128)(2,1)}, bf16[384,2048]{1,0:T(8,128)(2,1)}, u32[]{:S(2)}, u32[]{:S(2)}) collective-permute-start(bf16[384,2048]{1,0:T(8,128)(2,1)} %get-tuple-element.132.p0), channel_id=1, source_target_pairs={{0,1},{1,0},{2,3},{3,2},{4,5},{5,4},{6,7},{7,6},{8,9},{9,8},{10,11... | collective-permute-start | bytes 4718600 | tf_op jit(solution)/shard_map/ppermute | solution.py:37
  480.0 123.2 %reduce-scatter.14.cloned.1.call-start = ((), (), s32[]{:S(2)}) async-start(), calls=%async_computation.14 | async-start | bytes 1310720 | tf_op jit(solution)/shard_map/reduce_scatter | solution.py:585
  500.9 37.0 %collective-permute-start.28 = (bf16[384,2048]{1,0:T(8,128)(2,1)}, bf16[384,2048]{1,0:T(8,128)(2,1)S(1)}, u32[]{:S(2)}, u32[]{:S(2)}) collective-permute-start(bf16[384,2048]{1,0:T(8,128)(2,1)} %shard_map.227), channel_id=1, source_target_pairs={{0,2},{2,0},{1,3},{3,1},{4,6},{6,4},{5,7},{7,5},{8,10},{10,8},{9,1... | collective-permute-start | bytes 4718600 | tf_op jit(solution)/shard_map/ppermute | solution.py:37
  550.8 72.0 %reduce-scatter.12.cloned.1.call-start = ((), (), s32[]{:S(2)}) async-start(), calls=%async_computation.13 | async-start | bytes 1740800 | tf_op jit(solution)/shard_map/reduce_scatter | solution.py:585
  (57 other events, 603.5 us)
Sparse Core Ops, SparseCore 0:
  11.7 36.7 all-gather.5
  50.6 26.8 all-gather.9
  79.1 58.6 all-gather.7
  139.2 57.8 all-gather.11
  199.1 105.3 all-gather.13
  306.7 100.5 reduce-scatter.5
  415.1 53.3 reduce-scatter.7
  480.1 54.2 reduce-scatter.9
  551.0 23.9 reduce-scatter.13
  588.7 29.0 reduce-scatter.11

commit v7 on v6

--- a/solution.py
+++ b/solution.py
@@ -79,7 +79,7 @@
             scratch_shapes=list(scratch),
         ),
         cost_estimate=pl.CostEstimate(flops=work * 300, bytes_accessed=work + step, transcendentals=0),
-        compiler_params=pltpu.CompilerParams(vmem_limit_bytes=56 << 20),
+        compiler_params=pltpu.CompilerParams(vmem_limit_bytes=30 << 20),
     )(*scalars, *[a for a, _ in ins])
 
 

time: 642 us -> 636 us (level)
  Pallas kernels: 353 us -> 254 us
  local copies, waits for them, and re-layouts: 41.6 us -> 112 us
  waiting for transfers between devices: 180 us -> 202 us
    pallas_call x39, Pallas kernels: 353 us -> 254 us  [call(): pl.pallas_call(kernel, out_shape=[jax.ShapeDtypeStruct(shape, kind) for s...]
    unnamed x75 -> x241, local copies, waits for them, and re-layouts: 27 us -> 99.4 us
    ppermute x39, waiting for transfers between devices: 144 us -> 156 us  [swap(): return lax.ppermute(value, axis, SWAP)]
    all_gather x5, waiting for transfers between devices: 35 us -> 44 us  [gather(): return lax.all_gather(part, 'fh', axis=0, tiled=True)]
  transfers between devices with their start and end apart: 49 -> 49, of which waited for: 23 -> 21; matrix products, arithmetic and copies ran while one was open for 5% -> 5% of each run, Pallas kernels for 56% -> 40%
where the time goes in v7:
time: 636 us; the launch traced here: 631 us
  Pallas kernels  254 us (40%)
  waiting for transfers between devices  202 us (32%)
  local copies, waits for them, and re-layouts  112 us (18%)
  starting transfers between devices  31.9 us (5%)
  other arithmetic  15.9 us (2%)
  between operations  15.6 us (2%)
    pallas_call x39, Pallas kernels, call(): pl.pallas_call(kernel, out_shape=[jax.ShapeDtypeStruct(shape, kind) for s...  254 us
    ppermute x39, waiting for transfers between devices, swap(): return lax.ppermute(value, axis, SWAP)  156 us
    unnamed x241, local copies, waits for them, and re-layouts  99.4 us
    all_gather x5, waiting for transfers between devices, gather(): return lax.all_gather(part, 'fh', axis=0, tiled=True)  44 us
    ppermute x39, starting transfers between devices, swap(): return lax.ppermute(value, axis, SWAP)  31.5 us
  transfers between devices with their start and end apart: 49, of which 21 were waited for; matrix products, arithmetic and copies ran while one was open for 5% of the time, Pallas kernels for 40%

profile of v7, /device:TPU:0, one launch (start us, length us, event | category | flops | bytes accessed | tf_op | source)
XLA Modules:
  0.0 630.5 jit_solution(17645606768078487282)
XLA Ops:
  20.4 14.8 %collective-permute-done.6 = bf16[256,1408]{1,0:T(8,128)(2,1)S(1)} collective-permute-done((bf16[256,1408]{1,0:T(8,128)(2,1)}, bf16[256,1408]{1,0:T(8,128)(2,1)S(1)}, u32[]{:S(2)}, u32[]{:S(2)}) %collective-permute-start.6) | collective-permute-done | bytes 720928 | tf_op jit(solution)/shard_map/ppermute | solution.py:37
  37.5 11.0 %all-gather.6.cloned.1.call-done = bf16[1088,640]{1,0:T(8,128)(2,1)} async-done(((bf16[272,640]{1,0:T(8,128)(2,1)}), bf16[1088,640]{1,0:T(8,128)(2,1)}) %all-gather.6.cloned.1.call-update) | async-done | bytes 1392656 | tf_op jit(solution)/shard_map/all_gather | solution.py:422
  61.7 15.8 %all-gather.10.cloned.1.call-done.weight.w_own = bf16[1024,512]{1,0:T(8,128)(2,1)} async-done(((bf16[256,512]{1,0:T(8,128)(2,1)}), bf16[1024,512]{1,0:T(8,128)(2,1)}) %all-gather.10.cloned.1.call-update) | async-done | bytes 1048592 | tf_op jit(solution)/shard_map/all_gather | solution.py:422
  86.9 6.9 %shard_map.204 = (bf16[4,3,128,1024]{3,2,1,0:T(8,128)(2,1)S(1)}, bf16[4,3,128,1024]{3,2,1,0:T(8,128)(2,1)S(1)}, bf16[384,1024]{1,0:T(8,128)(2,1)S(1)}, bf16[384,1024]{1,0:T(8,128)(2,1)S(1)}) custom-call(s32[1]{0:T(128)} %bitcast.at, bf16[384,2048]{1,0:T(8,128)(2,1)S(1)} %bitcast.102, bf16[384,2048]{1,0:T(8,128)(2,1)} %collective-permute-done.p1, ...), custom_call_target="tpu_custom_call" | custom-call | flops 666000000 | bytes 2220002 | tf_op jit(solution)/shard_map/pallas_call | solution.py:71
  99.9 19.3 %shard_map.206 = (bf16[4,3,128,512]{3,2,1,0:T(8,128)(2,1)S(1)}, bf16[4,3,128,128]{3,2,1,0:T(8,128)(2,1)S(1)}, bf16[4,3,128,512]{3,2,1,0:T(8,128)(2,1)S(1)}, f32[3,8,512]{2,1,0:T(8,128)S(1)}) custom-call(s32[3]{0:T(128)S(1)} %bitcast.113, f32[4,3,128,640]{3,2,1,0:T(8,128)S(1)} %bitcast.96, f32[512,128]{1,0:T(8,128)S(1)} %copy-done.94, ...), custom_call_target="tpu_custom_call" | custom-call | flops 1688999936 | bytes 5630004 | tf_op jit(solution)/shard_map/pallas_call | solution.py:71
  127.2 10.6 %all-gather.8.cloned.1.call-done.w_own.gate_w = bf16[1024,1408]{1,0:T(8,128)(2,1)} async-done(((bf16[256,1408]{1,0:T(8,128)(2,1)}), bf16[1024,1408]{1,0:T(8,128)(2,1)}) %all-gather.8.cloned.1.call-update) | async-done | bytes 2883600 | tf_op jit(solution)/shard_map/all_gather | solution.py:422
  151.8 14.7 %collective-permute-done.12.b2 = bf16[384,1024]{1,0:T(8,128)(2,1)S(1)} collective-permute-done((bf16[384,1024]{1,0:T(8,128)(2,1)S(1)}, bf16[384,1024]{1,0:T(8,128)(2,1)S(1)}, u32[]{:S(2)}, u32[]{:S(2)}) %collective-permute-start.12) | collective-permute-done | bytes 786464 | tf_op jit(solution)/shard_map/ppermute | solution.py:37
  166.5 16.4 %collective-permute-done.11.a2 = bf16[384,1024]{1,0:T(8,128)(2,1)S(1)} collective-permute-done((bf16[384,1024]{1,0:T(8,128)(2,1)S(1)}, bf16[384,1024]{1,0:T(8,128)(2,1)S(1)}, u32[]{:S(2)}, u32[]{:S(2)}) %collective-permute-start.11) | collective-permute-done | bytes 786464 | tf_op jit(solution)/shard_map/ppermute | solution.py:37
  190.6 6.6 %all-gather.12.cloned.1.call-done.u_own.up_w = bf16[1024,1408]{1,0:T(8,128)(2,1)} async-done(((bf16[256,1408]{1,0:T(8,128)(2,1)}), bf16[1024,1408]{1,0:T(8,128)(2,1)}) %all-gather.12.cloned.1.call-update) | async-done | bytes 2883600 | tf_op jit(solution)/shard_map/all_gather | solution.py:422
  207.2 18.3 %collective-permute-done.13.p1 = bf16[384,2048]{1,0:T(8,128)(2,1)} collective-permute-done((bf16[384,2048]{1,0:T(8,128)(2,1)}, bf16[384,2048]{1,0:T(8,128)(2,1)}, u32[]{:S(2)}, u32[]{:S(2)}) %collective-permute-start.13) | collective-permute-done | bytes 1572896 | tf_op jit(solution)/shard_map/ppermute | solution.py:37
  232.3 13.8 %shard_map.213.gate_in = f32[1536,1408]{1,0:T(8,128)S(1)} custom-call(bf16[1536,1024]{1,0:T(8,128)(2,1)S(1)} %bitcast.62, bf16[1536,1024]{1,0:T(8,128)(2,1)S(1)} %bitcast.66, bf16[1024,1408]{1,0:T(8,128)(2,1)S(1)} %copy-done.29, bf16[1024,1408]{1,0:T(8,128)(2,1)} %collective-permute-done.14.w_oth.gate_w), custom_call_target="tpu_custom_call" | custom-call | flops 1169400064 | bytes 3898038 | tf_op jit(solution)/shard_map/pallas_call | solution.py:71
  249.4 16.4 %collective-permute-done.17.u_oth.up_w = bf16[1024,1408]{1,0:T(8,128)(2,1)S(1)} collective-permute-done((bf16[1024,1408]{1,0:T(8,128)(2,1)}, bf16[1024,1408]{1,0:T(8,128)(2,1)S(1)}, u32[]{:S(2)}, u32[]{:S(2)}) %collective-permute-start.17) | collective-permute-done | bytes 2883616 | tf_op jit(solution)/shard_map/ppermute | solution.py:37
  267.8 13.9 %shard_map.214 = (bf16[1536,1408]{1,0:T(8,128)(2,1)S(1)}, bf16[1536,1408]{1,0:T(8,128)(2,1)S(1)}, bf16[1536,1408]{1,0:T(8,128)(2,1)S(1)}) custom-call(bf16[1536,1024]{1,0:T(8,128)(2,1)S(1)} %bitcast.63, bf16[1536,1024]{1,0:T(8,128)(2,1)S(1)} %bitcast.67, bf16[1024,1408]{1,0:T(8,128)(2,1)S(1)} %copy-done.31, ...), custom_call_target="tpu_custom_call" | custom-call | flops 1378800000 | bytes 4596011 | tf_op jit(solution)/shard_map/pallas_call | solution.py:71
  290.2 12.3 %shard_map.215 = bf16[2048,1408]{1,0:T(8,128)(2,1)S(1)} custom-call(bf16[1536,2048]{1,0:T(8,128)(2,1)S(1)} %bitcast.60, bf16[1536,1408]{1,0:T(8,128)(2,1)S(1)} %copy-done.15), custom_call_target="tpu_custom_call" | custom-call | flops 1184999936 | bytes 3950012 | tf_op jit(solution)/shard_map/pallas_call | solution.py:71
  313.2 12.8 %shard_map.216 = (bf16[1536,1408]{1,0:T(8,128)(2,1)S(1)}, bf16[1536,1408]{1,0:T(8,128)(2,1)S(1)}) custom-call(bf16[1536,2048]{1,0:T(8,128)(2,1)} %bitcast.61, bf16[2048,1408]{1,0:T(8,128)(2,1)S(1)} %copy-done.13, bf16[1536,1408]{1,0:T(8,128)(2,1)S(1)} %copy-done.63, bf16[1536,1408]{1,0:T(8,128)(2,1)S(1)} %copy-done.65), custom_call_target="tpu_custom_call" | custom-call | flops 1301400064 | bytes 4338013 | tf_op jit(solution)/shard_map/pallas_call | solution.py:71
  326.0 7.0 %shard_map.217 = bf16[1024,1408]{1,0:T(8,128)(2,1)} custom-call(bf16[1536,1024]{1,0:T(8,128)(2,1)S(1)} %bitcast.68, bf16[1536,1408]{1,0:T(8,128)(2,1)S(1)} %get-tuple-element.126.grad.gate_g), custom_call_target="tpu_custom_call" | custom-call | flops 704400000 | bytes 2348016 | tf_op jit(solution)/shard_map/pallas_call | solution.py:71
  334.2 13.2 %shard_map.218 = (bf16[768,1024]{1,0:T(8,128)(2,1)S(1)}, bf16[768,1024]{1,0:T(8,128)(2,1)S(1)}) custom-call(bf16[1536,1408]{1,0:T(8,128)(2,1)S(1)} %get-tuple-element.126.grad.gate_g, bf16[1536,1408]{1,0:T(8,128)(2,1)S(1)} %get-tuple-element.129.up_g.grad, bf16[1024,1408]{1,0:T(8,128)(2,1)} %collective-permute-done.14.w_oth.gate_w, ...), custom_call_target="tpu_custom_call" | custom-call | flops 1169400064 | bytes 3898014 | tf_op jit(solution)/shard_map/pallas_call | solution.py:71
  347.5 11.2 %shard_map.219 = (bf16[768,1024]{1,0:T(8,128)(2,1)S(1)}, bf16[768,1024]{1,0:T(8,128)(2,1)S(1)}) custom-call(bf16[1536,1408]{1,0:T(8,128)(2,1)S(1)} %get-tuple-element.126.grad.gate_g, bf16[1536,1408]{1,0:T(8,128)(2,1)S(1)} %get-tuple-element.129.up_g.grad, bf16[1024,1408]{1,0:T(8,128)(2,1)S(1)} %copy-done.30, bf16[1024,1408]{1,0:T(8,128)(2,1)S(1)} %copy-done.32), custom_call_target="tpu_custom_call" | custom-call | flops 1161600000 | bytes 3872017 | tf_op jit(solution)/shard_map/pallas_call | solution.py:71
  365.0 7.0 %shard_map.221 = bf16[1024,1408]{1,0:T(8,128)(2,1)} custom-call(bf16[1536,1024]{1,0:T(8,128)(2,1)S(1)} %bitcast.69, bf16[1536,1408]{1,0:T(8,128)(2,1)S(1)} %get-tuple-element.129.up_g.grad), custom_call_target="tpu_custom_call" | custom-call | flops 704400000 | bytes 2348019 | tf_op jit(solution)/shard_map/pallas_call | solution.py:71
  372.5 26.1 %collective-permute-done.30.came = bf16[1024,1408]{1,0:T(8,128)(2,1)S(1)} collective-permute-done((bf16[1024,1408]{1,0:T(8,128)(2,1)}, bf16[1024,1408]{1,0:T(8,128)(2,1)S(1)}, u32[]{:S(2)}, u32[]{:S(2)}) %collective-permute-start.30) | collective-permute-done | bytes 2883616 | tf_op jit(solution)/shard_map/ppermute | solution.py:37
  429.8 12.6 %shard_map.224 = (bf16[768,2048]{1,0:T(8,128)(2,1)S(1)}, bf16[768,2048]{1,0:T(8,128)(2,1)}) custom-call(bf16[1536,1408]{1,0:T(8,128)(2,1)S(1)} %copy-done.16, bf16[2048,1408]{1,0:T(8,128)(2,1)S(1)} %bitcast.81), custom_call_target="tpu_custom_call" | custom-call | flops 1146000000 | bytes 3820021 | tf_op jit(solution)/shard_map/pallas_call | solution.py:71
  444.0 14.5 %collective-permute-done.24.came = bf16[1024,1408]{1,0:T(8,128)(2,1)} collective-permute-done((bf16[1024,1408]{1,0:T(8,128)(2,1)}, bf16[1024,1408]{1,0:T(8,128)(2,1)}, u32[]{:S(2)}, u32[]{:S(2)}) %collective-permute-start.24) | collective-permute-done | bytes 2883616 | tf_op jit(solution)/shard_map/ppermute | solution.py:37
  460.7 8.0 %shard_map.225 = bf16[1024,1408]{1,0:T(8,128)(2,1)} custom-call(bf16[1536,1024]{1,0:T(8,128)(2,1)S(1)} %bitcast.65, bf16[1536,1408]{1,0:T(8,128)(2,1)S(1)} %copy-done.1, bf16[1024,1408]{1,0:T(8,128)(2,1)} %collective-permute-done.24.came), custom_call_target="tpu_custom_call" | custom-call | flops 3068400128 | bytes 10228028 | tf_op jit(solution)/shard_map/pallas_call | solution.py:71
  499.5 24.9 %shard_map.230 = bf16[4,3,128,640]{3,2,1,0:T(8,128)(2,1)S(1)} custom-call(s32[3]{0:T(128)S(1)} %bitcast.114, bf16[4,3,128,512]{3,2,1,0:T(8,128)(2,1)S(1)} %copy-done.103, bf16[4,3,128,128]{3,2,1,0:T(8,128)(2,1)S(1)} %copy-done.105, bf16[4,3,128,512]{3,2,1,0:T(8,128)(2,1)S(1)} %bitcast.99, bf16[4,3,128,512]{3,2,1,0:T(8,128)(2,1)S(1)} %copy-done.18, ...), custom_call_target="tpu_custom_call" | custom-call | flops 38310600704 | bytes 127702024 | tf_op jit(solution)/shard_map/pallas_call | solution.py:71
  (413 shorter events, 286.9 us)
Async XLA Ops:
  7.2 41.3 %all-gather.6.cloned.1.call-start = ((), (), s32[]{:S(2)}) async-start(), calls=%async_computation.5 | async-start | bytes 1740800 | tf_op jit(solution)/shard_map/all_gather | solution.py:422
  11.5 66.0 %all-gather.10.cloned.1.call-start = ((), (), s32[]{:S(2)}) async-start(), calls=%async_computation.7 | async-start | bytes 1310720 | tf_op jit(solution)/shard_map/all_gather | solution.py:422
  13.4 124.4 %all-gather.8.cloned.1.call-start = ((), (), s32[]{:S(2)}) async-start(), calls=%async_computation.6 | async-start | bytes 3604480 | tf_op jit(solution)/shard_map/all_gather | solution.py:422
  14.2 183.0 %all-gather.12.cloned.1.call-start = ((), (), s32[]{:S(2)}) async-start(), calls=%async_computation.8 | async-start | bytes 3604480 | tf_op jit(solution)/shard_map/all_gather | solution.py:422
  14.7 290.3 %all-gather.14.cloned.1.call-start = ((), (), s32[]{:S(2)}) async-start(), calls=%async_computation.10 | async-start | bytes 7208960 | tf_op jit(solution)/shard_map/all_gather | solution.py:422
  50.0 36.9 %collective-permute-start.4 = (bf16[384,2048]{1,0:T(8,128)(2,1)S(1)}, bf16[384,2048]{1,0:T(8,128)(2,1)}, u32[]{:S(2)}, u32[]{:S(2)}) collective-permute-start(bf16[384,2048]{1,0:T(8,128)(2,1)S(1)} %bitcast.101), channel_id=1, source_target_pairs={{0,1},{1,0},{2,3},{3,2},{4,5},{5,4},{6,7},{7,6},{8,9},{9,8},{10,11... | collective-permute-start | bytes 4718600 | tf_op jit(solution)/shard_map/ppermute | solution.py:37
  54.8 45.0 %collective-permute-start.1 = (bf16[384,2048]{1,0:T(8,128)(2,1)S(1)}, bf16[384,2048]{1,0:T(8,128)(2,1)}, u32[]{:S(2)}, u32[]{:S(2)}) collective-permute-start(bf16[384,2048]{1,0:T(8,128)(2,1)S(1)} %bitcast.92), channel_id=1, source_target_pairs={{0,2},{2,0},{1,3},{3,1},{4,6},{6,4},{5,7},{7,5},{8,10},{10,8},{9,1... | collective-permute-start | bytes 4718600 | tf_op jit(solution)/shard_map/ppermute | solution.py:37
  61.7 396.9 %reduce-scatter.6.cloned.1.call-start = ((), (), s32[]{:S(2)}) async-start(), calls=%async_computation.9 | async-start | bytes 7208960 | tf_op jit(solution)/shard_map/reduce_scatter | solution.py:585
  80.4 41.5 %collective-permute-start.8 = (bf16[1024,512]{1,0:T(8,128)(2,1)}, bf16[1024,512]{1,0:T(8,128)(2,1)S(1)}, u32[]{:S(2)}, u32[]{:S(2)}) collective-permute-start(bf16[1024,512]{1,0:T(8,128)(2,1)} %all-gather.10.cloned.1.call-done.weight.w_own), channel_id=1, source_target_pairs={{0,4},{4,0},{1,5},{5,1},{2,6},{6,2},{3,7},{7,3},{8,12},{12,8},{9,1... | collective-permute-start | bytes 3145736 | tf_op jit(solution)/shard_map/ppermute | solution.py:37
  137.8 64.5 %collective-permute-start.14 = (bf16[1024,1408]{1,0:T(8,128)(2,1)}, bf16[1024,1408]{1,0:T(8,128)(2,1)}, u32[]{:S(2)}, u32[]{:S(2)}) collective-permute-start(bf16[1024,1408]{1,0:T(8,128)(2,1)} %all-gather.8.cloned.1.call-done.w_own.gate_w), channel_id=1, source_target_pairs={{0,4},{4,0},{1,5},{5,1},{2,6},{6,2},{3,7},{7,3},{8,12},{12,8},{9,1... | collective-permute-start | bytes 8650760 | tf_op jit(solution)/shard_map/ppermute | solution.py:37
  151.3 52.5 %collective-permute-start.2 = (bf16[384,2048]{1,0:T(8,128)(2,1)S(1)}, bf16[384,2048]{1,0:T(8,128)(2,1)S(1)}, u32[]{:S(2)}, u32[]{:S(2)}) collective-permute-start(bf16[384,2048]{1,0:T(8,128)(2,1)S(1)} %bitcast.93), channel_id=1, source_target_pairs={{0,1},{1,0},{2,3},{3,2},{4,5},{5,4},{6,7},{7,6},{8,9},{9,8},{10,11... | collective-permute-start | bytes 4718600 | tf_op jit(solution)/shard_map/ppermute | solution.py:37
  151.3 52.5 %collective-permute-start.3 = (bf16[384,2048]{1,0:T(8,128)(2,1)}, bf16[384,2048]{1,0:T(8,128)(2,1)}, u32[]{:S(2)}, u32[]{:S(2)}) collective-permute-start(bf16[384,2048]{1,0:T(8,128)(2,1)} %collective-permute-done.1.p1), channel_id=1, source_target_pairs={{0,1},{1,0},{2,3},{3,2},{4,5},{5,4},{6,7},{7,6},{8,9},{9,8},{10,11... | collective-permute-start | bytes 4718600 | tf_op jit(solution)/shard_map/ppermute | solution.py:37
  189.1 36.4 %collective-permute-start.13 = (bf16[384,2048]{1,0:T(8,128)(2,1)}, bf16[384,2048]{1,0:T(8,128)(2,1)}, u32[]{:S(2)}, u32[]{:S(2)}) collective-permute-start(bf16[384,2048]{1,0:T(8,128)(2,1)} %get-tuple-element.109.p0), channel_id=1, source_target_pairs={{0,2},{2,0},{1,3},{3,1},{4,6},{6,4},{5,7},{7,5},{8,10},{10,8},{9,1... | collective-permute-start | bytes 4718600 | tf_op jit(solution)/shard_map/ppermute | solution.py:37
  202.3 63.5 %collective-permute-start.17 = (bf16[1024,1408]{1,0:T(8,128)(2,1)}, bf16[1024,1408]{1,0:T(8,128)(2,1)S(1)}, u32[]{:S(2)}, u32[]{:S(2)}) collective-permute-start(bf16[1024,1408]{1,0:T(8,128)(2,1)} %all-gather.12.cloned.1.call-done.u_own.up_w), channel_id=1, source_target_pairs={{0,4},{4,0},{1,5},{5,1},{2,6},{6,2},{3,7},{7,3},{8,12},{12,8},{9,1... | collective-permute-start | bytes 8650760 | tf_op jit(solution)/shard_map/ppermute | solution.py:37
  305.0 220.4 %reduce-scatter.8.cloned.1.call-start = ((), (), s32[]{:S(2)}) async-start(), calls=%async_computation.11 | async-start | bytes 3604480 | tf_op jit(solution)/shard_map/reduce_scatter | solution.py:585
  333.0 65.6 %collective-permute-start.30 = (bf16[1024,1408]{1,0:T(8,128)(2,1)}, bf16[1024,1408]{1,0:T(8,128)(2,1)S(1)}, u32[]{:S(2)}, u32[]{:S(2)}) collective-permute-start(bf16[1024,1408]{1,0:T(8,128)(2,1)} %shard_map.217), channel_id=1, source_target_pairs={{0,4},{4,0},{1,5},{5,1},{2,6},{6,2},{3,7},{7,3},{8,12},{12,8},{9,1... | collective-permute-start | bytes 8650760 | tf_op jit(solution)/shard_map/ppermute | solution.py:37
  360.5 38.1 %collective-permute-start.22 = (bf16[384,1024]{1,0:T(8,128)(2,1)S(1)}, bf16[384,1024]{1,0:T(8,128)(2,1)S(1)}, u32[]{:S(2)}, u32[]{:S(2)}) collective-permute-start(bf16[384,1024]{1,0:T(8,128)(2,1)S(1)} %shard_map.222), channel_id=1, source_target_pairs={{0,2},{2,0},{1,3},{3,1},{4,6},{6,4},{5,7},{7,5},{8,10},{10,8},{9,1... | collective-permute-start | bytes 2359304 | tf_op jit(solution)/shard_map/ppermute | solution.py:37
  372.0 86.5 %collective-permute-start.24 = (bf16[1024,1408]{1,0:T(8,128)(2,1)}, bf16[1024,1408]{1,0:T(8,128)(2,1)}, u32[]{:S(2)}, u32[]{:S(2)}) collective-permute-start(bf16[1024,1408]{1,0:T(8,128)(2,1)} %shard_map.221), channel_id=1, source_target_pairs={{0,4},{4,0},{1,5},{5,1},{2,6},{6,2},{3,7},{7,3},{8,12},{12,8},{9,1... | collective-permute-start | bytes 8650760 | tf_op jit(solution)/shard_map/ppermute | solution.py:37
  408.1 167.9 %reduce-scatter.10.cloned.1.call-start = ((), (), s32[]{:S(2)}) async-start(), calls=%async_computation.12 | async-start | bytes 3604480 | tf_op jit(solution)/shard_map/reduce_scatter | solution.py:585
  426.5 42.3 %collective-permute-start.23 = (bf16[384,2048]{1,0:T(8,128)(2,1)}, bf16[384,2048]{1,0:T(8,128)(2,1)}, u32[]{:S(2)}, u32[]{:S(2)}) collective-permute-start(bf16[384,2048]{1,0:T(8,128)(2,1)} %get-tuple-element.132.p0), channel_id=1, source_target_pairs={{0,2},{2,0},{1,3},{3,1},{4,6},{6,4},{5,7},{7,5},{8,10},{10,8},{9,1... | collective-permute-start | bytes 4718600 | tf_op jit(solution)/shard_map/ppermute | solution.py:37
  427.5 41.2 %collective-permute-start.25 = (bf16[384,2048]{1,0:T(8,128)(2,1)}, bf16[384,2048]{1,0:T(8,128)(2,1)}, u32[]{:S(2)}, u32[]{:S(2)}) collective-permute-start(bf16[384,2048]{1,0:T(8,128)(2,1)} %get-tuple-element.132.p0), channel_id=1, source_target_pairs={{0,1},{1,0},{2,3},{3,2},{4,5},{5,4},{6,7},{7,6},{8,9},{9,8},{10,11... | collective-permute-start | bytes 4718600 | tf_op jit(solution)/shard_map/ppermute | solution.py:37
  479.2 115.0 %reduce-scatter.14.cloned.1.call-start = ((), (), s32[]{:S(2)}) async-start(), calls=%async_computation.14 | async-start | bytes 1310720 | tf_op jit(solution)/shard_map/reduce_scatter | solution.py:585
  498.0 37.5 %collective-permute-start.28 = (bf16[384,2048]{1,0:T(8,128)(2,1)}, bf16[384,2048]{1,0:T(8,128)(2,1)}, u32[]{:S(2)}, u32[]{:S(2)}) collective-permute-start(bf16[384,2048]{1,0:T(8,128)(2,1)} %shard_map.227), channel_id=1, source_target_pairs={{0,2},{2,0},{1,3},{3,1},{4,6},{6,4},{5,7},{7,5},{8,10},{10,8},{9,1... | collective-permute-start | bytes 4718600 | tf_op jit(solution)/shard_map/ppermute | solution.py:37
  544.2 73.2 %reduce-scatter.12.cloned.1.call-start = ((), (), s32[]{:S(2)}) async-start(), calls=%async_computation.13 | async-start | bytes 1740800 | tf_op jit(solution)/shard_map/reduce_scatter | solution.py:585
  (140 other events, 1251.2 us)
Sparse Core Ops, SparseCore 0:
  11.7 36.7 all-gather.5
  50.6 26.8 all-gather.9
  79.1 58.6 all-gather.7
  139.2 57.8 all-gather.11
  199.1 105.3 all-gather.13
  306.7 100.5 reduce-scatter.5
  409.6 56.6 reduce-scatter.7
  479.4 54.3 reduce-scatter.9
  544.3 23.7 reduce-scatter.13
  581.5 29.1 reduce-scatter.11

commit v8 on v7

--- a/solution.py
+++ b/solution.py
@@ -79,7 +79,7 @@
             scratch_shapes=list(scratch),
         ),
         cost_estimate=pl.CostEstimate(flops=work * 300, bytes_accessed=work + step, transcendentals=0),
-        compiler_params=pltpu.CompilerParams(vmem_limit_bytes=30 << 20),
+        compiler_params=pltpu.CompilerParams(vmem_limit_bytes=48 << 20),
     )(*scalars, *[a for a, _ in ins])
 
 

time: 636 us -> 635 us (level)
  Pallas kernels: 254 us -> 305 us
  local copies, waits for them, and re-layouts: 112 us -> 61.9 us
    unnamed x241 -> x157, local copies, waits for them, and re-layouts: 99.4 us -> 47.7 us
    pallas_call x39, Pallas kernels: 254 us -> 305 us  [call(): pl.pallas_call(kernel, out_shape=[jax.ShapeDtypeStruct(shape, kind) for s...]
  transfers between devices with their start and end apart: 49 -> 49, of which waited for: 21 -> 23; matrix products, arithmetic and copies ran while one was open for 5% -> 6% of each run, Pallas kernels for 40% -> 49%
where the time goes in v8:
time: 635 us; the launch traced here: 629 us
  Pallas kernels  305 us (48%)
  waiting for transfers between devices  197 us (31%)
  local copies, waits for them, and re-layouts  61.9 us (10%)
  starting transfers between devices  32.9 us (5%)
  other arithmetic  16.4 us (3%)
  between operations  15.2 us (2%)
    pallas_call x39, Pallas kernels, call(): pl.pallas_call(kernel, out_shape=[jax.ShapeDtypeStruct(shape, kind) for s...  305 us
    ppermute x39, waiting for transfers between devices, swap(): return lax.ppermute(value, axis, SWAP)  153 us
    unnamed x157, local copies, waits for them, and re-layouts  47.7 us
    all_gather x5, waiting for transfers between devices, gather(): return lax.all_gather(part, 'fh', axis=0, tiled=True)  43.1 us
    ppermute x39, starting transfers between devices, swap(): return lax.ppermute(value, axis, SWAP)  31.3 us
  transfers between devices with their start and end apart: 49, of which 23 were waited for; matrix products, arithmetic and copies ran while one was open for 6% of the time, Pallas kernels for 49%

profile of v8, /device:TPU:0, one launch (start us, length us, event | category | flops | bytes accessed | tf_op | source)
XLA Modules:
  0.0 629.0 jit_solution(16146144248008565354)
XLA Ops:
  20.4 14.8 %collective-permute-done.6 = bf16[256,1408]{1,0:T(8,128)(2,1)S(1)} collective-permute-done((bf16[256,1408]{1,0:T(8,128)(2,1)}, bf16[256,1408]{1,0:T(8,128)(2,1)S(1)}, u32[]{:S(2)}, u32[]{:S(2)}) %collective-permute-start.6) | collective-permute-done | bytes 720928 | tf_op jit(solution)/shard_map/ppermute | solution.py:37
  37.5 11.0 %all-gather.6.cloned.1.call-done = bf16[1088,640]{1,0:T(8,128)(2,1)} async-done(((bf16[272,640]{1,0:T(8,128)(2,1)}), bf16[1088,640]{1,0:T(8,128)(2,1)}) %all-gather.6.cloned.1.call-update) | async-done | bytes 1392656 | tf_op jit(solution)/shard_map/all_gather | solution.py:422
  62.2 15.3 %all-gather.10.cloned.1.call-done.weight.w_own = bf16[1024,512]{1,0:T(8,128)(2,1)} async-done(((bf16[256,512]{1,0:T(8,128)(2,1)}), bf16[1024,512]{1,0:T(8,128)(2,1)}) %all-gather.10.cloned.1.call-update) | async-done | bytes 1048592 | tf_op jit(solution)/shard_map/all_gather | solution.py:422
  86.9 7.9 %shard_map.204 = (bf16[4,3,128,1024]{3,2,1,0:T(8,128)(2,1)}, bf16[4,3,128,1024]{3,2,1,0:T(8,128)(2,1)}, bf16[384,1024]{1,0:T(8,128)(2,1)S(1)}, bf16[384,1024]{1,0:T(8,128)(2,1)S(1)}) custom-call(s32[1]{0:T(128)} %bitcast.at, bf16[384,2048]{1,0:T(8,128)(2,1)S(1)} %bitcast.88, bf16[384,2048]{1,0:T(8,128)(2,1)} %collective-permute-done.p1, ...), custom_call_target="tpu_custom_call" | custom-call | flops 666000000 | bytes 2220002 | tf_op jit(solution)/shard_map/pallas_call | solution.py:71
  97.3 8.5 %shard_map.205 = f32[1536,640]{1,0:T(8,128)} custom-call(bf16[1536,1024]{1,0:T(8,128)(2,1)S(1)} %bitcast.70, bf16[1536,1024]{1,0:T(8,128)(2,1)} %bitcast.107, bf16[1024,640]{1,0:T(8,128)(2,1)S(1)} %bitcast.75, bf16[1024,640]{1,0:T(8,128)(2,1)S(1)} %bitcast.77), custom_call_target="tpu_custom_call" | custom-call | flops 774600000 | bytes 2582003 | tf_op jit(solution)/shard_map/pallas_call | solution.py:71
  105.9 20.4 %shard_map.206 = (bf16[4,3,128,512]{3,2,1,0:T(8,128)(2,1)S(1)}, bf16[4,3,128,128]{3,2,1,0:T(8,128)(2,1)S(1)}, bf16[4,3,128,512]{3,2,1,0:T(8,128)(2,1)S(1)}, f32[3,8,512]{2,1,0:T(8,128)S(1)}) custom-call(s32[3]{0:T(128)S(1)} %bitcast.99, f32[4,3,128,640]{3,2,1,0:T(8,128)} %bitcast.112, f32[512,128]{1,0:T(8,128)S(1)} %copy-done.54, ...), custom_call_target="tpu_custom_call" | custom-call | flops 1688999936 | bytes 5630004 | tf_op jit(solution)/shard_map/pallas_call | solution.py:71
  152.7 13.9 %collective-permute-done.12.b2 = bf16[384,1024]{1,0:T(8,128)(2,1)S(1)} collective-permute-done((bf16[384,1024]{1,0:T(8,128)(2,1)S(1)}, bf16[384,1024]{1,0:T(8,128)(2,1)S(1)}, u32[]{:S(2)}, u32[]{:S(2)}) %collective-permute-start.12) | collective-permute-done | bytes 786464 | tf_op jit(solution)/shard_map/ppermute | solution.py:37
  166.5 16.4 %collective-permute-done.11.a2 = bf16[384,1024]{1,0:T(8,128)(2,1)S(1)} collective-permute-done((bf16[384,1024]{1,0:T(8,128)(2,1)S(1)}, bf16[384,1024]{1,0:T(8,128)(2,1)S(1)}, u32[]{:S(2)}, u32[]{:S(2)}) %collective-permute-start.11) | collective-permute-done | bytes 786464 | tf_op jit(solution)/shard_map/ppermute | solution.py:37
  209.7 15.5 %collective-permute-done.13.p1 = bf16[384,2048]{1,0:T(8,128)(2,1)} collective-permute-done((bf16[384,2048]{1,0:T(8,128)(2,1)}, bf16[384,2048]{1,0:T(8,128)(2,1)}, u32[]{:S(2)}, u32[]{:S(2)}) %collective-permute-start.13) | collective-permute-done | bytes 1572896 | tf_op jit(solution)/shard_map/ppermute | solution.py:37
  235.1 14.3 %shard_map.213.gate_in = f32[1536,1408]{1,0:T(8,128)} custom-call(bf16[1536,1024]{1,0:T(8,128)(2,1)} %bitcast.103, bf16[1536,1024]{1,0:T(8,128)(2,1)} %bitcast.60, bf16[1024,1408]{1,0:T(8,128)(2,1)S(1)} %copy-done.12, bf16[1024,1408]{1,0:T(8,128)(2,1)} %collective-permute-done.14.w_oth.gate_w), custom_call_target="tpu_custom_call" | custom-call | flops 1169400064 | bytes 3898038 | tf_op jit(solution)/shard_map/pallas_call | solution.py:71
  249.4 16.4 %collective-permute-done.17.u_oth.up_w = bf16[1024,1408]{1,0:T(8,128)(2,1)S(1)} collective-permute-done((bf16[1024,1408]{1,0:T(8,128)(2,1)}, bf16[1024,1408]{1,0:T(8,128)(2,1)S(1)}, u32[]{:S(2)}, u32[]{:S(2)}) %collective-permute-start.17) | collective-permute-done | bytes 2883616 | tf_op jit(solution)/shard_map/ppermute | solution.py:37
  265.8 16.9 %shard_map.214 = (bf16[1536,1408]{1,0:T(8,128)(2,1)}, bf16[1536,1408]{1,0:T(8,128)(2,1)}, bf16[1536,1408]{1,0:T(8,128)(2,1)}) custom-call(bf16[1536,1024]{1,0:T(8,128)(2,1)} %bitcast.104, bf16[1536,1024]{1,0:T(8,128)(2,1)} %bitcast.61, bf16[1024,1408]{1,0:T(8,128)(2,1)S(1)} %copy-done.14, bf16[1024,1408]{1,0:T(8,128)(2,1)S(1)} %collective-permute-done.17.u_oth.up_w, ...), custom_call_target="tpu_custom_call" | custom-call | flops 1378800000 | bytes 4596011 | tf_op jit(solution)/shard_map/pallas_call | solution.py:71
  285.0 13.4 %shard_map.215 = bf16[2048,1408]{1,0:T(8,128)(2,1)} custom-call(bf16[1536,2048]{1,0:T(8,128)(2,1)} %bitcast.101, bf16[1536,1408]{1,0:T(8,128)(2,1)S(1)} %copy-done.5), custom_call_target="tpu_custom_call" | custom-call | flops 1184999936 | bytes 3950012 | tf_op jit(solution)/shard_map/pallas_call | solution.py:71
  304.6 16.6 %shard_map.216 = (bf16[1536,1408]{1,0:T(8,128)(2,1)S(1)}, bf16[1536,1408]{1,0:T(8,128)(2,1)}) custom-call(bf16[1536,2048]{1,0:T(8,128)(2,1)} %bitcast.102, bf16[2048,1408]{1,0:T(8,128)(2,1)} %all-gather.14.cloned.1.call-done.weight, bf16[1536,1408]{1,0:T(8,128)(2,1)} %get-tuple-element.120.for_gate, bf16[1536,1408]{1,0:T(8,128)(2,1)} %get-tuple-element.121.for_up), custom_call_target="tpu_custom_call" | custom-call | flops 1301400064 | bytes 4338013 | tf_op jit(solution)/shard_map/pallas_call | solution.py:71
  323.1 9.1 %shard_map.217 = bf16[1024,1408]{1,0:T(8,128)(2,1)} custom-call(bf16[1536,1024]{1,0:T(8,128)(2,1)S(1)} %bitcast.62, bf16[1536,1408]{1,0:T(8,128)(2,1)} %copy-done), custom_call_target="tpu_custom_call" | custom-call | flops 704400000 | bytes 2348016 | tf_op jit(solution)/shard_map/pallas_call | solution.py:71
  333.7 15.4 %shard_map.218 = (bf16[768,1024]{1,0:T(8,128)(2,1)S(1)}, bf16[768,1024]{1,0:T(8,128)(2,1)}) custom-call(bf16[1536,1408]{1,0:T(8,128)(2,1)} %copy-done, bf16[1536,1408]{1,0:T(8,128)(2,1)} %get-tuple-element.129.up_g.grad, bf16[1024,1408]{1,0:T(8,128)(2,1)} %collective-permute-done.14.w_oth.gate_w, bf16[1024,1408]{1,0:T(8,128)(2,1)} %copy-done.15), custom_call_target="tpu_custom_call" | custom-call | flops 1169400064 | bytes 3898014 | tf_op jit(solution)/shard_map/pallas_call | solution.py:71
  349.2 14.2 %shard_map.219 = (bf16[768,1024]{1,0:T(8,128)(2,1)S(1)}, bf16[768,1024]{1,0:T(8,128)(2,1)S(1)}) custom-call(bf16[1536,1408]{1,0:T(8,128)(2,1)} %copy-done, bf16[1536,1408]{1,0:T(8,128)(2,1)} %get-tuple-element.129.up_g.grad, bf16[1024,1408]{1,0:T(8,128)(2,1)S(1)} %copy-done.13, bf16[1024,1408]{1,0:T(8,128)(2,1)} %all-gather.12.cloned.1.call-done.u_own.up_w), custom_call_target="tpu_custom_call" | custom-call | flops 1161600000 | bytes 3872017 | tf_op jit(solution)/shard_map/pallas_call | solution.py:71
  369.6 9.1 %shard_map.221 = bf16[1024,1408]{1,0:T(8,128)(2,1)} custom-call(bf16[1536,1024]{1,0:T(8,128)(2,1)S(1)} %bitcast.63, bf16[1536,1408]{1,0:T(8,128)(2,1)} %get-tuple-element.129.up_g.grad), custom_call_target="tpu_custom_call" | custom-call | flops 704400000 | bytes 2348019 | tf_op jit(solution)/shard_map/pallas_call | solution.py:71
  379.2 18.8 %collective-permute-done.30.came = bf16[1024,1408]{1,0:T(8,128)(2,1)} collective-permute-done((bf16[1024,1408]{1,0:T(8,128)(2,1)}, bf16[1024,1408]{1,0:T(8,128)(2,1)}, u32[]{:S(2)}, u32[]{:S(2)}) %collective-permute-start.30) | collective-permute-done | bytes 2883616 | tf_op jit(solution)/shard_map/ppermute | solution.py:37
  401.5 8.7 %shard_map.232 = bf16[1024,1408]{1,0:T(8,128)(2,1)S(1)} custom-call(bf16[1536,1024]{1,0:T(8,128)(2,1)} %bitcast.105, bf16[1536,1408]{1,0:T(8,128)(2,1)} %copy-done, bf16[1024,1408]{1,0:T(8,128)(2,1)} %collective-permute-done.30.came), custom_call_target="tpu_custom_call" | custom-call | flops 766800000 | bytes 2556023 | tf_op jit(solution)/shard_map/pallas_call | solution.py:71
  421.8 15.6 %shard_map.224 = (bf16[768,2048]{1,0:T(8,128)(2,1)S(1)}, bf16[768,2048]{1,0:T(8,128)(2,1)}) custom-call(bf16[1536,1408]{1,0:T(8,128)(2,1)} %get-tuple-element.133.grad.rows, bf16[2048,1408]{1,0:T(8,128)(2,1)} %all-gather.14.cloned.1.call-done.weight), custom_call_target="tpu_custom_call" | custom-call | flops 1146000000 | bytes 3820021 | tf_op jit(solution)/shard_map/pallas_call | solution.py:71
  439.1 19.8 %collective-permute-done.24.came = bf16[1024,1408]{1,0:T(8,128)(2,1)} collective-permute-done((bf16[1024,1408]{1,0:T(8,128)(2,1)}, bf16[1024,1408]{1,0:T(8,128)(2,1)}, u32[]{:S(2)}, u32[]{:S(2)}) %collective-permute-start.24) | collective-permute-done | bytes 2883616 | tf_op jit(solution)/shard_map/ppermute | solution.py:37
  458.8 8.8 %shard_map.225 = bf16[1024,1408]{1,0:T(8,128)(2,1)S(1)} custom-call(bf16[1536,1024]{1,0:T(8,128)(2,1)} %bitcast.106, bf16[1536,1408]{1,0:T(8,128)(2,1)} %get-tuple-element.129.up_g.grad, bf16[1024,1408]{1,0:T(8,128)(2,1)} %collective-permute-done.24.came), custom_call_target="tpu_custom_call" | custom-call | flops 3068400128 | bytes 10228028 | tf_op jit(solution)/shard_map/pallas_call | solution.py:71
  498.6 25.6 %shard_map.230 = bf16[4,3,128,640]{3,2,1,0:T(8,128)(2,1)} custom-call(s32[3]{0:T(128)S(1)} %bitcast.100, bf16[4,3,128,512]{3,2,1,0:T(8,128)(2,1)S(1)} %copy-done.63, bf16[4,3,128,128]{3,2,1,0:T(8,128)(2,1)S(1)} %copy-done.65, bf16[4,3,128,512]{3,2,1,0:T(8,128)(2,1)S(1)} %bitcast.85, bf16[4,3,128,512]{3,2,1,0:T(8,128)(2,1)S(1)} %get-tuple-element.102.mixed_in, ...), custom_call_target="tpu_custom_call" | custom-call | flops 38310600704 | bytes 127702024 | tf_op jit(solution)/shard_map/pallas_call | solution.py:71
  (328 shorter events, 267.1 us)
Async XLA Ops:
  7.2 41.3 %all-gather.6.cloned.1.call-start = ((), (), s32[]{:S(2)}) async-start(), calls=%async_computation.5 | async-start | bytes 1740800 | tf_op jit(solution)/shard_map/all_gather | solution.py:422
  11.5 66.0 %all-gather.10.cloned.1.call-start = ((), (), s32[]{:S(2)}) async-start(), calls=%async_computation.7 | async-start | bytes 1310720 | tf_op jit(solution)/shard_map/all_gather | solution.py:422
  13.4 124.4 %all-gather.8.cloned.1.call-start = ((), (), s32[]{:S(2)}) async-start(), calls=%async_computation.6 | async-start | bytes 3604480 | tf_op jit(solution)/shard_map/all_gather | solution.py:422
  14.2 183.0 %all-gather.12.cloned.1.call-start = ((), (), s32[]{:S(2)}) async-start(), calls=%async_computation.8 | async-start | bytes 3604480 | tf_op jit(solution)/shard_map/all_gather | solution.py:422
  14.7 289.8 %all-gather.14.cloned.1.call-start = ((), (), s32[]{:S(2)}) async-start(), calls=%async_computation.10 | async-start | bytes 7208960 | tf_op jit(solution)/shard_map/all_gather | solution.py:422
  18.9 36.0 %collective-permute-start = (bf16[384,2048]{1,0:T(8,128)(2,1)S(1)}, bf16[384,2048]{1,0:T(8,128)(2,1)}, u32[]{:S(2)}, u32[]{:S(2)}) collective-permute-start(bf16[384,2048]{1,0:T(8,128)(2,1)S(1)} %bitcast.86), channel_id=1, source_target_pairs={{0,2},{2,0},{1,3},{3,1},{4,6},{6,4},{5,7},{7,5},{8,10},{10,8},{9,1... | collective-permute-start | bytes 4718600 | tf_op jit(solution)/shard_map/ppermute | solution.py:37
  50.0 36.9 %collective-permute-start.4 = (bf16[384,2048]{1,0:T(8,128)(2,1)S(1)}, bf16[384,2048]{1,0:T(8,128)(2,1)}, u32[]{:S(2)}, u32[]{:S(2)}) collective-permute-start(bf16[384,2048]{1,0:T(8,128)(2,1)S(1)} %bitcast.87), channel_id=1, source_target_pairs={{0,1},{1,0},{2,3},{3,2},{4,5},{5,4},{6,7},{7,6},{8,9},{9,8},{10,11... | collective-permute-start | bytes 4718600 | tf_op jit(solution)/shard_map/ppermute | solution.py:37
  54.8 51.0 %collective-permute-start.1 = (bf16[384,2048]{1,0:T(8,128)(2,1)S(1)}, bf16[384,2048]{1,0:T(8,128)(2,1)}, u32[]{:S(2)}, u32[]{:S(2)}) collective-permute-start(bf16[384,2048]{1,0:T(8,128)(2,1)S(1)} %bitcast.80), channel_id=1, source_target_pairs={{0,2},{2,0},{1,3},{3,1},{4,6},{6,4},{5,7},{7,5},{8,10},{10,8},{9,1... | collective-permute-start | bytes 4718600 | tf_op jit(solution)/shard_map/ppermute | solution.py:37
  61.6 397.2 %reduce-scatter.6.cloned.1.call-start = ((), (), s32[]{:S(2)}) async-start(), calls=%async_computation.9 | async-start | bytes 7208960 | tf_op jit(solution)/shard_map/reduce_scatter | solution.py:585
  80.4 47.9 %collective-permute-start.8 = (bf16[1024,512]{1,0:T(8,128)(2,1)}, bf16[1024,512]{1,0:T(8,128)(2,1)S(1)}, u32[]{:S(2)}, u32[]{:S(2)}) collective-permute-start(bf16[1024,512]{1,0:T(8,128)(2,1)} %all-gather.10.cloned.1.call-done.weight.w_own), channel_id=1, source_target_pairs={{0,4},{4,0},{1,5},{5,1},{2,6},{6,2},{3,7},{7,3},{8,12},{12,8},{9,1... | collective-permute-start | bytes 3145736 | tf_op jit(solution)/shard_map/ppermute | solution.py:37
  137.8 64.5 %collective-permute-start.14 = (bf16[1024,1408]{1,0:T(8,128)(2,1)}, bf16[1024,1408]{1,0:T(8,128)(2,1)}, u32[]{:S(2)}, u32[]{:S(2)}) collective-permute-start(bf16[1024,1408]{1,0:T(8,128)(2,1)} %all-gather.8.cloned.1.call-done.w_own.gate_w), channel_id=1, source_target_pairs={{0,4},{4,0},{1,5},{5,1},{2,6},{6,2},{3,7},{7,3},{8,12},{12,8},{9,1... | collective-permute-start | bytes 8650760 | tf_op jit(solution)/shard_map/ppermute | solution.py:37
  152.1 51.7 %collective-permute-start.2 = (bf16[384,2048]{1,0:T(8,128)(2,1)S(1)}, bf16[384,2048]{1,0:T(8,128)(2,1)}, u32[]{:S(2)}, u32[]{:S(2)}) collective-permute-start(bf16[384,2048]{1,0:T(8,128)(2,1)S(1)} %bitcast.81), channel_id=1, source_target_pairs={{0,1},{1,0},{2,3},{3,2},{4,5},{5,4},{6,7},{7,6},{8,9},{9,8},{10,11... | collective-permute-start | bytes 4718600 | tf_op jit(solution)/shard_map/ppermute | solution.py:37
  152.1 51.7 %collective-permute-start.3 = (bf16[384,2048]{1,0:T(8,128)(2,1)}, bf16[384,2048]{1,0:T(8,128)(2,1)}, u32[]{:S(2)}, u32[]{:S(2)}) collective-permute-start(bf16[384,2048]{1,0:T(8,128)(2,1)} %collective-permute-done.1.p1), channel_id=1, source_target_pairs={{0,1},{1,0},{2,3},{3,2},{4,5},{5,4},{6,7},{7,6},{8,9},{9,8},{10,11... | collective-permute-start | bytes 4718600 | tf_op jit(solution)/shard_map/ppermute | solution.py:37
  188.9 36.4 %collective-permute-start.13 = (bf16[384,2048]{1,0:T(8,128)(2,1)}, bf16[384,2048]{1,0:T(8,128)(2,1)}, u32[]{:S(2)}, u32[]{:S(2)}) collective-permute-start(bf16[384,2048]{1,0:T(8,128)(2,1)} %get-tuple-element.109.p0), channel_id=1, source_target_pairs={{0,2},{2,0},{1,3},{3,1},{4,6},{6,4},{5,7},{7,5},{8,10},{10,8},{9,1... | collective-permute-start | bytes 4718600 | tf_op jit(solution)/shard_map/ppermute | solution.py:37
  202.3 63.5 %collective-permute-start.17 = (bf16[1024,1408]{1,0:T(8,128)(2,1)}, bf16[1024,1408]{1,0:T(8,128)(2,1)S(1)}, u32[]{:S(2)}, u32[]{:S(2)}) collective-permute-start(bf16[1024,1408]{1,0:T(8,128)(2,1)} %all-gather.12.cloned.1.call-done.u_own.up_w), channel_id=1, source_target_pairs={{0,4},{4,0},{1,5},{5,1},{2,6},{6,2},{3,7},{7,3},{8,12},{12,8},{9,1... | collective-permute-start | bytes 8650760 | tf_op jit(solution)/shard_map/ppermute | solution.py:37
  298.5 226.7 %reduce-scatter.8.cloned.1.call-start = ((), (), s32[]{:S(2)}) async-start(), calls=%async_computation.11 | async-start | bytes 3604480 | tf_op jit(solution)/shard_map/reduce_scatter | solution.py:585
  332.3 65.7 %collective-permute-start.30 = (bf16[1024,1408]{1,0:T(8,128)(2,1)}, bf16[1024,1408]{1,0:T(8,128)(2,1)}, u32[]{:S(2)}, u32[]{:S(2)}) collective-permute-start(bf16[1024,1408]{1,0:T(8,128)(2,1)} %shard_map.217), channel_id=1, source_target_pairs={{0,4},{4,0},{1,5},{5,1},{2,6},{6,2},{3,7},{7,3},{8,12},{12,8},{9,1... | collective-permute-start | bytes 8650760 | tf_op jit(solution)/shard_map/ppermute | solution.py:37
  378.7 80.1 %collective-permute-start.24 = (bf16[1024,1408]{1,0:T(8,128)(2,1)}, bf16[1024,1408]{1,0:T(8,128)(2,1)}, u32[]{:S(2)}, u32[]{:S(2)}) collective-permute-start(bf16[1024,1408]{1,0:T(8,128)(2,1)} %shard_map.221), channel_id=1, source_target_pairs={{0,4},{4,0},{1,5},{5,1},{2,6},{6,2},{3,7},{7,3},{8,12},{12,8},{9,1... | collective-permute-start | bytes 8650760 | tf_op jit(solution)/shard_map/ppermute | solution.py:37
  411.9 166.9 %reduce-scatter.10.cloned.1.call-start = ((), (), s32[]{:S(2)}) async-start(), calls=%async_computation.12 | async-start | bytes 3604480 | tf_op jit(solution)/shard_map/reduce_scatter | solution.py:585
  420.5 48.8 %collective-permute-start.23 = (bf16[384,2048]{1,0:T(8,128)(2,1)}, bf16[384,2048]{1,0:T(8,128)(2,1)}, u32[]{:S(2)}, u32[]{:S(2)}) collective-permute-start(bf16[384,2048]{1,0:T(8,128)(2,1)} %get-tuple-element.132.p0), channel_id=1, source_target_pairs={{0,2},{2,0},{1,3},{3,1},{4,6},{6,4},{5,7},{7,5},{8,10},{10,8},{9,1... | collective-permute-start | bytes 4718600 | tf_op jit(solution)/shard_map/ppermute | solution.py:37
  421.8 47.5 %collective-permute-start.25 = (bf16[384,2048]{1,0:T(8,128)(2,1)}, bf16[384,2048]{1,0:T(8,128)(2,1)}, u32[]{:S(2)}, u32[]{:S(2)}) collective-permute-start(bf16[384,2048]{1,0:T(8,128)(2,1)} %get-tuple-element.132.p0), channel_id=1, source_target_pairs={{0,1},{1,0},{2,3},{3,2},{4,5},{5,4},{6,7},{7,6},{8,9},{9,8},{10,11... | collective-permute-start | bytes 4718600 | tf_op jit(solution)/shard_map/ppermute | solution.py:37
  479.9 117.7 %reduce-scatter.14.cloned.1.call-start = ((), (), s32[]{:S(2)}) async-start(), calls=%async_computation.14 | async-start | bytes 1310720 | tf_op jit(solution)/shard_map/reduce_scatter | solution.py:585
  497.1 38.3 %collective-permute-start.28 = (bf16[384,2048]{1,0:T(8,128)(2,1)}, bf16[384,2048]{1,0:T(8,128)(2,1)}, u32[]{:S(2)}, u32[]{:S(2)}) collective-permute-start(bf16[384,2048]{1,0:T(8,128)(2,1)} %shard_map.227), channel_id=1, source_target_pairs={{0,2},{2,0},{1,3},{3,1},{4,6},{6,4},{5,7},{7,5},{8,10},{10,8},{9,1... | collective-permute-start | bytes 4718600 | tf_op jit(solution)/shard_map/ppermute | solution.py:37
  546.7 69.1 %reduce-scatter.12.cloned.1.call-start = ((), (), s32[]{:S(2)}) async-start(), calls=%async_computation.13 | async-start | bytes 1740800 | tf_op jit(solution)/shard_map/reduce_scatter | solution.py:585
  (98 other events, 957.0 us)
Sparse Core Ops, SparseCore 0:
  11.7 36.7 all-gather.5
  50.6 26.8 all-gather.9
  79.1 58.6 all-gather.7
  139.2 57.8 all-gather.11
  199.1 105.3 all-gather.13
  306.7 100.5 reduce-scatter.5
  412.0 54.3 reduce-scatter.7
  480.0 54.4 reduce-scatter.9
  546.8 23.9 reduce-scatter.13
  584.2 29.2 reduce-scatter.11

commit v9 on v8

--- a/solution.py
+++ b/solution.py
@@ -79,7 +79,7 @@
             scratch_shapes=list(scratch),
         ),
         cost_estimate=pl.CostEstimate(flops=work * 300, bytes_accessed=work + step, transcendentals=0),
-        compiler_params=pltpu.CompilerParams(vmem_limit_bytes=48 << 20),
+        compiler_params=pltpu.CompilerParams(vmem_limit_bytes=53 << 20),
     )(*scalars, *[a for a, _ in ins])
 
 

time: 635 us -> 635 us (level)
  Pallas kernels: 305 us -> 346 us
  local copies, waits for them, and re-layouts: 61.9 us -> 32.8 us
    pallas_call x39, Pallas kernels: 305 us -> 346 us  [call(): pl.pallas_call(kernel, out_shape=[jax.ShapeDtypeStruct(shape, kind) for s...]
    unnamed x157 -> x59, local copies, waits for them, and re-layouts: 47.7 us -> 20.3 us
  transfers between devices with their start and end apart: 49 -> 49, of which waited for: 23 -> 23; matrix products, arithmetic and copies ran while one was open for 6% -> 4% of each run, Pallas kernels for 49% -> 55%
where the time goes in v9:
time: 635 us; the launch traced here: 629 us
  Pallas kernels  346 us (54%)
  waiting for transfers between devices  191 us (30%)
  local copies, waits for them, and re-layouts  32.8 us (5%)
  starting transfers between devices  32.7 us (5%)
  between operations  14.9 us (2%)
  other arithmetic  11.1 us (2%)
    pallas_call x39, Pallas kernels, call(): pl.pallas_call(kernel, out_shape=[jax.ShapeDtypeStruct(shape, kind) for s...  346 us
    ppermute x39, waiting for transfers between devices, swap(): return lax.ppermute(value, axis, SWAP)  148 us
    all_gather x5, waiting for transfers between devices, gather(): return lax.all_gather(part, 'fh', axis=0, tiled=True)  41.9 us
    ppermute x39, starting transfers between devices, swap(): return lax.ppermute(value, axis, SWAP)  31.1 us
    unnamed x59, local copies, waits for them, and re-layouts  20.3 us
  transfers between devices with their start and end apart: 49, of which 23 were waited for; matrix products, arithmetic and copies ran while one was open for 4% of the time, Pallas kernels for 55%

profile of v9, /device:TPU:0, one launch (start us, length us, event | category | flops | bytes accessed | tf_op | source)
XLA Modules:
  0.0 629.1 jit_solution(17068603390724424300)
XLA Ops:
  19.7 14.6 %collective-permute-done.6 = bf16[256,1408]{1,0:T(8,128)(2,1)S(1)} collective-permute-done((bf16[256,1408]{1,0:T(8,128)(2,1)S(1)}, bf16[256,1408]{1,0:T(8,128)(2,1)S(1)}, u32[]{:S(2)}, u32[]{:S(2)}) %collective-permute-start.6) | collective-permute-done | bytes 720928 | tf_op jit(solution)/shard_map/ppermute | solution.py:37
  35.5 13.0 %all-gather.6.cloned.1.call-done = bf16[1088,640]{1,0:T(8,128)(2,1)} async-done(((bf16[272,640]{1,0:T(8,128)(2,1)}), bf16[1088,640]{1,0:T(8,128)(2,1)}) %all-gather.6.cloned.1.call-update) | async-done | bytes 1392656 | tf_op jit(solution)/shard_map/all_gather | solution.py:422
  58.2 19.3 %all-gather.10.cloned.1.call-done.weight.w_own = bf16[1024,512]{1,0:T(8,128)(2,1)} async-done(((bf16[256,512]{1,0:T(8,128)(2,1)}), bf16[1024,512]{1,0:T(8,128)(2,1)}) %all-gather.10.cloned.1.call-update) | async-done | bytes 1048592 | tf_op jit(solution)/shard_map/all_gather | solution.py:422
  96.8 9.9 %shard_map.205 = f32[1536,640]{1,0:T(8,128)} custom-call(bf16[1536,1024]{1,0:T(8,128)(2,1)} %bitcast.89, bf16[1536,1024]{1,0:T(8,128)(2,1)} %bitcast.86, bf16[1024,640]{1,0:T(8,128)(2,1)} %bitcast.98, bf16[1024,640]{1,0:T(8,128)(2,1)} %bitcast.100), custom_call_target="tpu_custom_call" | custom-call | flops 774600000 | bytes 2582003 | tf_op jit(solution)/shard_map/pallas_call | solution.py:71
  106.7 21.2 %shard_map.206 = (bf16[4,3,128,512]{3,2,1,0:T(8,128)(2,1)}, bf16[4,3,128,128]{3,2,1,0:T(8,128)(2,1)}, bf16[4,3,128,512]{3,2,1,0:T(8,128)(2,1)}, f32[3,8,512]{2,1,0:T(8,128)S(1)}) custom-call(s32[3]{0:T(128)S(1)} %bitcast.70, f32[4,3,128,640]{3,2,1,0:T(8,128)} %bitcast.106, f32[512,128]{1,0:T(8,128)S(1)} %copy.56.cos, f32[512,128]{1,0:T(8,128)S(1)} %pad_maximum_fusion.1.sine, ...), custom_call_target="tpu_custom_call" | custom-call | flops 1688999936 | bytes 5630004 | tf_op jit(solution)/shard_map/pallas_call | solution.py:71
  157.7 11.5 %collective-permute-done.12.b2 = bf16[384,1024]{1,0:T(8,128)(2,1)S(1)} collective-permute-done((bf16[384,1024]{1,0:T(8,128)(2,1)S(1)}, bf16[384,1024]{1,0:T(8,128)(2,1)S(1)}, u32[]{:S(2)}, u32[]{:S(2)}) %collective-permute-start.12) | collective-permute-done | bytes 786464 | tf_op jit(solution)/shard_map/ppermute | solution.py:37
  169.2 16.3 %collective-permute-done.11.a2 = bf16[384,1024]{1,0:T(8,128)(2,1)S(1)} collective-permute-done((bf16[384,1024]{1,0:T(8,128)(2,1)S(1)}, bf16[384,1024]{1,0:T(8,128)(2,1)S(1)}, u32[]{:S(2)}, u32[]{:S(2)}) %collective-permute-start.11) | collective-permute-done | bytes 786464 | tf_op jit(solution)/shard_map/ppermute | solution.py:37
  210.5 18.0 %collective-permute-done.13.p1 = bf16[384,2048]{1,0:T(8,128)(2,1)} collective-permute-done((bf16[384,2048]{1,0:T(8,128)(2,1)}, bf16[384,2048]{1,0:T(8,128)(2,1)}, u32[]{:S(2)}, u32[]{:S(2)}) %collective-permute-start.13) | collective-permute-done | bytes 1572896 | tf_op jit(solution)/shard_map/ppermute | solution.py:37
  239.6 15.1 %shard_map.213.gate_in = f32[1536,1408]{1,0:T(8,128)} custom-call(bf16[1536,1024]{1,0:T(8,128)(2,1)} %bitcast.74, bf16[1536,1024]{1,0:T(8,128)(2,1)} %bitcast.78, bf16[1024,1408]{1,0:T(8,128)(2,1)} %all-gather.8.cloned.1.call-done.w_own.gate_w, bf16[1024,1408]{1,0:T(8,128)(2,1)} %collective-permute-done.14.w_oth.gate_w), custom_call_target="tpu_custom_call" | custom-call | flops 1169400064 | bytes 3898038 | tf_op jit(solution)/shard_map/pallas_call | solution.py:71
  254.7 11.2 %collective-permute-done.17.u_oth.up_w = bf16[1024,1408]{1,0:T(8,128)(2,1)S(1)} collective-permute-done((bf16[1024,1408]{1,0:T(8,128)(2,1)}, bf16[1024,1408]{1,0:T(8,128)(2,1)S(1)}, u32[]{:S(2)}, u32[]{:S(2)}) %collective-permute-start.17) | collective-permute-done | bytes 2883616 | tf_op jit(solution)/shard_map/ppermute | solution.py:37
  267.4 17.9 %shard_map.214 = (bf16[1536,1408]{1,0:T(8,128)(2,1)}, bf16[1536,1408]{1,0:T(8,128)(2,1)}, bf16[1536,1408]{1,0:T(8,128)(2,1)}) custom-call(bf16[1536,1024]{1,0:T(8,128)(2,1)} %bitcast.75, bf16[1536,1024]{1,0:T(8,128)(2,1)} %bitcast.79, bf16[1024,1408]{1,0:T(8,128)(2,1)} %all-gather.12.cloned.1.call-done.u_own.up_w, bf16[1024,1408]{1,0:T(8,128)(2,1)} %copy-done.1, ...), custom_call_target="tpu_custom_call" | custom-call | flops 1378800000 | bytes 4596011 | tf_op jit(solution)/shard_map/pallas_call | solution.py:71
  285.4 14.8 %shard_map.215 = bf16[2048,1408]{1,0:T(8,128)(2,1)} custom-call(bf16[1536,2048]{1,0:T(8,128)(2,1)} %bitcast.72, bf16[1536,1408]{1,0:T(8,128)(2,1)} %get-tuple-element.133.grad.rows), custom_call_target="tpu_custom_call" | custom-call | flops 1184999936 | bytes 3950012 | tf_op jit(solution)/shard_map/pallas_call | solution.py:71
  304.6 17.2 %shard_map.216 = (bf16[1536,1408]{1,0:T(8,128)(2,1)}, bf16[1536,1408]{1,0:T(8,128)(2,1)}) custom-call(bf16[1536,2048]{1,0:T(8,128)(2,1)} %bitcast.73, bf16[2048,1408]{1,0:T(8,128)(2,1)} %all-gather.14.cloned.1.call-done.weight, bf16[1536,1408]{1,0:T(8,128)(2,1)} %get-tuple-element.120.for_gate, bf16[1536,1408]{1,0:T(8,128)(2,1)} %get-tuple-element.121.for_up), custom_call_target="tpu_custom_call" | custom-call | flops 1301400064 | bytes 4338013 | tf_op jit(solution)/shard_map/pallas_call | solution.py:71
  321.8 9.2 %shard_map.217 = bf16[1024,1408]{1,0:T(8,128)(2,1)} custom-call(bf16[1536,1024]{1,0:T(8,128)(2,1)} %bitcast.80, bf16[1536,1408]{1,0:T(8,128)(2,1)} %get-tuple-element.126.grad.gate_g), custom_call_target="tpu_custom_call" | custom-call | flops 704400000 | bytes 2348016 | tf_op jit(solution)/shard_map/pallas_call | solution.py:71
  332.4 15.6 %shard_map.218 = (bf16[768,1024]{1,0:T(8,128)(2,1)}, bf16[768,1024]{1,0:T(8,128)(2,1)}) custom-call(bf16[1536,1408]{1,0:T(8,128)(2,1)} %get-tuple-element.126.grad.gate_g, bf16[1536,1408]{1,0:T(8,128)(2,1)} %get-tuple-element.129.up_g.grad, bf16[1024,1408]{1,0:T(8,128)(2,1)} %collective-permute-done.14.w_oth.gate_w, bf16[1024,1408]{1,0:T(8,128)(2,1)} %copy-done.1), custom_call_target="tpu_custom_call" | custom-call | flops 1169400064 | bytes 3898014 | tf_op jit(solution)/shard_map/pallas_call | solution.py:71
  348.1 15.7 %shard_map.219 = (bf16[768,1024]{1,0:T(8,128)(2,1)}, bf16[768,1024]{1,0:T(8,128)(2,1)}) custom-call(bf16[1536,1408]{1,0:T(8,128)(2,1)} %get-tuple-element.126.grad.gate_g, bf16[1536,1408]{1,0:T(8,128)(2,1)} %get-tuple-element.129.up_g.grad, bf16[1024,1408]{1,0:T(8,128)(2,1)} %all-gather.8.cloned.1.call-done.w_own.gate_w, ...), custom_call_target="tpu_custom_call" | custom-call | flops 1161600000 | bytes 3872017 | tf_op jit(solution)/shard_map/pallas_call | solution.py:71
  373.2 9.2 %shard_map.221 = bf16[1024,1408]{1,0:T(8,128)(2,1)} custom-call(bf16[1536,1024]{1,0:T(8,128)(2,1)} %bitcast.81, bf16[1536,1408]{1,0:T(8,128)(2,1)} %get-tuple-element.129.up_g.grad), custom_call_target="tpu_custom_call" | custom-call | flops 704400000 | bytes 2348019 | tf_op jit(solution)/shard_map/pallas_call | solution.py:71
  382.8 13.8 %collective-permute-done.30.came = bf16[1024,1408]{1,0:T(8,128)(2,1)S(1)} collective-permute-done((bf16[1024,1408]{1,0:T(8,128)(2,1)}, bf16[1024,1408]{1,0:T(8,128)(2,1)S(1)}, u32[]{:S(2)}, u32[]{:S(2)}) %collective-permute-start.30) | collective-permute-done | bytes 2883616 | tf_op jit(solution)/shard_map/ppermute | solution.py:37
  404.1 9.8 %shard_map.232 = bf16[1024,1408]{1,0:T(8,128)(2,1)} custom-call(bf16[1536,1024]{1,0:T(8,128)(2,1)} %bitcast.76, bf16[1536,1408]{1,0:T(8,128)(2,1)} %get-tuple-element.126.grad.gate_g, bf16[1024,1408]{1,0:T(8,128)(2,1)} %copy-done.9), custom_call_target="tpu_custom_call" | custom-call | flops 766800000 | bytes 2556023 | tf_op jit(solution)/shard_map/pallas_call | solution.py:71
  422.8 16.0 %shard_map.224 = (bf16[768,2048]{1,0:T(8,128)(2,1)}, bf16[768,2048]{1,0:T(8,128)(2,1)}) custom-call(bf16[1536,1408]{1,0:T(8,128)(2,1)} %get-tuple-element.133.grad.rows, bf16[2048,1408]{1,0:T(8,128)(2,1)} %all-gather.14.cloned.1.call-done.weight), custom_call_target="tpu_custom_call" | custom-call | flops 1146000000 | bytes 3820021 | tf_op jit(solution)/shard_map/pallas_call | solution.py:71
  438.9 18.6 %collective-permute-done.24.came = bf16[1024,1408]{1,0:T(8,128)(2,1)} collective-permute-done((bf16[1024,1408]{1,0:T(8,128)(2,1)}, bf16[1024,1408]{1,0:T(8,128)(2,1)}, u32[]{:S(2)}, u32[]{:S(2)}) %collective-permute-start.24) | collective-permute-done | bytes 2883616 | tf_op jit(solution)/shard_map/ppermute | solution.py:37
  457.5 9.9 %shard_map.225 = bf16[1024,1408]{1,0:T(8,128)(2,1)} custom-call(bf16[1536,1024]{1,0:T(8,128)(2,1)} %bitcast.77, bf16[1536,1408]{1,0:T(8,128)(2,1)} %get-tuple-element.129.up_g.grad, bf16[1024,1408]{1,0:T(8,128)(2,1)} %collective-permute-done.24.came), custom_call_target="tpu_custom_call" | custom-call | flops 3068400128 | bytes 10228028 | tf_op jit(solution)/shard_map/pallas_call | solution.py:71
  499.2 26.8 %shard_map.230 = bf16[4,3,128,640]{3,2,1,0:T(8,128)(2,1)} custom-call(s32[3]{0:T(128)S(1)} %bitcast.71, bf16[4,3,128,512]{3,2,1,0:T(8,128)(2,1)} %get-tuple-element.142.query_in, bf16[4,3,128,128]{3,2,1,0:T(8,128)(2,1)} %get-tuple-element.143.kv_in, bf16[4,3,128,512]{3,2,1,0:T(8,128)(2,1)} %bitcast.113, ...), custom_call_target="tpu_custom_call" | custom-call | flops 38310600704 | bytes 127702024 | tf_op jit(solution)/shard_map/pallas_call | solution.py:71
  526.1 8.7 %shard_map.233 = (bf16[768,1024]{1,0:T(8,128)(2,1)}, bf16[768,1024]{1,0:T(8,128)(2,1)}, f32[1,1024]{1,0:T(1,128)S(1)}) custom-call(bf16[1536,640]{1,0:T(8,128)(2,1)} %bitcast.82, bf16[1024,640]{1,0:T(8,128)(2,1)} %bitcast.101, bf16[1536,1024]{1,0:T(8,128)(2,1)} %bitcast.87), custom_call_target="tpu_custom_call" | custom-call | bytes 29 | tf_op jit(solution)/shard_map/pallas_call | solution.py:71
  (230 shorter events, 260.9 us)
Async XLA Ops:
  7.2 41.3 %all-gather.6.cloned.1.call-start = ((), (), s32[]{:S(2)}) async-start(), calls=%async_computation.5 | async-start | bytes 1740800 | tf_op jit(solution)/shard_map/all_gather | solution.py:422
  11.5 66.0 %all-gather.10.cloned.1.call-start = ((), (), s32[]{:S(2)}) async-start(), calls=%async_computation.7 | async-start | bytes 1310720 | tf_op jit(solution)/shard_map/all_gather | solution.py:422
  13.4 124.4 %all-gather.8.cloned.1.call-start = ((), (), s32[]{:S(2)}) async-start(), calls=%async_computation.6 | async-start | bytes 3604480 | tf_op jit(solution)/shard_map/all_gather | solution.py:422
  14.2 183.0 %all-gather.12.cloned.1.call-start = ((), (), s32[]{:S(2)}) async-start(), calls=%async_computation.8 | async-start | bytes 3604480 | tf_op jit(solution)/shard_map/all_gather | solution.py:422
  14.7 289.8 %all-gather.14.cloned.1.call-start = ((), (), s32[]{:S(2)}) async-start(), calls=%async_computation.10 | async-start | bytes 7208960 | tf_op jit(solution)/shard_map/all_gather | solution.py:422
  18.1 36.2 %collective-permute-start = (bf16[384,2048]{1,0:T(8,128)(2,1)}, bf16[384,2048]{1,0:T(8,128)(2,1)}, u32[]{:S(2)}, u32[]{:S(2)}) collective-permute-start(bf16[384,2048]{1,0:T(8,128)(2,1)} %bitcast.114), channel_id=1, source_target_pairs={{0,2},{2,0},{1,3},{3,1},{4,6},{6,4},{5,7},{7,5},{8,10},{10,8},{9,1... | collective-permute-start | bytes 4718600 | tf_op jit(solution)/shard_map/ppermute | solution.py:37
  50.0 38.5 %collective-permute-start.4 = (bf16[384,2048]{1,0:T(8,128)(2,1)}, bf16[384,2048]{1,0:T(8,128)(2,1)}, u32[]{:S(2)}, u32[]{:S(2)}) collective-permute-start(bf16[384,2048]{1,0:T(8,128)(2,1)} %bitcast.115), channel_id=1, source_target_pairs={{0,1},{1,0},{2,3},{3,2},{4,5},{5,4},{6,7},{7,6},{8,9},{9,8},{10,11... | collective-permute-start | bytes 4718600 | tf_op jit(solution)/shard_map/ppermute | solution.py:37
  54.3 52.4 %collective-permute-start.1 = (bf16[384,2048]{1,0:T(8,128)(2,1)S(1)}, bf16[384,2048]{1,0:T(8,128)(2,1)}, u32[]{:S(2)}, u32[]{:S(2)}) collective-permute-start(bf16[384,2048]{1,0:T(8,128)(2,1)S(1)} %bitcast.104), channel_id=1, source_target_pairs={{0,2},{2,0},{1,3},{3,1},{4,6},{6,4},{5,7},{7,5},{8,10},{10,8},{9,1... | collective-permute-start | bytes 4718600 | tf_op jit(solution)/shard_map/ppermute | solution.py:37
  57.7 399.8 %reduce-scatter.6.cloned.1.call-start = ((), (), s32[]{:S(2)}) async-start(), calls=%async_computation.9 | async-start | bytes 7208960 | tf_op jit(solution)/shard_map/reduce_scatter | solution.py:585
  80.4 47.6 %collective-permute-start.8 = (bf16[1024,512]{1,0:T(8,128)(2,1)}, bf16[1024,512]{1,0:T(8,128)(2,1)S(1)}, u32[]{:S(2)}, u32[]{:S(2)}) collective-permute-start(bf16[1024,512]{1,0:T(8,128)(2,1)} %all-gather.10.cloned.1.call-done.weight.w_own), channel_id=1, source_target_pairs={{0,4},{4,0},{1,5},{5,1},{2,6},{6,2},{3,7},{7,3},{8,12},{12,8},{9,1... | collective-permute-start | bytes 3145736 | tf_op jit(solution)/shard_map/ppermute | solution.py:37
  137.8 64.5 %collective-permute-start.14 = (bf16[1024,1408]{1,0:T(8,128)(2,1)}, bf16[1024,1408]{1,0:T(8,128)(2,1)}, u32[]{:S(2)}, u32[]{:S(2)}) collective-permute-start(bf16[1024,1408]{1,0:T(8,128)(2,1)} %all-gather.8.cloned.1.call-done.w_own.gate_w), channel_id=1, source_target_pairs={{0,4},{4,0},{1,5},{5,1},{2,6},{6,2},{3,7},{7,3},{8,12},{12,8},{9,1... | collective-permute-start | bytes 8650760 | tf_op jit(solution)/shard_map/ppermute | solution.py:37
  157.2 46.6 %collective-permute-start.2 = (bf16[384,2048]{1,0:T(8,128)(2,1)S(1)}, bf16[384,2048]{1,0:T(8,128)(2,1)}, u32[]{:S(2)}, u32[]{:S(2)}) collective-permute-start(bf16[384,2048]{1,0:T(8,128)(2,1)S(1)} %bitcast.105), channel_id=1, source_target_pairs={{0,1},{1,0},{2,3},{3,2},{4,5},{5,4},{6,7},{7,6},{8,9},{9,8},{10,11... | collective-permute-start | bytes 4718600 | tf_op jit(solution)/shard_map/ppermute | solution.py:37
  157.2 46.6 %collective-permute-start.3 = (bf16[384,2048]{1,0:T(8,128)(2,1)}, bf16[384,2048]{1,0:T(8,128)(2,1)}, u32[]{:S(2)}, u32[]{:S(2)}) collective-permute-start(bf16[384,2048]{1,0:T(8,128)(2,1)} %collective-permute-done.1.p1), channel_id=1, source_target_pairs={{0,1},{1,0},{2,3},{3,2},{4,5},{5,4},{6,7},{7,6},{8,9},{9,8},{10,11... | collective-permute-start | bytes 4718600 | tf_op jit(solution)/shard_map/ppermute | solution.py:37
  192.2 36.3 %collective-permute-start.13 = (bf16[384,2048]{1,0:T(8,128)(2,1)}, bf16[384,2048]{1,0:T(8,128)(2,1)}, u32[]{:S(2)}, u32[]{:S(2)}) collective-permute-start(bf16[384,2048]{1,0:T(8,128)(2,1)} %get-tuple-element.109.p0), channel_id=1, source_target_pairs={{0,2},{2,0},{1,3},{3,1},{4,6},{6,4},{5,7},{7,5},{8,10},{10,8},{9,1... | collective-permute-start | bytes 4718600 | tf_op jit(solution)/shard_map/ppermute | solution.py:37
  202.3 63.5 %collective-permute-start.17 = (bf16[1024,1408]{1,0:T(8,128)(2,1)}, bf16[1024,1408]{1,0:T(8,128)(2,1)S(1)}, u32[]{:S(2)}, u32[]{:S(2)}) collective-permute-start(bf16[1024,1408]{1,0:T(8,128)(2,1)} %all-gather.12.cloned.1.call-done.u_own.up_w), channel_id=1, source_target_pairs={{0,4},{4,0},{1,5},{5,1},{2,6},{6,2},{3,7},{7,3},{8,12},{12,8},{9,1... | collective-permute-start | bytes 8650760 | tf_op jit(solution)/shard_map/ppermute | solution.py:37
  300.2 225.8 %reduce-scatter.8.cloned.1.call-start = ((), (), s32[]{:S(2)}) async-start(), calls=%async_computation.11 | async-start | bytes 3604480 | tf_op jit(solution)/shard_map/reduce_scatter | solution.py:585
  331.0 65.6 %collective-permute-start.30 = (bf16[1024,1408]{1,0:T(8,128)(2,1)}, bf16[1024,1408]{1,0:T(8,128)(2,1)S(1)}, u32[]{:S(2)}, u32[]{:S(2)}) collective-permute-start(bf16[1024,1408]{1,0:T(8,128)(2,1)} %shard_map.217), channel_id=1, source_target_pairs={{0,4},{4,0},{1,5},{5,1},{2,6},{6,2},{3,7},{7,3},{8,12},{12,8},{9,1... | collective-permute-start | bytes 8650760 | tf_op jit(solution)/shard_map/ppermute | solution.py:37
  382.4 75.1 %collective-permute-start.24 = (bf16[1024,1408]{1,0:T(8,128)(2,1)}, bf16[1024,1408]{1,0:T(8,128)(2,1)}, u32[]{:S(2)}, u32[]{:S(2)}) collective-permute-start(bf16[1024,1408]{1,0:T(8,128)(2,1)} %shard_map.221), channel_id=1, source_target_pairs={{0,4},{4,0},{1,5},{5,1},{2,6},{6,2},{3,7},{7,3},{8,12},{12,8},{9,1... | collective-permute-start | bytes 8650760 | tf_op jit(solution)/shard_map/ppermute | solution.py:37
  413.9 165.1 %reduce-scatter.10.cloned.1.call-start = ((), (), s32[]{:S(2)}) async-start(), calls=%async_computation.12 | async-start | bytes 3604480 | tf_op jit(solution)/shard_map/reduce_scatter | solution.py:585
  421.4 46.0 %collective-permute-start.23 = (bf16[384,2048]{1,0:T(8,128)(2,1)}, bf16[384,2048]{1,0:T(8,128)(2,1)}, u32[]{:S(2)}, u32[]{:S(2)}) collective-permute-start(bf16[384,2048]{1,0:T(8,128)(2,1)} %get-tuple-element.132.p0), channel_id=1, source_target_pairs={{0,2},{2,0},{1,3},{3,1},{4,6},{6,4},{5,7},{7,5},{8,10},{10,8},{9,1... | collective-permute-start | bytes 4718600 | tf_op jit(solution)/shard_map/ppermute | solution.py:37
  422.8 44.5 %collective-permute-start.25 = (bf16[384,2048]{1,0:T(8,128)(2,1)}, bf16[384,2048]{1,0:T(8,128)(2,1)}, u32[]{:S(2)}, u32[]{:S(2)}) collective-permute-start(bf16[384,2048]{1,0:T(8,128)(2,1)} %get-tuple-element.132.p0), channel_id=1, source_target_pairs={{0,1},{1,0},{2,3},{3,2},{4,5},{5,4},{6,7},{7,6},{8,9},{9,8},{10,11... | collective-permute-start | bytes 4718600 | tf_op jit(solution)/shard_map/ppermute | solution.py:37
  478.5 118.5 %reduce-scatter.14.cloned.1.call-start = ((), (), s32[]{:S(2)}) async-start(), calls=%async_computation.14 | async-start | bytes 1310720 | tf_op jit(solution)/shard_map/reduce_scatter | solution.py:585
  497.8 37.0 %collective-permute-start.28 = (bf16[384,2048]{1,0:T(8,128)(2,1)}, bf16[384,2048]{1,0:T(8,128)(2,1)}, u32[]{:S(2)}, u32[]{:S(2)}) collective-permute-start(bf16[384,2048]{1,0:T(8,128)(2,1)} %shard_map.227), channel_id=1, source_target_pairs={{0,2},{2,0},{1,3},{3,1},{4,6},{6,4},{5,7},{7,5},{8,10},{10,8},{9,1... | collective-permute-start | bytes 4718600 | tf_op jit(solution)/shard_map/ppermute | solution.py:37
  547.0 69.2 %reduce-scatter.12.cloned.1.call-start = ((), (), s32[]{:S(2)}) async-start(), calls=%async_computation.13 | async-start | bytes 1740800 | tf_op jit(solution)/shard_map/reduce_scatter | solution.py:585
  (49 other events, 594.4 us)
Sparse Core Ops, SparseCore 0:
  11.7 36.7 all-gather.5
  50.6 26.8 all-gather.9
  79.1 58.6 all-gather.7
  139.3 57.8 all-gather.11
  199.1 105.3 all-gather.13
  306.7 100.5 reduce-scatter.5
  414.0 53.4 reduce-scatter.7
  478.7 54.3 reduce-scatter.9
  547.2 24.1 reduce-scatter.13
  583.2 29.1 reduce-scatter.11
